TPU v7x, 32 devices: a whole 2x2x4 slice. The times are simulated.
32 devices in a mesh: ctx: 8 (over y, x, core), wt: 4 (over z).
Axes of the slice: x: 2, y: 2, z: 4, core: 2. Of those that a mesh axis runs over, the one named last changes fastest.
Arguments:
- tokens: bfloat16 [1, 1024, 2048], P(None, 'ctx'), may hold values from -6 to 6
- cotangent: bfloat16 [1, 1024, 2048], P(None, 'ctx'), may hold values from -6 to 6
- routes: int32 [1024, 8], P(('ctx', 'wt')), may hold values from 0 to 31, all different within a row; in each aligned block of 32 rows (0 to 31, 32 to 63, ...) at most 11 rows name the same one
- attn_gain: float32 [2048], replicated, may hold values from 0.5 to 1.5
- query_gain: float32 [128], replicated, may hold values from 0.25 to 1.75
- key_gain: float32 [128], replicated, may hold values from 0.25 to 1.75
- w_query: bfloat16 [2048, 4096], P(None, 'wt'), may hold values from -0.125 to 0.125
- key_weight: bfloat16 [2048, 512], P(None, 'wt'), may hold values from -0.125 to 0.125
- value_weight: bfloat16 [2048, 512], P(None, 'wt'), may hold values from -0.125 to 0.125
- w_output: bfloat16 [4096, 2048], P('wt'), may hold values from -1 to 1
- moe_gain: float32 [2048], replicated, may hold values from 0.5 to 1.5
- w_router: bfloat16 [2048, 32], replicated, may hold values from -0.0625 to 0.0625
- w_gate_up: bfloat16 [32, 2048, 1536], P(('ctx', 'wt')), may hold values from -0.125 to 0.125
- w_down: bfloat16 [32, 768, 2048], P(('ctx', 'wt')), may hold values from -0.875 to 0.875
Outputs:
- block_out: bfloat16 [1, 1024, 2048], P(None, 'ctx')
- tokens_grad: bfloat16 [1, 1024, 2048], P(None, 'ctx')
- attn_gain_grad: float32 [2048], replicated
- query_gain_grad: float32 [128], replicated
- key_gain_grad: float32 [128], replicated
- w_query_grad: float32 [2048, 4096], P('ctx', 'wt')
- w_key_grad: float32 [2048, 512], P('ctx', 'wt')
- w_value_grad: float32 [2048, 512], P('ctx', 'wt')
- w_output_grad: float32 [4096, 2048], P('wt', 'ctx')
- moe_gain_grad: float32 [2048], replicated
- w_router_grad: float32 [2048, 32], replicated
- w_gate_up_grad: float32 [32, 2048, 1536], P(('ctx', 'wt'))
- w_down_grad: float32 [32, 768, 2048], P(('ctx', 'wt'))
Inputs may be any that keep to these rules, and one draw needn't show every extreme that they name: `routes`: each row names 8 different experts. In each aligned block of 32 rows (the rows of one device of ctx and wt together) no expert is named by more than 11 rows, and in every draw some block has an expert named by exactly 11 of its rows.
All inputs are finite; a program needn't handle non-finite values.
Results may differ from a plain program's by a relative error of at most 0.018.
Values may be sent and summed in bfloat16 or wider, within the bound.
No kernel may reach another device: no remote copies, remote signals or barrier semaphores. Data moves between devices by JAX's collectives and lax.ppermute only.
A program may use at most 192 MiB of HBM per device.

v0:
```python
import functools

import jax
import jax.numpy as jnp
from jax import lax
from jax.experimental import pallas as pl
from jax.experimental.pallas import tpu as pltpu
from jax.sharding import PartitionSpec as P

epsilon = 1e-06
rope_base = 1000000.0
low = jnp.bfloat16
full = jnp.float32
vmem_bytes = 60 * 1024 * 1024

in_vmem = pl.BlockSpec(memory_space=pltpu.VMEM)
in_smem = pl.BlockSpec(memory_space=pltpu.SMEM)
in_any = pl.BlockSpec(memory_space=pl.ANY)


def dot(a, b, a_dim=1, b_dim=0):
    return lax.dot_general(a, b, (((a_dim,), (b_dim,)), ((), ())), preferred_element_type=full)


def swap(array, axis, mask):
    count = lax.axis_size(axis)
    return lax.ppermute(array, axis, [(i, i ^ mask) for i in range(count)])


def fence(*values):
    return lax.optimization_barrier(values)


def shape_of(shape, dtype):
    return jax.ShapeDtypeStruct(tuple(shape), dtype)


def kernel_call(kernel, outs, ins, args, after=(), through=(), **more):
    single = not isinstance(outs, list)
    outs = [outs] if single else list(outs)
    after, through = jax.tree.leaves(after), jax.tree.leaves(through)
    count, lead = len(args), len(outs)
    every = count + len(after) + len(through)

    def body(*refs):
        kernel(*refs[:count], *refs[every : every + lead], *refs[every + lead + len(through) :])

    aliases = dict(more.pop("input_output_aliases", {}))
    if through:
        aliases.update({count + len(after) + i: lead + i for i in range(len(through))})
        more["out_specs"] = list(more.get("out_specs", [in_vmem] * lead)) + [in_any] * len(through)
    results = pl.pallas_call(
        body,
        out_shape=outs + [shape_of(one.shape, one.dtype) for one in through],
        in_specs=[*ins] + [in_any] * (len(after) + len(through)),
        input_output_aliases=aliases,
        compiler_params=pltpu.CompilerParams(vmem_limit_bytes=vmem_bytes),
        **more,
    )(*args, *after, *through)
    return results[0] if single else results


def rms_scale(value_matrix):
    return lax.rsqrt(jnp.mean(value_matrix * value_matrix, axis=-1, keepdims=True) + epsilon)


def norm_back(grad_out, value_matrix, inverse, gain_vec):
    scaled = grad_out * gain_vec
    inner_mean = jnp.mean(scaled * value_matrix, axis=-1, keepdims=True)
    return inverse * (scaled - value_matrix * inverse * inverse * inner_mean)


def mirrored(device, offset, groups, block_len):
    which_block = jnp.where(offset < block_len, device, 2 * groups - 1 - device)
    return which_block * block_len + offset % block_len


def rotate(value_matrix, cosine, sine):
    return value_matrix * cosine + pltpu.roll(value_matrix, value_matrix.shape[-1] // 2, 1) * sine


def front_kernel(
    index_ref, x_ref, gain_ref, kw_ref, vw_ref, kgain_ref, cos_ref, sin_ref,
    rows_ref, normed_ref, inv_ref, raw_ref, *message_refs
):
    blocks, share, _ = x_ref.shape
    for i in range(blocks):
        x_low = x_ref[index_ref[0] ^ i]
        rows_ref[i] = x_low
        x = x_low.astype(full)
        inverse = rms_scale(x)
        inv_ref[i * share : (i + 1) * share] = inverse
        normed_ref[i * share : (i + 1) * share] = (x * inverse * gain_ref[...]).astype(low)
    normed = normed_ref[...]
    raw = dot(normed, kw_ref[...])
    raw_ref[...] = raw
    head_dim = raw.shape[1]
    turned = rotate(raw * rms_scale(raw) * kgain_ref[...], cos_ref[...], sin_ref[...])
    keys = turned.astype(low)
    values = dot(normed, vw_ref[...]).astype(low)
    for k, ref in enumerate(message_refs):
        ref[:, :head_dim] = keys
        ref[:, head_dim : 2 * head_dim] = values
        cols = ref.shape[1] - 2 * head_dim
        start = pl.multiple_of((index_ref[1] ^ k) * cols, 128)
        ref[:, 2 * head_dim :] = normed_ref[:, pl.ds(start, cols)]


def query_kernel(normed_ref, w_ref, gain_ref, cos_ref, sin_ref, raw_ref, q_ref):
    rows, head_dim = cos_ref.shape
    raw = dot(normed_ref[...], w_ref[...])
    raw_ref[...] = raw
    for h in range(raw.shape[1] // head_dim):
        one = raw[:, h * head_dim : (h + 1) * head_dim]
        turned = rotate(one * rms_scale(one) * gain_ref[...], cos_ref[...], sin_ref[...])
        q_ref[h * rows : (h + 1) * rows] = turned.astype(low)


def attend_kernel(scale, pieces, qpos_ref, kpos_ref, q_ref, w_ref, *refs):
    kv_refs = refs[:pieces]
    rows_ref, probs_ref, keys_ref, values_ref, own_ref, *rest_refs, attn, weight, sem = refs[pieces:]
    step = pl.program_id(0)
    tokens, head_dim = rows_ref.shape[0], kv_refs[0].shape[1] // 2
    copy = pltpu.make_async_copy(w_ref, weight, sem)

    @pl.when(step == 0)
    def _():
        copy.start()
        at = 0
        for ref in kv_refs:
            keys_ref[at : at + ref.shape[0]] = ref[:, :head_dim]
            values_ref[at : at + ref.shape[0]] = ref[:, head_dim : 2 * head_dim]
            at += ref.shape[0]

    scores = dot(q_ref[...], keys_ref[...], 1, 1) * scale
    scores = jnp.where(kpos_ref[...] <= qpos_ref[...], scores, -1e30)
    weights = jnp.exp(scores - jnp.max(scores, axis=-1, keepdims=True))
    probs = (weights / jnp.sum(weights, axis=-1, keepdims=True)).astype(low)
    probs_ref[...] = probs
    out = dot(probs, values_ref[...]).astype(low)
    heads = out.shape[0] // tokens
    attn[step] = jnp.concatenate([out[h * tokens : (h + 1) * tokens] for h in range(heads)], axis=1)

    @pl.when(step == pl.num_programs(0) - 1)
    def _():
        copy.wait()
        for i in range(attn.shape[0]):
            rows_ref[:, i * heads * head_dim : (i + 1) * heads * head_dim] = attn[i]
        total = dot(rows_ref[...], weight[...])
        share = own_ref.shape[0]
        own_ref[...] = total[:share]
        for i, ref in enumerate(rest_refs):
            ref[...] = total[(i + 1) * share : (i + 2) * share].astype(low)


def mid_kernel(x_ref, gain_ref, mask_ref, own_ref, *refs):
    received, (mid_ref, inv_ref, message_ref) = refs[:-3], refs[-3:]
    mid = own_ref[...]
    for one in received:
        mid = mid + one[...].astype(full)
    mid = x_ref[0].astype(full) + mid
    inverse = rms_scale(mid)
    mid_ref[...] = mid
    inv_ref[...] = inverse
    width = mid.shape[1]
    message_ref[:, :width] = (mid * inverse * gain_ref[...]).astype(low)
    message_ref[:, width:] = mask_ref[...]


def expert_kernel(
    tiles, first, inner, merged, index_ref, row_near, row_far, grad_near, grad_far, router_ref,
    gu_any, down_any, *refs
):
    if merged:
        near_ref, far_ref, *refs = refs
        moe_near_ref, moe_far_ref = near_ref, far_ref
    else:
        near_ref, far_ref, moe_near_ref, moe_far_ref, *refs = refs
    x_ref, hidden_ref, dgu_ref, deo_ref, x_tile, g_tile, gu, down, sems = refs
    step = pl.program_id(0)
    width = g_tile.shape[1]
    ffw = down.shape[0]
    experts = router_ref.shape[0]
    expert = index_ref[0]
    chips, _, share, _ = grad_near.shape
    copy_gu = pltpu.make_async_copy(gu_any.at[0], gu, sems.at[0])
    copy_down = pltpu.make_async_copy(down_any.at[0], down, sems.at[1])

    @pl.when(step == 0)
    def _():
        copy_gu.start()
        copy_down.start()

    def load(row_ref, grad_ref):
        x_tile[...] = row_ref[...]
        for c in range(chips):
            for w in range(inner):
                to = slice((c * inner + w) * share, (c * inner + w + 1) * share)
                g_tile[to] = grad_ref[c, index_ref[1] ^ (first + w)][:, : g_tile.shape[1]]

    @pl.when(step < tiles // 2)
    def _():
        load(row_near, grad_near)

    @pl.when(step >= tiles // 2)
    def _():
        load(row_far, grad_far)

    x = x_tile[:, :width]
    x_ref[...] = x
    g = g_tile[...].astype(full)
    chosen = x_tile[:, width:][:, :experts].astype(full) > 0.5
    logits = jnp.where(chosen, dot(x, router_ref[...], 1, 1), -1e30)
    shifted = jnp.exp(logits - jnp.max(logits, axis=-1, keepdims=True))
    shifted = jnp.where(chosen, shifted, 0.0)
    mine = lax.broadcasted_iota(jnp.int32, shifted.shape, 1) == expert
    own = jnp.sum(jnp.where(mine, shifted, 0.0), axis=-1, keepdims=True) / jnp.sum(
        shifted, axis=-1, keepdims=True
    )
    deo = (g * own).astype(low)
    deo_ref[...] = deo

    @pl.when(step == 0)
    def _():
        copy_gu.wait()

    gate_up = dot(x, gu[...])

    @pl.when(step == 0)
    def _():
        copy_down.wait()

    gate, up = gate_up[:, :ffw], gate_up[:, ffw:]
    dhid = dot(deo, down[...], 1, 1)
    sig = jax.nn.sigmoid(gate)
    silu = gate * sig
    hidden = (silu * up).astype(low)
    hidden_ref[...] = hidden
    dgate = (dhid * up * (sig + silu * (1.0 - sig))).astype(low)
    dup = (dhid * silu).astype(low)
    dgu_ref[:, :ffw] = dgate
    dgu_ref[:, ffw:] = dup
    out = dot(hidden, down[...]).astype(low).astype(full)
    dlw = jnp.sum(out * g, axis=-1, keepdims=True)
    moe = (out * own).astype(low)
    back = (dot(dgate, gu[:, :ffw], 1, 1) + dot(dup, gu[:, ffw:], 1, 1)).astype(low)
    high = dlw.astype(low)
    rest = (dlw - high.astype(full)).astype(low).astype(full)
    cols = near_ref.shape[1] - (2 if merged else 1) * width
    lane = lax.broadcasted_iota(jnp.int32, (x.shape[0], cols), 1)
    extra = jnp.where(lane == expert, high.astype(full), 0.0)
    extra = jnp.where(lane == experts + expert, rest, extra).astype(low)

    def store(row_ref, moe_ref):
        row_ref[:, :width] = back
        row_ref[:, width : width + cols] = extra
        moe_ref[:, moe_ref.shape[1] - width :] = moe

    @pl.when(step < tiles // 2)
    def _():
        store(near_ref, moe_near_ref)

    @pl.when(step >= tiles // 2)
    def _():
        store(far_ref, moe_far_ref)


def run_expert(part, part_count, inner, merged, rows, grads, router, w_gate_up, w_down, index, into, cols):
    chips, wt_count, share, width = grads[0].shape
    half_rows = chips * inner * share
    tile = min(256, half_rows)
    near = half_rows // tile
    tiles = 2 * near
    each = chips // near
    ffw = w_down.shape[1]
    wide = rows[0].shape[-1]
    everything = 2 * half_rows * part_count
    offset = part * tiles
    near_map = lambda i: (jnp.minimum(i, near - 1), 0)
    far_map = lambda i: (jnp.maximum(i - near, 0), 0)
    all_map = lambda i: (i + offset, 0)
    widths = [cols + width] if merged else [cols, width]
    outs, out_specs = [], []
    for one in widths:
        outs += [shape_of((half_rows, one), low)] * 2
        out_specs += [pl.BlockSpec((tile, one), near_map), pl.BlockSpec((tile, one), far_map)]
    lead_outs = len(outs)
    for one in (width, ffw, 2 * ffw, width):
        outs.append(shape_of((everything, one), low))
        out_specs.append(pl.BlockSpec((tile, one), all_map))
    ins = [in_smem]
    for where in (near_map, far_map):
        ins.append(pl.BlockSpec((tile, wide), where))
    for where, grad in ((near_map, grads[0]), (far_map, grads[1])):
        ins.append(pl.BlockSpec((each, *grad.shape[1:]), lambda i, where=where: (where(i)[0], 0, 0, 0)))
    ins += [pl.BlockSpec(router.shape, lambda i: (0, 0)), in_any, in_any]
    args = [index, *rows, *grads, router, w_gate_up, w_down]
    lead = len(args)
    aliases = {}
    if into is not None:
        for i, array in enumerate(into):
            aliases[len(args)] = lead_outs + i
            ins.append(in_any)
            args.append(array)

    def body(*refs):
        expert_kernel(tiles, part * inner, inner, merged, *refs[:lead], *refs[len(args) :])

    results = kernel_call(
        body,
        outs,
        ins,
        args,
        grid=(tiles,),
        out_specs=out_specs,
        scratch_shapes=[
            pltpu.VMEM((tile, wide), low),
            pltpu.VMEM((tile, width), low),
            pltpu.VMEM(w_gate_up.shape[1:], low),
            pltpu.VMEM(w_down.shape[1:], low),
            pltpu.SemaphoreType.DMA((2,)),
        ],
        input_output_aliases=aliases,
    )
    return results[:lead_outs], results[lead_outs:]


def pack_kernel(attn_ref, *refs):
    out_ref, share = refs[-1], refs[0].shape[0]
    wide = refs[0].shape[1]
    for i, ref in enumerate(refs[:-1]):
        out_ref[i * share : (i + 1) * share, :wide] = ref[...]
    rows, cols = out_ref.shape[0], attn_ref.shape[1]
    for i in range(attn_ref.shape[0] // rows):
        out_ref[:, wide + i * cols : wide + (i + 1) * cols] = attn_ref[i * rows : (i + 1) * rows]


def unpack_kernel(*refs):
    in_refs, (rows_ref, attn_ref) = refs[:-2], refs[-2:]
    rows, wide, cols = in_refs[0].shape[0], rows_ref.shape[1], attn_ref.shape[1]
    at = 0
    for i, ref in enumerate(in_refs):
        rows_ref[i * rows : (i + 1) * rows] = ref[:, :wide]
        for j in range((ref.shape[1] - wide) // cols):
            attn_ref[at : at + rows] = ref[:, wide + j * cols : wide + (j + 1) * cols]
            at += rows


def last_kernel(index_ref, x_ref, inv_ref, gain_ref, grad_ref, out_rows_ref, proj_ref, gains_ref, own_ref, *refs):
    *received, last_ref, message_ref, parts, stack = refs
    total = own_ref[...]
    share, width = total.shape
    for one in received:
        total = total + one[:, :width].astype(full)
    last_ref[:, :width] = out_rows_ref[...]
    grad = grad_ref[...] + norm_back(total, x_ref[0].astype(full), inv_ref[:share], gain_ref[...])
    last_ref[:, width:] = grad.astype(low)
    parts[index_ref[0]] = gains_ref[...]
    for i, one in enumerate(received):
        for j in range(gains_ref.shape[0] // share):
            cols = slice(width + j * 128, width + (j + 1) * 128)
            parts[index_ref[0] ^ (i + 1), j * share : (j + 1) * share] = one[:, cols].astype(full)
    gains = parts[0]
    for i in range(1, parts.shape[0]):
        gains = gains + parts[i]
    count = 2 * width // 128 + 2 * 1
    stack_split(stack, gains[:count] + gains[count : 2 * count])
    rows = proj_ref.shape[0]
    more = message_ref.shape[0] - rows
    message_ref[:rows] = proj_ref[...]
    message_ref[rows:] = jnp.zeros((more, message_ref.shape[1]), low)
    for j in range(stack.shape[0] // more):
        message_ref[rows:, j * 128 : (j + 1) * 128] = stack[j * more : (j + 1) * more].astype(low)


def join_kernel(*refs):
    out_ref, at = refs[-1], 0
    for ref in refs[:-1]:
        out_ref[at : at + ref.shape[0]] = ref[...]
        at += ref.shape[0]


def join(pieces, after=()):
    rows = sum(one.shape[0] for one in pieces)
    return kernel_call(
        join_kernel,
        shape_of((rows, pieces[0].shape[1]), pieces[0].dtype),
        [in_vmem] * len(pieces),
        list(pieces),
        after,
    )


def cut_kernel(pieces, index_ref, rows_ref, from_ref, *out_refs):
    whole = rows_ref.shape[1]
    cols = out_refs[0].shape[1] - whole
    for k in range(pieces):
        out_refs[k][:, :whole] = rows_ref[...]
        start = pl.multiple_of((index_ref[0] ^ k) * cols, 128)
        out_refs[k][:, whole:] = from_ref[:, pl.ds(start, cols)]


def deal_kernel(pieces, whole, index_ref, *refs):
    in_refs, (own_ref, keep_ref, give_ref) = refs[:pieces], refs[pieces:]
    rows = in_refs[0].shape[0]
    cols = (in_refs[0].shape[1] - whole) // 2
    for i, ref in enumerate(in_refs):
        at = slice(i * rows, (i + 1) * rows)
        own_ref[at] = ref[:, :whole]
        give_ref[at, :whole] = ref[:, :whole]
        keep = pl.multiple_of(whole + index_ref[0] * cols, 128)
        give = pl.multiple_of(whole + (1 - index_ref[0]) * cols, 128)
        keep_ref[at] = ref[:, pl.ds(keep, cols)]
        give_ref[at, whole:] = ref[:, pl.ds(give, cols)]


def deal(core, pieces, whole, **more):
    rows, wide = pieces[0].shape
    cols = (wide - whole) // 2
    total = rows * len(pieces)
    return kernel_call(
        functools.partial(deal_kernel, len(pieces), whole),
        [shape_of((total, whole), low), shape_of((total, cols), low), shape_of((total, whole + cols), low)],
        [in_smem] + [in_vmem] * len(pieces),
        [core, *pieces],
        **more,
    )


def attend_back_kernel(scale, pieces, index_ref, w_ref, probs_ref, keys_ref, values_ref, q_ref, raw_ref,
                       gain_ref, cos_ref, sin_ref, *refs):
    da_refs = refs[:pieces]
    kv_near_ref, kv_far_ref, dq_ref, part_ref, *message_refs, da_ref, acc = refs[pieces:]
    step = pl.program_id(0)
    tokens, head_dim = cos_ref.shape
    share = da_refs[0].shape[0]
    width = da_ref.shape[1]
    logit_cols = da_refs[0].shape[1] - width

    @pl.when(step == 0)
    def _():
        for i, ref in enumerate(da_refs):
            da_ref[i * share : (i + 1) * share] = ref[:, :width]
            for k, one in enumerate(message_refs):
                one[i * share : (i + 1) * share, :logit_cols] = ref[:, width:]
        for k, one in enumerate(message_refs):
            cols = one.shape[1] - logit_cols
            start = pl.multiple_of((index_ref[0] ^ k) * cols, 128)
            one[:, logit_cols:] = da_ref[:, pl.ds(start, cols)]
        acc[...] = jnp.zeros_like(acc)
        part_ref[...] = jnp.zeros_like(part_ref)

    dattn = dot(da_ref[...], w_ref[...], 1, 1).astype(low)
    heads = dattn.shape[1] // head_dim
    out_grad = jnp.concatenate(
        [dattn[:, h * head_dim : (h + 1) * head_dim] for h in range(heads)], axis=0
    )
    probs_low = probs_ref[...]
    probs = probs_low.astype(full)
    prob_grad = dot(out_grad, values_ref[...], 1, 1)
    inner = jnp.sum(probs * prob_grad, axis=-1, keepdims=True)
    score_grad = (probs * (prob_grad - inner)).astype(low)
    query_grad = (dot(score_grad, keys_ref[...]) * scale).astype(low).astype(full)
    acc[:, :head_dim] += dot(score_grad, q_ref[...], 0, 0)
    acc[:, head_dim:] += dot(probs_low, out_grad, 0, 0)
    gain = gain_ref[...]
    part = part_ref[...]
    for h in range(heads):
        cols = slice(h * head_dim, (h + 1) * head_dim)
        turned = rotate(query_grad[h * tokens : (h + 1) * tokens], cos_ref[...], -sin_ref[...])
        raw = raw_ref[:, cols]
        inverse = rms_scale(raw)
        part = part + jnp.sum(turned * raw * inverse, axis=0, keepdims=True)
        dq_ref[:, cols] = norm_back(turned, raw, inverse, gain).astype(low)
    part_ref[...] = part

    @pl.when(step == pl.num_programs(0) - 1)
    def _():
        near = kv_near_ref.shape[0]
        for ref, at in ((kv_near_ref, 0), (kv_far_ref, near)):
            ref[:, :head_dim] = (acc[at : at + near, :head_dim] * scale).astype(low)
            ref[:, head_dim:] = acc[at : at + near, head_dim:].astype(low)


def stack_rows(stack, at, row):
    for k in range(row.shape[1] // 128):
        stack[at + k : at + k + 1] = row[:, k * 128 : (k + 1) * 128]


def stack_split(stack, values):
    count = values.shape[0]
    high = values.astype(low).astype(full)
    stack[...] = jnp.zeros_like(stack)
    stack[:count] = high
    stack[count : 2 * count] = (values - high).astype(low).astype(full)


def tail_kernel(pieces, moe_part_ref, query_part_ref, dn_ref, dq_ref, raw_ref, kgain_ref, cos_ref, sin_ref, kw_ref, vw_ref, x_ref,
                inv_ref, *refs):
    kv_refs = refs[:pieces]
    own_ref, *rest_refs, proj_ref, gains_ref, values = refs[pieces:]
    total = kv_refs[0][...].astype(full)
    for ref in kv_refs[1:]:
        total = total + ref[...].astype(full)
    head_dim = raw_ref.shape[1]
    query_cols = dq_ref.shape[1]
    turned = rotate(total[:, :head_dim].astype(low).astype(full), cos_ref[...], -sin_ref[...])
    dv = total[:, head_dim:].astype(low)
    raw = raw_ref[...]
    inverse = rms_scale(raw)
    key_part = jnp.sum(turned * raw * inverse, axis=0, keepdims=True)
    dk = norm_back(turned, raw, inverse, kgain_ref[...]).astype(low)
    proj_ref[:, :query_cols] = dq_ref[...]
    proj_ref[:, query_cols : query_cols + head_dim] = dk
    proj_ref[:, query_cols + head_dim :] = dv
    grad = dn_ref[...] + dot(dk, kw_ref[...], 1, 1) + dot(dv, vw_ref[...], 1, 1)
    blocks, share, _ = x_ref.shape
    width = grad.shape[1]
    part = jnp.zeros((1, width), full)
    for i in range(blocks):
        one = grad[i * share : (i + 1) * share]
        x = x_ref[i].astype(full)
        part = part + jnp.sum(one * x * inv_ref[i * share : (i + 1) * share], axis=0, keepdims=True)
        if i == 0:
            own_ref[...] = one
        else:
            rest_refs[i - 1][:, :width] = one.astype(low)
    stack_rows(values, 0, part)
    stack_rows(values, width // 128, moe_part_ref[...])
    stack_rows(values, 2 * width // 128, query_part_ref[...])
    stack_rows(values, (2 * width + head_dim) // 128, key_part)
    stack_split(gains_ref, values[...])
    for ref in rest_refs:
        for j in range(gains_ref.shape[0] // share):
            cols = slice(width + j * 128, width + (j + 1) * 128)
            ref[:, cols] = gains_ref[j * share : (j + 1) * share].astype(low)


def output_kernel(a_near, a_far, b_near, b_far, out_ref):
    rows, cols = out_ref.shape
    far = b_far.shape[1] - cols
    out_ref[...] = dot(a_near[...], b_near[...], 0, 0) + dot(a_far[:, :rows], b_far[:, far:], 0, 0)


def projection_kernel(pieces, index_ref, a_near, a_far, b_near, b_far, query_ref, key_ref, value_ref, *refs):
    *gain_refs, b, parts = refs
    far = a_far.shape[1] - a_near.shape[1]
    each = a_near.shape[0] // pieces
    rows = b_near.shape[0] // pieces
    more = rows - each
    for i, b_ref in enumerate((b_near, b_far)):
        for k in range(pieces):
            at = i * pieces + k
            b[at * each : (at + 1) * each] = b_ref[k * rows : k * rows + each]
            for j in range(parts.shape[1] // more):
                cols = slice(j * 128, (j + 1) * 128)
                parts[index_ref[0] ^ (2 * k + i), j * more : (j + 1) * more] = b_ref[
                    k * rows + each : (k + 1) * rows, cols
                ].astype(full)
    gains = parts[0]
    for i in range(1, 2 * pieces):
        gains = gains + parts[i]
    count = sum(ref.shape[0] for ref in gain_refs)
    gains = gains[:count] + gains[count : 2 * count]
    at = 0
    for ref in gain_refs:
        ref[...] = gains[at : at + ref.shape[0]]
        at += ref.shape[0]
    half = pieces * each
    total = dot(a_near[...], b[:half], 0, 0) + dot(a_far[:, far:], b[half:], 0, 0)
    cols, more = query_ref.shape[1], key_ref.shape[1]
    query_ref[...] = total[:, :cols]
    key_ref[...] = total[:, cols : cols + more]
    value_ref[...] = total[:, cols + more :]


def router_kernel(index_ref, rows_any, near_ref, far_ref, out_ref, rows, grads, sems):
    part_count, groups, inner, share, _ = rows_any.shape
    copies = []
    for p in range(part_count):
        for c in range(groups):
            half = groups // 2
            mask = 2 * (c % half) + c // half
            for w in range(inner):
                to = (index_ref[0] ^ mask) * (part_count * inner) + (index_ref[1] ^ (p * inner + w))
                copy = pltpu.make_async_copy(rows_any.at[p, c, w], rows.at[to], sems.at[len(copies)])
                copy.start()
                copies.append(copy)
                grad_ref = near_ref if c < half else far_ref
                at = ((c % half) * (part_count * inner) + p * inner + w) * share
                grads[to] = grad_ref[at : at + share, : grads.shape[2]]
    for copy in copies:
        copy.wait()
    count = rows.shape[0] * share
    total = dot(grads[...].reshape(count, grads.shape[2]), rows[...].reshape(count, rows.shape[2]), 0, 0)
    experts = out_ref.shape[0]
    out_ref[...] = total[:experts] + total[experts : 2 * experts]


def place_kernel(pieces, index_ref, *refs):
    piece_refs, out_refs = refs[:pieces], refs[pieces:]
    width = out_refs[0].shape[2]
    for i, ref in enumerate(piece_refs):
        for j, out_ref in enumerate(out_refs):
            out_ref[index_ref[0] ^ i] = ref[:, j * width : (j + 1) * width]


def place_rows(index, pieces, width, count, **more):
    share = pieces[0].shape[0]
    return kernel_call(
        functools.partial(place_kernel, len(pieces)),
        [shape_of((len(pieces), share, width), pieces[0].dtype)] * count,
        [in_smem] + [in_vmem] * len(pieces),
        [index.reshape(1), *pieces],
        **more,
    )


def gather_wt(array):
    return [array] + [swap(array, "wt", m) for m in range(1, lax.axis_size("wt"))]


def near_ctx(array):
    return [array] + [swap(array, "ctx", 2 * k) for k in range(1, lax.axis_size("ctx") // 2)]


def far_ctx(arrays):
    return [swap(one, "ctx", 1) for one in arrays]


def split_low(array):
    high = array.astype(low)
    return high, (array - high.astype(full)).astype(low)


def on_device(
    tokens,
    cotangent,
    routes,
    attn_gain,
    query_gain,
    key_gain,
    w_query,
    key_weight,
    value_weight,
    w_output,
    moe_gain,
    w_router,
    w_gate_up,
    w_down,
):
    _, pair_len, width = tokens.shape
    head_dim = query_gain.shape[0]
    query_cols = w_query.shape[1]
    heads = query_cols // head_dim
    share, top_count = routes.shape
    experts = w_router.shape[1]
    ctx_count = lax.axis_size("ctx")
    wt_count = lax.axis_size("wt")
    half = ctx_count // 2
    ctx_index = lax.axis_index("ctx")
    wt_index = lax.axis_index("wt")
    my_expert = ctx_index * wt_count + wt_index
    scale = head_dim ** (-0.5)
    head_step = 2
    parts = 2
    inner = wt_count // parts
    mask_cols = -(-experts // 128) * 128
    extra_cols = -(-2 * experts // 128) * 128
    index = wt_index.reshape(1)
    chip = (ctx_index >> 1).reshape(1)
    core = (ctx_index & 1).reshape(1)
    router = w_router.T

    def plane_swap(blocks):
        return [swap(blocks[k], "ctx", 2 * k) for k in range(1, half)]

    def joined(pieces):
        return jnp.concatenate(pieces, axis=0) if len(pieces) > 1 else pieces[0]

    def both(pieces, after=()):
        near = join(pieces, after)
        return [near, swap(near, "ctx", 1)]


    place = jnp.arange(pair_len, dtype=jnp.int32)
    offsets = ((place // share) ^ wt_index) * share + place % share
    near_masks = 2 * jnp.arange(half, dtype=jnp.int32)
    masks = jnp.concatenate([near_masks, near_masks + 1])
    own_positions = mirrored(ctx_index, offsets, ctx_count, pair_len // 2)
    key_positions = mirrored(
        (ctx_index ^ masks)[:, None], offsets[None, :], ctx_count, pair_len // 2
    ).reshape(1, -1)
    row_positions = jnp.tile(own_positions, head_step).reshape(-1, 1)
    frequency = rope_base ** (-2.0 * jnp.arange(head_dim // 2, dtype=full) / head_dim)
    angles = own_positions.astype(full)[:, None] * frequency[None, :]
    cosine, sine = jnp.cos(angles), jnp.sin(angles)
    cosine = jnp.concatenate([cosine, cosine], axis=1)
    sine = jnp.concatenate([-sine, sine], axis=1)

    expert_ids = jnp.arange(mask_cols, dtype=jnp.int32)
    own_mask = jnp.any(routes[:, :, None] == expert_ids, axis=1).astype(low)
    block_cols = width // ctx_count
    token_rows, normed_one, inverse_one, raw_key, *kv_messages = kernel_call(
        front_kernel,
        [
            shape_of((wt_count, share, width), low),
            shape_of((pair_len, width), low),
            shape_of((pair_len, 1), full),
            shape_of((pair_len, head_dim), full),
        ]
        + [shape_of((pair_len, 2 * head_dim + 2 * block_cols), low)] * half,
        [in_smem] + [in_vmem] * 7,
        [
            jnp.stack([wt_index, ctx_index >> 1]),
            tokens.reshape(wt_count, share, width),
            attn_gain.reshape(1, -1),
            key_weight,
            value_weight,
            key_gain.reshape(1, -1),
            cosine,
            sine,
        ],
    )

    kv_near = [kv_messages[0]] + plane_swap(kv_messages)
    raw_query, queries = kernel_call(
        query_kernel,
        [shape_of((pair_len, query_cols), full), shape_of((heads * pair_len, head_dim), low)],
        [
            pl.BlockSpec((pair_len, width), lambda i: (0, 0)),
            pl.BlockSpec((width, head_step * head_dim), lambda i: (0, i)),
            pl.BlockSpec((1, head_dim), lambda i: (0, 0)),
            pl.BlockSpec((pair_len, head_dim), lambda i: (0, 0)),
            pl.BlockSpec((pair_len, head_dim), lambda i: (0, 0)),
        ],
        [normed_one, w_query, query_gain.reshape(1, -1), cosine, sine],
        grid=(heads // head_step,),
        out_specs=[
            pl.BlockSpec((pair_len, head_step * head_dim), lambda i: (0, i)),
            pl.BlockSpec((head_step * pair_len, head_dim), lambda i: (i, 0)),
        ],
    )

    grad_near = near_ctx(cotangent[0])
    kv_here, normed_keep, kv_give = deal(core, kv_near, 2 * head_dim)
    kv_got = swap(kv_give, "ctx", 1)
    kv_pieces = [kv_here, kv_got]

    total_keys = ctx_count * pair_len
    attn_rows, probs, keys, values, branch_own, *branch_rest = kernel_call(
        functools.partial(attend_kernel, scale, 2),
        [
            shape_of((pair_len, query_cols), low),
            shape_of((heads * pair_len, total_keys), low),
            shape_of((total_keys, head_dim), low),
            shape_of((total_keys, head_dim), low),
            shape_of((share, width), full),
        ]
        + [shape_of((share, width), low)] * (wt_count - 1),
        [
            pl.BlockSpec((head_step * pair_len, 1), lambda i: (0, 0)),
            pl.BlockSpec((1, total_keys), lambda i: (0, 0)),
            pl.BlockSpec((head_step * pair_len, head_dim), lambda i: (i, 0)),
            in_any,
        ]
        + [pl.BlockSpec(one.shape, lambda i: (0, 0)) for one in kv_pieces],
        [row_positions, key_positions, queries, w_output, *kv_pieces],
        grid=(heads // head_step,),
        out_specs=[
            pl.BlockSpec((pair_len, query_cols), lambda i: (0, 0)),
            pl.BlockSpec((head_step * pair_len, total_keys), lambda i: (i, 0)),
            pl.BlockSpec((total_keys, head_dim), lambda i: (0, 0)),
            pl.BlockSpec((total_keys, head_dim), lambda i: (0, 0)),
        ]
        + [pl.BlockSpec((share, width), lambda i: (0, 0))] * wt_count,
        scratch_shapes=[
            pltpu.VMEM((heads // head_step, pair_len, head_step * head_dim), low),
            pltpu.VMEM(w_output.shape, low),
            pltpu.SemaphoreType.DMA,
        ],
    )
    branch_rest, branch_own, attn_rows = fence(branch_rest, branch_own, attn_rows)
    received = [swap(branch_rest[m - 1], "wt", m) for m in range(1, wt_count)]
    mid_rows, inverse_two, message = kernel_call(
        mid_kernel,
        [
            shape_of((share, width), full),
            shape_of((share, 1), full),
            shape_of((share, width + mask_cols), low),
        ],
        [in_vmem] * (3 + wt_count),
        [token_rows, moe_gain.reshape(1, -1), own_mask, branch_own, *received],
    )
    residual_rows = token_rows[0].astype(full)

    first = join([message] + [swap(message, "wt", m) for m in range(1, inner)])
    others = [swap(message, "wt", m) for m in range(inner, wt_count)]
    grads = [one.reshape(half, wt_count, share, width) for one in both(grad_near, message)]
    rows_first = both(near_ctx(first), others)
    chunks = pair_len // (inner * share)
    second = kernel_call(
        pack_kernel,
        shape_of((inner * share, width + mask_cols + chunks * query_cols), low),
        [in_vmem] * (1 + inner),
        [attn_rows, *others],
    )
    near_second = near_ctx(second)
    places = jnp.stack([my_expert, wt_index])
    sums_cols = width + extra_cols
    results, into = run_expert(
        0, parts, inner, True, rows_first, grads, router, w_gate_up, w_down, places, None, sums_cols,
    )
    results, into, near_second = fence(results, into, near_second)
    rows_second, attn_near = kernel_call(
        unpack_kernel,
        [shape_of((half * inner * share, width + mask_cols), low), shape_of((half * pair_len, query_cols), low)],
        [in_vmem] * half,
        near_second,
    )
    rows_second = [rows_second, swap(rows_second, "ctx", 1)]
    attn_got = swap(attn_near, "ctx", 1)

    def split_parts(near, far_sent):
        cols = near.shape[1]
        total = (near + far_sent).reshape(half, inner * share, cols)
        return [total[k] for k in range(half)]

    def plane_sum(blocks, received):
        total = blocks[0].astype(full)
        for one in received:
            total = total + one.astype(full)
        return total

    def wt_parts(sums):
        return [one[w * share : (w + 1) * share] for one in sums for w in range(inner)]

    back_blocks = [split_parts(results[0], swap(results[1], "ctx", 1))]
    rows_second, back_blocks, into = fence(rows_second, back_blocks, into)
    back_received = [plane_swap(back_blocks[0])]
    results, into = run_expert(
        1, parts, inner, False, rows_second, grads, router, w_gate_up, w_down, places, into, sums_cols,
    )

    results, into, back_received = fence(results, into, back_received)
    back_blocks.append(split_parts(results[0], swap(results[1], "ctx", 1)))
    back_blocks, moe_far, into = fence(back_blocks, results[3], into)
    rows_all, hidden, gate_up_grad, expert_grad = into
    back_received.append(plane_swap(back_blocks[1]))
    moe_far = swap(moe_far, "ctx", 1)
    w_gate_up_grad = dot(rows_all, gate_up_grad, 0, 0)
    w_down_grad = dot(hidden, expert_grad, 0, 0)
    back_received, moe_far, w_gate_up_grad, w_down_grad, attn_rows = fence(
        back_received, moe_far, w_gate_up_grad, w_down_grad, attn_rows
    )
    moe_blocks = [[one[:, sums_cols:] for one in back_blocks[0]], split_parts(results[2], moe_far)]
    moe_received = [[one[:, sums_cols:] for one in back_received[0]]]
    back_blocks[0] = [one[:, :sums_cols] for one in back_blocks[0]]
    back_received[0] = [one[:, :sums_cols] for one in back_received[0]]
    sums = wt_parts([plane_sum(b, r) for b, r in zip(back_blocks, back_received)])
    sums_low = [one.astype(low) for one in sums[1:]]
    sums_low, attn_rows, moe_blocks = fence(sums_low, attn_rows, moe_blocks)
    received = [swap(one, "wt", m + 1) for m, one in enumerate(sums_low)]
    received, moe_blocks = fence(received, moe_blocks)
    summed = plane_sum(sums, received)
    rows_sum = summed[:, :width]
    weight_grads = (
        summed[:, width : width + experts] + summed[:, width + experts : width + 2 * experts]
    )
    chosen = own_mask[:, :experts] > 0.5
    logits = jnp.where(chosen, dot(message[:, :width], router, 1, 1), -1e30)
    shifted = jnp.where(chosen, jnp.exp(logits - jnp.max(logits, axis=-1, keepdims=True)), 0.0)
    own_routes = shifted / jnp.sum(shifted, axis=-1, keepdims=True)
    logits_grad = own_routes * (
        weight_grads - jnp.sum(own_routes * weight_grads, axis=-1, keepdims=True)
    )
    logits_cols = jnp.concatenate(split_low(logits_grad), axis=1)
    router_term = dot(logits_cols, jnp.concatenate([router, router], axis=0), 1, 0)
    normed_two_grad = rows_sum + router_term
    moe_gain_part = jnp.sum(normed_two_grad * mid_rows * inverse_two, axis=0)
    grad_rows = lax.dynamic_slice_in_dim(cotangent[0], wt_index * share, share, 0).astype(full)
    mid_grad = grad_rows + norm_back(normed_two_grad, mid_rows, inverse_two, moe_gain)
    logits_cols = jnp.pad(logits_cols, ((0, 0), (0, extra_cols - 2 * experts)))
    mid_message = jnp.concatenate([mid_grad.astype(low), logits_cols], axis=1)

    mid_message, moe_blocks = fence(mid_message, moe_blocks)
    mid_pieces = gather_wt(mid_message)
    moe_received.append(plane_swap(moe_blocks[1]))
    mid_pieces, moe_received = fence(mid_pieces, moe_received)

    moe_sums = wt_parts([plane_sum(b, r) for b, r in zip(moe_blocks, moe_received)])
    moe_low = [one.astype(low) for one in moe_sums[1:]]
    moe_low, mid_pieces = fence(moe_low, mid_pieces)
    moe_received = [swap(one, "wt", m + 1) for m, one in enumerate(moe_low)]
    kv_part_near, kv_part_far, query_grad, query_gain_part, *logits_messages, _ = kernel_call(
        functools.partial(attend_back_kernel, scale, wt_count),
        [
            shape_of((total_keys // 2, 2 * head_dim), low),
            shape_of((total_keys // 2, 2 * head_dim), low),
            shape_of((pair_len, query_cols), low),
            shape_of((1, head_dim), full),
        ]
        + [shape_of((pair_len, extra_cols + 2 * block_cols), low)] * half
        + [shape_of((pair_len, width), low)],
        [
            in_smem,
            pl.BlockSpec((head_step * head_dim, width), lambda i: (i, 0)),
            pl.BlockSpec((head_step * pair_len, total_keys), lambda i: (i, 0)),
            pl.BlockSpec((total_keys, head_dim), lambda i: (0, 0)),
            pl.BlockSpec((total_keys, head_dim), lambda i: (0, 0)),
            pl.BlockSpec((head_step * pair_len, head_dim), lambda i: (i, 0)),
            pl.BlockSpec((pair_len, head_step * head_dim), lambda i: (0, i)),
            pl.BlockSpec((1, head_dim), lambda i: (0, 0)),
            pl.BlockSpec((pair_len, head_dim), lambda i: (0, 0)),
            pl.BlockSpec((pair_len, head_dim), lambda i: (0, 0)),
        ]
        + [pl.BlockSpec((share, width + extra_cols), lambda i: (0, 0))] * wt_count,
        [
            chip, w_output, probs, keys, values, queries, raw_query, query_gain.reshape(1, -1),
            cosine, sine, *mid_pieces,
        ],
        grid=(heads // head_step,),
        out_specs=[
            pl.BlockSpec((total_keys // 2, 2 * head_dim), lambda i: (0, 0)),
            pl.BlockSpec((total_keys // 2, 2 * head_dim), lambda i: (0, 0)),
            pl.BlockSpec((pair_len, head_step * head_dim), lambda i: (0, i)),
            pl.BlockSpec((1, head_dim), lambda i: (0, 0)),
        ]
        + [pl.BlockSpec((pair_len, extra_cols + 2 * block_cols), lambda i: (0, 0))] * half
        + [pl.BlockSpec((pair_len, width), lambda i: (0, 0))],
        scratch_shapes=[pltpu.VMEM((total_keys, 2 * head_dim), full)],
    )

    kv_part_near, kv_part_far, query_grad, moe_received, logits_messages = fence(
        kv_part_near, kv_part_far, query_grad, moe_received, logits_messages
    )
    kv_near = (kv_part_near + swap(kv_part_far, "ctx", 1)).reshape(half, pair_len, 2 * head_dim)
    kv_near = [kv_near[k] for k in range(half)]
    out_rows = (mid_rows + plane_sum(moe_sums, moe_received)).astype(low)
    kv_near, query_grad, out_rows = fence(kv_near, query_grad, out_rows)
    kv_received = plane_swap(kv_near)
    query_term = dot(query_grad, w_query, 1, 1)
    kv_received, query_term = fence(kv_received, query_term)
    gain_rows = 2 * width // 128 + 2 * head_dim // 128
    gain_blocks = -(-2 * gain_rows // share)
    one_own, *tail_results = kernel_call(
        functools.partial(tail_kernel, half),
        [shape_of((share, width), full)]
        + [shape_of((share, width + gain_blocks * 128), low)] * (wt_count - 1)
        + [
            shape_of((pair_len, query_cols + 2 * head_dim), low),
            shape_of((gain_blocks * share, 128), full),
        ],
        [in_vmem] * (12 + half),
        [
            moe_gain_part.reshape(1, -1), query_gain_part, query_term, query_grad, raw_key,
            key_gain.reshape(1, -1), cosine, sine, key_weight, value_weight, token_rows, inverse_one,
            kv_near[0], *kv_received,
        ],
        after=attn_got,
        through=logits_messages,
        scratch_shapes=[pltpu.VMEM((gain_rows, 128), full)],
    )
    one_rest, (projection_own, gains) = tail_results[: wt_count - 1], tail_results[wt_count - 1 : wt_count + 1]
    logits_messages = tail_results[wt_count + 1 :]
    received = [swap(one, "wt", m + 1) for m, one in enumerate(one_rest)]
    logits_near = [logits_messages[0]] + plane_swap(logits_messages)
    logits_own, mid_keep, logits_give = deal(core, logits_near, extra_cols)
    logits_got = swap(logits_give, "ctx", 1)
    message_rows = pair_len + 16
    last_rows, projection = kernel_call(
        last_kernel,
        [shape_of((share, 2 * width), low), shape_of((message_rows, query_cols + 2 * head_dim), low)],
        [in_smem] + [in_vmem] * (7 + wt_count),
        [
            index, token_rows, inverse_one, attn_gain.reshape(1, -1), mid_grad, out_rows, projection_own,
            gains, one_own, *received,
        ],
        after=logits_near,
        scratch_shapes=[
            pltpu.VMEM((wt_count, gain_blocks * share, 128), full),
            pltpu.VMEM((-(-2 * gain_rows // 16) * 16, 128), full),
        ],
    )

    last_pieces = gather_wt(last_rows)
    projection_near = near_ctx(projection)
    router_grad = kernel_call(
        router_kernel,
        shape_of((experts, width), full),
        [in_smem, in_any, in_vmem, in_vmem],
        [
            jnp.stack([ctx_index, wt_index]),
            rows_all.reshape(parts, ctx_count, inner, share, width),
            logits_own,
            logits_got,
        ],
        scratch_shapes=[
            pltpu.VMEM((ctx_count * wt_count, share, width), low),
            pltpu.VMEM((ctx_count * wt_count, share, extra_cols), low),
            pltpu.SemaphoreType.DMA((ctx_count * wt_count,)),
        ],
    )
    w_output_grad = kernel_call(
        output_kernel,
        shape_of((query_cols, block_cols), full),
        [in_vmem] * 4,
        [attn_near, attn_got, mid_keep, logits_got],
        after=last_rows,
    )
    w_query_grad, w_key_grad, w_value_grad, *gains = kernel_call(
        functools.partial(projection_kernel, half),
        [
            shape_of((block_cols, query_cols), full),
            shape_of((block_cols, head_dim), full),
            shape_of((block_cols, head_dim), full),
        ]
        + [shape_of((size // 128, 128), full) for size in (width, width, head_dim, head_dim)],
        [in_smem] + [in_vmem] * 4,
        [ctx_index.reshape(1), normed_keep, kv_got, *both(projection_near, [last_pieces[1:], w_output_grad, router_grad])],
        scratch_shapes=[
            pltpu.VMEM((total_keys, query_cols + 2 * head_dim), low),
            pltpu.VMEM((ctx_count, -(-2 * gain_rows // 16) * 16, 128), full),
        ],
    )
    attn_gain_grad, moe_gain_grad, query_gain_grad, key_gain_grad = [one.reshape(-1) for one in gains]
    block_out, tokens_grad = place_rows(
        index, last_pieces, width, 2, after=[router_grad, w_output_grad, w_query_grad]
    )
    w_router_grad = router_grad.T

    return (
        block_out.reshape(1, pair_len, width),
        tokens_grad.reshape(1, pair_len, width),
        attn_gain_grad,
        query_gain_grad,
        key_gain_grad,
        w_query_grad,
        w_key_grad,
        w_value_grad,
        w_output_grad,
        moe_gain_grad,
        w_router_grad,
        w_gate_up_grad[None],
        w_down_grad[None],
    )


def solution(mesh):
    in_specs = (
        P(None, "ctx", None),
        P(None, "ctx", None),
        P(("ctx", "wt"), None),
        P(),
        P(),
        P(),
        P(None, "wt"),
        P(None, "wt"),
        P(None, "wt"),
        P("wt", None),
        P(),
        P(),
        P(("ctx", "wt"), None, None),
        P(("ctx", "wt"), None, None),
    )
    out_specs = (
        P(None, "ctx", None),
        P(None, "ctx", None),
        P(),
        P(),
        P(),
        P("ctx", "wt"),
        P("ctx", "wt"),
        P("ctx", "wt"),
        P("wt", "ctx"),
        P(),
        P(),
        P(("ctx", "wt"), None, None),
        P(("ctx", "wt"), None, None),
    )
    return jax.shard_map(
        on_device, mesh=mesh, in_specs=in_specs, out_specs=out_specs, check_vma=False
    )
```

profile of v0, /device:TPU:0, one launch (start us, length us, event | category | flops | bytes accessed | tf_op | source)
XLA Modules:
  0.0 315.2 jit_solution(5309680460827332750)
XLA Ops:
  3.0 3.0 shard_map.237
  6.0 3.0 collective-permute-start
  14.9 3.0 collective-permute-start.16
  17.9 3.2 %collective-permute-done.1.refs_3_ = bf16[128,768]{1,0:T(8,128)(2,1)S(1)} collective-permute-done((bf16[128,768]{1,0:T(8,128)(2,1)}, bf16[128,768]{1,0:T(8,128)(2,1)S(1)}, u32[]{:S(2)}, u32[]{:S(2)}) %collective-permute-start.1) | collective-permute-done | bytes 196640 | tf_op jit(solution)/shard_map/ppermute | solution.py:27
  25.0 4.9 %shard_map.238 = (f32[128,1024]{1,0:T(8,128)}, bf16[1024,128]{1,0:T(8,128)(2,1)}) custom-call(bf16[128,2048]{1,0:T(8,128)(2,1)} %get-tuple-element.201.refs_0_, bf16[2048,1024]{1,0:T(8,128)(2,1)} %refs_1_.2, f32[1,128]{1,0:T(1,128)} %bitcast.59, f32[128,128]{1,0:T(8,128)} %pad_maximum_fusion.refs_6_.refs_3_.refs_8_, ...), custom_call_target="tpu_custom_call" | custom-call | tf_op jit(solution)/shard_map/pallas_call | solution.py:52
  31.4 7.4 %shard_map.240 = (bf16[128,1024]{1,0:T(8,128)(2,1)}, bf16[1024,1024]{1,0:T(8,128)(2,1)}, bf16[1024,128]{1,0:T(8,128)(2,1)}, bf16[1024,128]{1,0:T(8,128)(2,1)}, f...) custom-call(s32[256,1]{1,0:T(8,128)} %copy.39.refs_0_, ...), custom_call_target="tpu_custom_call" | custom-call | tf_op jit(solution)/shard_map/pallas_call | solution.py:52
  43.0 4.6 %collective-permute-done.4.refs_4_ = bf16[32,2048]{1,0:T(8,128)(2,1)S(1)} collective-permute-done((bf16[32,2048]{1,0:T(8,128)(2,1)}, bf16[32,2048]{1,0:T(8,128)(2,1)S(1)}, u32[]{:S(2)}, u32[]{:S(2)}) %collective-permute-start.4) | collective-permute-done | bytes 131104 | tf_op jit(solution)/shard_map/ppermute | solution.py:27
  51.0 3.7 %collective-permute-done.6.refs_6_ = bf16[32,2048]{1,0:T(8,128)(2,1)S(1)} collective-permute-done((bf16[32,2048]{1,0:T(8,128)(2,1)}, bf16[32,2048]{1,0:T(8,128)(2,1)S(1)}, u32[]{:S(2)}, u32[]{:S(2)}) %collective-permute-start.6) | collective-permute-done | bytes 131104 | tf_op jit(solution)/shard_map/ppermute | solution.py:27
  58.6 2.9 shard_map.244
  64.7 5.7 %collective-permute-done.7.refs_1_ = bf16[32,2176]{1,0:T(8,128)(2,1)S(1)} collective-permute-done((bf16[32,2176]{1,0:T(8,128)(2,1)S(1)}, bf16[32,2176]{1,0:T(8,128)(2,1)S(1)}, u32[]{:S(2)}, u32[]{:S(2)}) %collective-permute-start.7) | collective-permute-done | bytes 139296 | tf_op jit(solution)/shard_map/ppermute | solution.py:27
  77.9 5.4 %collective-permute-done.12.refs_5_.refs_2_ = bf16[32,2176]{1,0:T(8,128)(2,1)S(1)} collective-permute-done((bf16[32,2176]{1,0:T(8,128)(2,1)S(1)}, bf16[32,2176]{1,0:T(8,128)(2,1)S(1)}, u32[]{:S(2)}, u32[]{:S(2)}) %collective-permute-start.12) | collective-permute-done | bytes 139296 | tf_op jit(solution)/shard_map/ppermute | solution.py:27
  83.3 3.0 collective-permute-done.9.refs_2_
  98.6 21.9 %shard_map.245 = (bf16[256,4224]{1,0:T(8,128)(2,1)}, bf16[256,4224]{1,0:T(8,128)(2,1)}, bf16[1024,2048]{1,0:T(8,128)(2,1)}, bf16[1024,768]{1,0:T(8,128)(2,1)}, b...) custom-call(s32[2]{0:T(128)} %pad_add_fusion.1.refs_0_, bf16[256,2176]{1,0:T(8,128)(2,1)} %shard_map.243.refs_1_, ...), custom_call_target="tpu_custom_call" | custom-call | tf_op jit(solution)/shard_map/pallas_call | solution.py:52
  120.6 3.1 shard_map.247
  131.1 22.1 %shard_map.248 = (bf16[256,2176]{1,0:T(8,128)(2,1)}, bf16[256,2176]{1,0:T(8,128)(2,1)}, bf16[256,2048]{1,0:T(8,128)(2,1)}, bf16[256,2048]{1,0:T(8,128)(2,1)}, bf...) custom-call(s32[2]{0:T(128)} %pad_add_fusion.1.refs_0_, ...), custom_call_target="tpu_custom_call", output_to_operand_aliasing={{4}: (8, {}), {5}: (9, {}), {6}: (10, {}), {7}: (11, {})} | custom-call | tf_op jit(solution)/shard_map/pallas_call | solution.py:52
  154.8 2.9 collective-permute-done.26
  162.9 11.7 %fusion.30 = f32[2048,1536]{1,0:T(8,128)} fusion(bf16[1024,2048]{1,0:T(8,128)(2,1)S(1)} %copy-done.1, bf16[1024,1536]{1,0:T(8,128)(2,1)} %get-tuple-element.272), kind=kOutput, calls=%fused_computation.76 | convolution fusion | flops 6442450944 | bytes 19922944 | tf_op jit(solution)/shard_map/dot_general | solution.py:22
  174.6 5.4 %fusion.31 = f32[768,2048]{1,0:T(8,128)} fusion(bf16[1024,768]{1,0:T(8,128)(2,1)S(1)} %copy-done.3, bf16[1024,2048]{1,0:T(8,128)(2,1)S(1)} %copy-done), kind=kOutput, calls=%fused_computation.77 | convolution fusion | flops 3221225472 | bytes 12058624 | tf_op jit(solution)/shard_map/dot_general | solution.py:22
  187.9 3.3 %collective-permute-done.31 = bf16[32,2176]{1,0:T(8,128)(2,1)S(1)} collective-permute-done((bf16[32,2176]{1,0:T(8,128)(2,1)S(1)}, bf16[32,2176]{1,0:T(8,128)(2,1)S(1)}, u32[]{:S(2)}, u32[]{:S(2)}) %collective-permute-start.31) | collective-permute-done | bytes 139296 | tf_op jit(solution)/shard_map/ppermute | solution.py:27
  191.2 5.2 %collective-permute-done.32 = bf16[32,2176]{1,0:T(8,128)(2,1)S(1)} collective-permute-done((bf16[32,2176]{1,0:T(8,128)(2,1)S(1)}, bf16[32,2176]{1,0:T(8,128)(2,1)S(1)}, u32[]{:S(2)}, u32[]{:S(2)}) %collective-permute-start.32) | collective-permute-done | bytes 139296 | tf_op jit(solution)/shard_map/ppermute | solution.py:27
  199.5 3.1 collective-permute-start.34
  212.1 5.5 %collective-permute-done.35.refs_12_ = bf16[32,2176]{1,0:T(8,128)(2,1)S(1)} collective-permute-done((bf16[32,2176]{1,0:T(8,128)(2,1)S(1)}, bf16[32,2176]{1,0:T(8,128)(2,1)S(1)}, u32[]{:S(2)}, u32[]{:S(2)}) %collective-permute-start.35) | collective-permute-done | bytes 139296 | tf_op jit(solution)/shard_map/ppermute | solution.py:27
  218.7 2.8 collective-permute-start.40
  223.9 10.8 %shard_map.249 = (bf16[512,256]{1,0:T(8,128)(2,1)}, bf16[512,256]{1,0:T(8,128)(2,1)}, bf16[128,1024]{1,0:T(8,128)(2,1)}, f32[1,128]{1,0:T(1,128)}, bf16[128,640]...) custom-call(s32[1]{0:T(128)} %bitcast.1.refs_0_, ...), custom_call_target="tpu_custom_call" | custom-call | tf_op jit(solution)/shard_map/pallas_call | solution.py:52
  241.8 4.8 %fusion.32.refs_2_ = f32[128,2048]{1,0:T(8,128)} fusion(bf16[128,1024]{1,0:T(8,128)(2,1)} %get-tuple-element.346.refs_3_, bf16[2048,1024]{1,0:T(8,128)(2,1)} %refs_1_.2), kind=kOutput, calls=%fused_computation.78 | convolution fusion | flops 536870912 | bytes 5505024 | tf_op jit(solution)/shard_map/dot_general | solution.py:22
  247.7 3.5 %shard_map.250 = (f32[32,2048]{1,0:T(8,128)}, bf16[32,2432]{1,0:T(8,128)(2,1)}, bf16[32,2432]{1,0:T(8,128)(2,1)}, bf16[32,2432]{1,0:T(8,128)(2,1)}, bf16[128,128...) custom-call(f32[1,2048]{1,0:T(1,128)} %bitcast.57, ...), custom_call_target="tpu_custom_call", output_to_operand_aliasing={{6}: (17, {}), {7}: (18, {}), {8}: (19, {}), {9}: (20, {})} | custom-call | tf_op jit(solution)/shard_map/pallas_call | solution.py:52
  264.3 4.9 %collective-permute-done.49.refs_10_ = bf16[32,2432]{1,0:T(8,128)(2,1)S(1)} collective-permute-done((bf16[32,2432]{1,0:T(8,128)(2,1)}, bf16[32,2432]{1,0:T(8,128)(2,1)S(1)}, u32[]{:S(2)}, u32[]{:S(2)}) %collective-permute-start.49) | collective-permute-done | bytes 155680 | tf_op jit(solution)/shard_map/ppermute | solution.py:27
  285.1 3.5 %shard_map.254.refs_7_.refs_6_ = f32[1024,256]{1,0:T(8,128)} custom-call(bf16[512,1024]{1,0:T(8,128)(2,1)} %get-tuple-element.353.refs_0_, bf16[512,1024]{1,0:T(8,128)(2,1)} %copy-done.4, bf16[512,256]{1,0:T(8,128)(2,1)} %get-tuple-element.371.refs_2_, bf16[512,384]{1,0:T(8,128)(2,1)} %copy-done.8, bf16[32,4096]{1,0:T(8,128)(2,1)} %get-tuple-element.368.refs_4_.refs_1_), custom_call_target="tpu_custom_call" | custom-call | tf_op jit(solution)/shard_map/pallas_call | solution.py:52
  288.6 5.0 %shard_map.253.refs_8_.refs_5_ = f32[32,2048]{1,0:T(8,128)} custom-call(s32[2]{0:T(128)} %pad_add_fusion.2.refs_0_, bf16[2,8,2,32,2048]{4,3,2,1,0:T(8,128)(2,1)} %bitcast.41, bf16[512,128]{1,0:T(8,128)(2,1)} %get-tuple-element.369.refs_2_, bf16[512,384]{1,0:T(8,128)(2,1)} %copy-done.8), custom_call_target="tpu_custom_call" | custom-call | tf_op jit(solution)/shard_map/pallas_call | solution.py:52
  293.6 6.5 %collective-permute-done.55.refs_5_.refs_3_ = bf16[32,4096]{1,0:T(8,128)(2,1)S(1)} collective-permute-done((bf16[32,4096]{1,0:T(8,128)(2,1)}, bf16[32,4096]{1,0:T(8,128)(2,1)S(1)}, u32[]{:S(2)}, u32[]{:S(2)}) %collective-permute-start.55) | collective-permute-done | bytes 262176 | tf_op jit(solution)/shard_map/ppermute | solution.py:27
  304.4 3.5 %collective-permute-done.61.refs_4_ = bf16[576,1280]{1,0:T(8,128)(2,1)S(1)} collective-permute-done((bf16[576,1280]{1,0:T(8,128)(2,1)}, bf16[576,1280]{1,0:T(8,128)(2,1)S(1)}, u32[]{:S(2)}, u32[]{:S(2)}) %collective-permute-start.61) | collective-permute-done | bytes 1474592 | tf_op jit(solution)/shard_map/ppermute | solution.py:27
  309.0 4.0 %shard_map.256 = (f32[256,1024]{1,0:T(8,128)}, f32[256,128]{1,0:T(8,128)}, f32[256,128]{1,0:T(8,128)}, f32[16,128]{1,0:T(8,128)}, f32[16,128]{1,0:T(8,128)}, /*index=5*/f32[1,128]{1,0:T(1,128)}, f32[1,128]{1,0:T(1,128)}) custom-call(s32[1]{0:T(128)} %bitcast.17.refs_0_, bf16[512,256]{1,0:T(8,128)(2,1)} %get-tuple-element.372.refs_1_, ...), custom_call_target="tpu_custom_call" | custom-call | tf_op jit(solution)/shard_map/pallas_call | solution.py:52
  (281 shorter events, 130.5 us)
Async XLA Ops:
  10.5 46.9 %collective-permute-start.14 = (bf16[128,2048]{1,0:T(8,128)(2,1)}, bf16[128,2048]{1,0:T(8,128)(2,1)S(1)}, u32[]{:S(2)}, u32[]{:S(2)}) collective-permute-start(bf16[128,2048]{1,0:T(8,128)(2,1)} %bitcast.49), channel_id=1, source_target_pairs={{0,8},{4,12},{8,0},{12,4},{16,24},{20,28},{24,16},{28,20},{1,9},{5... | collective-permute-start | bytes 1572872 | tf_op jit(solution)/shard_map/ppermute | solution.py:27
  12.4 45.0 %collective-permute-start.15 = (bf16[128,2048]{1,0:T(8,128)(2,1)}, bf16[128,2048]{1,0:T(8,128)(2,1)S(1)}, u32[]{:S(2)}, u32[]{:S(2)}) collective-permute-start(bf16[128,2048]{1,0:T(8,128)(2,1)} %bitcast.50), channel_id=1, source_target_pairs={{0,16},{4,20},{8,24},{12,28},{16,0},{20,4},{24,8},{28,12},{1,17},{... | collective-permute-start | bytes 1572872 | tf_op jit(solution)/shard_map/ppermute | solution.py:27
  14.9 42.5 %collective-permute-start.16 = (bf16[128,2048]{1,0:T(8,128)(2,1)}, bf16[128,2048]{1,0:T(8,128)(2,1)S(1)}, u32[]{:S(2)}, u32[]{:S(2)}) collective-permute-start(bf16[128,2048]{1,0:T(8,128)(2,1)} %bitcast.51), channel_id=1, source_target_pairs={{0,24},{4,28},{8,16},{12,20},{16,8},{20,12},{24,0},{28,4},{1,25},{... | collective-permute-start | bytes 1572872 | tf_op jit(solution)/shard_map/ppermute | solution.py:27
  61.5 35.4 %collective-permute-start.17 = (bf16[512,2048]{1,0:T(8,128)(2,1)}, bf16[512,2048]{1,0:T(8,128)(2,1)S(1)}, u32[]{:S(2)}, u32[]{:S(2)}) collective-permute-start(bf16[512,2048]{1,0:T(8,128)(2,1)} %shard_map.244), channel_id=1, source_target_pairs={{0,4},{4,0},{8,12},{12,8},{16,20},{20,16},{24,28},{28,24},{1,5},{5... | collective-permute-start | bytes 6291464 | tf_op jit(solution)/shard_map/ppermute | solution.py:27
  63.1 13.2 %collective-permute-start.11 = (bf16[32,2176]{1,0:T(8,128)(2,1)S(1)}, bf16[32,2176]{1,0:T(8,128)(2,1)S(1)}, u32[]{:S(2)}, u32[]{:S(2)}) collective-permute-start(bf16[32,2176]{1,0:T(8,128)(2,1)S(1)} %copy-done.21), channel_id=1, source_target_pairs={{0,2},{1,3},{2,0},{3,1},{4,6},{5,7},{6,4},{7,5},{8,10},{9,11},{10,... | collective-permute-start | bytes 417800 | tf_op jit(solution)/shard_map/ppermute | solution.py:27
  73.8 12.6 %collective-permute-start.9 = (bf16[64,2176]{1,0:T(8,128)(2,1)}, bf16[64,2176]{1,0:T(8,128)(2,1)S(1)}, u32[]{:S(2)}, u32[]{:S(2)}) collective-permute-start(bf16[64,2176]{1,0:T(8,128)(2,1)} %shard_map.242.refs_0_), channel_id=1, source_target_pairs={{0,16},{4,20},{8,24},{12,28},{16,0},{20,4},{24,8},{28,12},{1,17},{... | collective-permute-start | bytes 835592 | tf_op jit(solution)/shard_map/ppermute | solution.py:27
  74.9 13.0 %collective-permute-start.10 = (bf16[64,2176]{1,0:T(8,128)(2,1)}, bf16[64,2176]{1,0:T(8,128)(2,1)S(1)}, u32[]{:S(2)}, u32[]{:S(2)}) collective-permute-start(bf16[64,2176]{1,0:T(8,128)(2,1)} %shard_map.242.refs_0_), channel_id=1, source_target_pairs={{0,24},{4,28},{8,16},{12,20},{16,8},{20,12},{24,0},{28,4},{1,25},{... | collective-permute-start | bytes 835592 | tf_op jit(solution)/shard_map/ppermute | solution.py:27
  92.9 27.7 %collective-permute-start.18 = (bf16[64,4224]{1,0:T(8,128)(2,1)}, bf16[64,4224]{1,0:T(8,128)(2,1)}, u32[]{:S(2)}, u32[]{:S(2)}) collective-permute-start(bf16[64,4224]{1,0:T(8,128)(2,1)} %shard_map.246.refs_0_), channel_id=1, source_target_pairs={{0,8},{4,12},{8,0},{12,4},{16,24},{20,28},{24,16},{28,20},{1,9},{5... | collective-permute-start | bytes 1622024 | tf_op jit(solution)/shard_map/ppermute | solution.py:27
  94.3 26.3 %collective-permute-start.19 = (bf16[64,4224]{1,0:T(8,128)(2,1)}, bf16[64,4224]{1,0:T(8,128)(2,1)}, u32[]{:S(2)}, u32[]{:S(2)}) collective-permute-start(bf16[64,4224]{1,0:T(8,128)(2,1)} %shard_map.246.refs_0_), channel_id=1, source_target_pairs={{0,16},{4,20},{8,24},{12,28},{16,0},{20,4},{24,8},{28,12},{1,17},{... | collective-permute-start | bytes 1622024 | tf_op jit(solution)/shard_map/ppermute | solution.py:27
  95.9 24.8 %collective-permute-start.20 = (bf16[64,4224]{1,0:T(8,128)(2,1)}, bf16[64,4224]{1,0:T(8,128)(2,1)}, u32[]{:S(2)}, u32[]{:S(2)}) collective-permute-start(bf16[64,4224]{1,0:T(8,128)(2,1)} %shard_map.246.refs_0_), channel_id=1, source_target_pairs={{0,24},{4,28},{8,16},{12,20},{16,8},{20,12},{24,0},{28,4},{1,25},{... | collective-permute-start | bytes 1622024 | tf_op jit(solution)/shard_map/ppermute | solution.py:27
  127.5 25.6 %collective-permute-start.23 = (bf16[64,4224]{1,0:T(8,128)(2,1)S(1)}, bf16[64,4224]{1,0:T(8,128)(2,1)}, u32[]{:S(2)}, u32[]{:S(2)}) collective-permute-start(bf16[64,4224]{1,0:T(8,128)(2,1)S(1)} %get-tuple-element.239), channel_id=1, source_target_pairs={{0,8},{4,12},{8,0},{12,4},{16,24},{20,28},{24,16},{28,20},{1,9},{5... | collective-permute-start | bytes 1622024 | tf_op jit(solution)/shard_map/ppermute | solution.py:27
  129.0 25.7 %collective-permute-start.24 = (bf16[64,4224]{1,0:T(8,128)(2,1)S(1)}, bf16[64,4224]{1,0:T(8,128)(2,1)}, u32[]{:S(2)}, u32[]{:S(2)}) collective-permute-start(bf16[64,4224]{1,0:T(8,128)(2,1)S(1)} %get-tuple-element.240), channel_id=1, source_target_pairs={{0,16},{4,20},{8,24},{12,28},{16,0},{20,4},{24,8},{28,12},{1,17},{... | collective-permute-start | bytes 1622024 | tf_op jit(solution)/shard_map/ppermute | solution.py:27
  130.6 24.2 %collective-permute-start.25 = (bf16[64,4224]{1,0:T(8,128)(2,1)S(1)}, bf16[64,4224]{1,0:T(8,128)(2,1)}, u32[]{:S(2)}, u32[]{:S(2)}) collective-permute-start(bf16[64,4224]{1,0:T(8,128)(2,1)S(1)} %get-tuple-element.241), channel_id=1, source_target_pairs={{0,24},{4,28},{8,16},{12,20},{16,8},{20,12},{24,0},{28,4},{1,25},{... | collective-permute-start | bytes 1622024 | tf_op jit(solution)/shard_map/ppermute | solution.py:27
  159.3 20.6 %collective-permute-start.27 = (bf16[64,2176]{1,0:T(8,128)(2,1)S(1)}, bf16[64,2176]{1,0:T(8,128)(2,1)S(1)}, u32[]{:S(2)}, u32[]{:S(2)}) collective-permute-start(bf16[64,2176]{1,0:T(8,128)(2,1)S(1)} %get-tuple-element.267), channel_id=1, source_target_pairs={{0,8},{4,12},{8,0},{12,4},{16,24},{20,28},{24,16},{28,20},{1,9},{5... | collective-permute-start | bytes 835592 | tf_op jit(solution)/shard_map/ppermute | solution.py:27
  160.7 19.3 %collective-permute-start.28 = (bf16[64,2176]{1,0:T(8,128)(2,1)S(1)}, bf16[64,2176]{1,0:T(8,128)(2,1)S(1)}, u32[]{:S(2)}, u32[]{:S(2)}) collective-permute-start(bf16[64,2176]{1,0:T(8,128)(2,1)S(1)} %get-tuple-element.268), channel_id=1, source_target_pairs={{0,16},{4,20},{8,24},{12,28},{16,0},{20,4},{24,8},{28,12},{1,17},{... | collective-permute-start | bytes 835592 | tf_op jit(solution)/shard_map/ppermute | solution.py:27
  161.5 18.5 %collective-permute-start.29 = (bf16[64,2176]{1,0:T(8,128)(2,1)S(1)}, bf16[64,2176]{1,0:T(8,128)(2,1)S(1)}, u32[]{:S(2)}, u32[]{:S(2)}) collective-permute-start(bf16[64,2176]{1,0:T(8,128)(2,1)S(1)} %get-tuple-element.269), channel_id=1, source_target_pairs={{0,24},{4,28},{8,16},{12,20},{16,8},{20,12},{24,0},{28,4},{1,25},{... | collective-permute-start | bytes 835592 | tf_op jit(solution)/shard_map/ppermute | solution.py:27
  162.9 17.1 %collective-permute-start.30 = (bf16[256,2048]{1,0:T(8,128)(2,1)S(1)}, bf16[256,2048]{1,0:T(8,128)(2,1)S(1)}, u32[]{:S(2)}, u32[]{:S(2)}) collective-permute-start(bf16[256,2048]{1,0:T(8,128)(2,1)S(1)} %copy-done.57), channel_id=1, source_target_pairs={{0,4},{4,0},{8,12},{12,8},{16,20},{20,16},{24,28},{28,24},{1,5},{5... | collective-permute-start | bytes 3145736 | tf_op jit(solution)/shard_map/ppermute | solution.py:27
  182.9 13.5 %collective-permute-start.32 = (bf16[32,2176]{1,0:T(8,128)(2,1)S(1)}, bf16[32,2176]{1,0:T(8,128)(2,1)S(1)}, u32[]{:S(2)}, u32[]{:S(2)}) collective-permute-start(bf16[32,2176]{1,0:T(8,128)(2,1)S(1)} %get-tuple-element.285), channel_id=1, source_target_pairs={{0,2},{1,3},{2,0},{3,1},{4,6},{5,7},{6,4},{7,5},{8,10},{9,11},{10,... | collective-permute-start | bytes 417800 | tf_op jit(solution)/shard_map/ppermute | solution.py:27
  202.6 15.0 %collective-permute-start.37 = (bf16[64,2048]{1,0:T(8,128)(2,1)S(1)}, bf16[64,2048]{1,0:T(8,128)(2,1)S(1)}, u32[]{:S(2)}, u32[]{:S(2)}) collective-permute-start(bf16[64,2048]{1,0:T(8,128)(2,1)S(1)} %copy-done.36), channel_id=1, source_target_pairs={{0,8},{4,12},{8,0},{12,4},{16,24},{20,28},{24,16},{28,20},{1,9},{5... | collective-permute-start | bytes 786440 | tf_op jit(solution)/shard_map/ppermute | solution.py:27
  203.9 13.8 %collective-permute-start.38 = (bf16[64,2048]{1,0:T(8,128)(2,1)S(1)}, bf16[64,2048]{1,0:T(8,128)(2,1)S(1)}, u32[]{:S(2)}, u32[]{:S(2)}) collective-permute-start(bf16[64,2048]{1,0:T(8,128)(2,1)S(1)} %copy-done.35), channel_id=1, source_target_pairs={{0,16},{4,20},{8,24},{12,28},{16,0},{20,4},{24,8},{28,12},{1,17},{... | collective-permute-start | bytes 786440 | tf_op jit(solution)/shard_map/ppermute | solution.py:27
  204.8 13.6 %collective-permute-start.39 = (bf16[64,2048]{1,0:T(8,128)(2,1)S(1)}, bf16[64,2048]{1,0:T(8,128)(2,1)S(1)}, u32[]{:S(2)}, u32[]{:S(2)}) collective-permute-start(bf16[64,2048]{1,0:T(8,128)(2,1)S(1)} %get-tuple-element.309), channel_id=1, source_target_pairs={{0,24},{4,28},{8,16},{12,20},{16,8},{20,12},{24,0},{28,4},{1,25},{... | collective-permute-start | bytes 786440 | tf_op jit(solution)/shard_map/ppermute | solution.py:27
  218.7 16.1 %collective-permute-start.40 = (bf16[32,2048]{1,0:T(8,128)(2,1)S(1)}, bf16[32,2048]{1,0:T(8,128)(2,1)S(1)}, u32[]{:S(2)}, u32[]{:S(2)}) collective-permute-start(bf16[32,2048]{1,0:T(8,128)(2,1)S(1)} %slice.236), channel_id=1, source_target_pairs={{0,1},{1,0},{2,3},{3,2},{4,5},{5,4},{6,7},{7,6},{8,9},{9,8},{10,11... | collective-permute-start | bytes 393224 | tf_op jit(solution)/shard_map/ppermute | solution.py:27
  221.5 13.3 %collective-permute-start.41 = (bf16[32,2048]{1,0:T(8,128)(2,1)S(1)}, bf16[32,2048]{1,0:T(8,128)(2,1)S(1)}, u32[]{:S(2)}, u32[]{:S(2)}) collective-permute-start(bf16[32,2048]{1,0:T(8,128)(2,1)S(1)} %get-tuple-element.329), channel_id=1, source_target_pairs={{0,2},{1,3},{2,0},{3,1},{4,6},{5,7},{6,4},{7,5},{8,10},{9,11},{10,... | collective-permute-start | bytes 393224 | tf_op jit(solution)/shard_map/ppermute | solution.py:27
  221.9 12.9 %collective-permute-start.42 = (bf16[32,2048]{1,0:T(8,128)(2,1)S(1)}, bf16[32,2048]{1,0:T(8,128)(2,1)S(1)}, u32[]{:S(2)}, u32[]{:S(2)}) collective-permute-start(bf16[32,2048]{1,0:T(8,128)(2,1)S(1)} %get-tuple-element.330), channel_id=1, source_target_pairs={{0,3},{1,2},{2,1},{3,0},{4,7},{5,6},{6,5},{7,4},{8,11},{9,10},{10,... | collective-permute-start | bytes 393224 | tf_op jit(solution)/shard_map/ppermute | solution.py:27
  223.9 22.7 %collective-permute-start.47 = (bf16[512,1024]{1,0:T(8,128)(2,1)S(1)}, bf16[512,1024]{1,0:T(8,128)(2,1)S(1)}, u32[]{:S(2)}, u32[]{:S(2)}) collective-permute-start(bf16[512,1024]{1,0:T(8,128)(2,1)S(1)} %copy-done.17), channel_id=1, source_target_pairs={{0,4},{4,0},{8,12},{12,8},{16,20},{20,16},{24,28},{28,24},{1,5},{5... | collective-permute-start | bytes 3145736 | tf_op jit(solution)/shard_map/ppermute | solution.py:27
  255.7 13.5 %collective-permute-start.49 = (bf16[32,2432]{1,0:T(8,128)(2,1)}, bf16[32,2432]{1,0:T(8,128)(2,1)S(1)}, u32[]{:S(2)}, u32[]{:S(2)}) collective-permute-start(bf16[32,2432]{1,0:T(8,128)(2,1)} %get-tuple-element.362), channel_id=1, source_target_pairs={{0,2},{1,3},{2,0},{3,1},{4,6},{5,7},{6,4},{7,5},{8,10},{9,11},{10,... | collective-permute-start | bytes 466952 | tf_op jit(solution)/shard_map/ppermute | solution.py:27
  264.3 18.0 %collective-permute-start.57 = (bf16[512,384]{1,0:T(8,128)(2,1)}, bf16[512,384]{1,0:T(8,128)(2,1)S(1)}, u32[]{:S(2)}, u32[]{:S(2)}) collective-permute-start(bf16[512,384]{1,0:T(8,128)(2,1)} %get-tuple-element.370), channel_id=1, source_target_pairs={{0,4},{4,0},{8,12},{12,8},{16,20},{20,16},{24,28},{28,24},{1,5},{5... | collective-permute-start | bytes 1179656 | tf_op jit(solution)/shard_map/ppermute | solution.py:27
  275.0 25.1 %collective-permute-start.58 = (bf16[144,1280]{1,0:T(8,128)(2,1)}, bf16[144,1280]{1,0:T(8,128)(2,1)S(1)}, u32[]{:S(2)}, u32[]{:S(2)}) collective-permute-start(bf16[144,1280]{1,0:T(8,128)(2,1)} %get-tuple-element.373.refs_0_), channel_id=1, source_target_pairs={{0,8},{4,12},{8,0},{12,4},{16,24},{20,28},{24,16},{28,20},{1,9},{5... | collective-permute-start | bytes 1105928 | tf_op jit(solution)/shard_map/ppermute | solution.py:27
  276.3 23.9 %collective-permute-start.59 = (bf16[144,1280]{1,0:T(8,128)(2,1)}, bf16[144,1280]{1,0:T(8,128)(2,1)S(1)}, u32[]{:S(2)}, u32[]{:S(2)}) collective-permute-start(bf16[144,1280]{1,0:T(8,128)(2,1)} %get-tuple-element.373.refs_0_), channel_id=1, source_target_pairs={{0,16},{4,20},{8,24},{12,28},{16,0},{20,4},{24,8},{28,12},{1,17},{... | collective-permute-start | bytes 1105928 | tf_op jit(solution)/shard_map/ppermute | solution.py:27
  277.1 23.0 %collective-permute-start.60 = (bf16[144,1280]{1,0:T(8,128)(2,1)}, bf16[144,1280]{1,0:T(8,128)(2,1)S(1)}, u32[]{:S(2)}, u32[]{:S(2)}) collective-permute-start(bf16[144,1280]{1,0:T(8,128)(2,1)} %get-tuple-element.373.refs_0_), channel_id=1, source_target_pairs={{0,24},{4,28},{8,16},{12,20},{16,8},{20,12},{24,0},{28,4},{1,25},{... | collective-permute-start | bytes 1105928 | tf_op jit(solution)/shard_map/ppermute | solution.py:27
  280.4 19.7 %collective-permute-start.55 = (bf16[32,4096]{1,0:T(8,128)(2,1)}, bf16[32,4096]{1,0:T(8,128)(2,1)S(1)}, u32[]{:S(2)}, u32[]{:S(2)}) collective-permute-start(bf16[32,4096]{1,0:T(8,128)(2,1)} %get-tuple-element.368.refs_4_.refs_1_), channel_id=1, source_target_pairs={{0,2},{1,3},{2,0},{3,1},{4,6},{5,7},{6,4},{7,5},{8,10},{9,11},{10,... | collective-permute-start | bytes 786440 | tf_op jit(solution)/shard_map/ppermute | solution.py:27
  282.4 17.7 %collective-permute-start.56 = (bf16[32,4096]{1,0:T(8,128)(2,1)}, bf16[32,4096]{1,0:T(8,128)(2,1)S(1)}, u32[]{:S(2)}, u32[]{:S(2)}) collective-permute-start(bf16[32,4096]{1,0:T(8,128)(2,1)} %get-tuple-element.368.refs_4_.refs_1_), channel_id=1, source_target_pairs={{0,3},{1,2},{2,1},{3,0},{4,7},{5,6},{6,5},{7,4},{8,11},{9,10},{10,... | collective-permute-start | bytes 786440 | tf_op jit(solution)/shard_map/ppermute | solution.py:27
  (88 other events, 563.7 us)
where the time goes:
time: 318 us; the launch traced here: 315 us
  Pallas kernels  112 us (35%)
  starting transfers between devices  77.4 us (24%)
  waiting for transfers between devices  68.1 us (21%)
  matrix products  22.9 us (7%)
  local copies, waits for them, and re-layouts  18.6 us (6%)
  other arithmetic  15.1 us (5%)
    pallas_call x21, Pallas kernels, kernel_call(): pl.pallas_call(body, out_shape=outs + [shape_of(one.shape, one.dtype) for...  112 us
    ppermute x62, starting transfers between devices, swap(): return lax.ppermute(array, axis, [(i, i ^ mask) for i in range(count)])  77.4 us
    ppermute x62, waiting for transfers between devices, swap(): return lax.ppermute(array, axis, [(i, i ^ mask) for i in range(count)])  68.1 us
    dot_general x5, matrix products, dot(): lax.dot_general(a, b, (((a_dim,), (b_dim,)), ((), ())), preferred_element...  22.9 us
    unnamed x117, local copies, waits for them, and re-layouts  13 us
  transfers between devices with their start and end apart: 62, of which 22 were waited for; matrix products, arithmetic and copies ran while one was open for 11% of the time, Pallas kernels for 30%

commit v1 on v0

--- a/solution.py
+++ b/solution.py
@@ -168,55 +168,76 @@
 
 
 def expert_kernel(
-    tiles, first, inner, merged, index_ref, row_near, row_far, grad_near, grad_far, router_ref,
-    gu_any, down_any, *refs
+    part, inner, merged, index_ref, row_near, row_far, grad_near, grad_far, router_ref, gu_any, down_any, *refs
 ):
     if merged:
         near_ref, far_ref, *refs = refs
         moe_near_ref, moe_far_ref = near_ref, far_ref
     else:
         near_ref, far_ref, moe_near_ref, moe_far_ref, *refs = refs
-    x_ref, hidden_ref, dgu_ref, deo_ref, x_tile, g_tile, gu, down, sems = refs
+    all_any, x_ref, hidden_ref, dgu_ref, deo_ref, x_tile, g_tile, gu, down, sems = refs
     step = pl.program_id(0)
-    width = g_tile.shape[1]
-    ffw = down.shape[0]
+    rows, width = g_tile.shape
+    tile = rows // 2
+    slots, ffw = hidden_ref.shape
     experts = router_ref.shape[0]
     expert = index_ref[0]
-    chips, _, share, _ = grad_near.shape
-    copy_gu = pltpu.make_async_copy(gu_any.at[0], gu, sems.at[0])
-    copy_down = pltpu.make_async_copy(down_any.at[0], down, sems.at[1])
+    share = grad_near.shape[2]
+    each = tile // (inner * share)
+    half_rows = row_near.shape[0]
+    x_in, x_out, g_in = [], [], []
+    used = 0
+    for i, ref in enumerate((row_near, row_far)):
+        here = x_tile.at[pl.ds(i * tile, tile)]
+        x_in.append(pltpu.make_async_copy(ref.at[pl.ds(step * tile, tile)], here, sems.at[used]))
+        to = (2 * part + i) * half_rows + step * tile
+        x_out.append(
+            pltpu.make_async_copy(
+                x_tile.at[pl.ds(i * tile, tile), pl.ds(0, width)], all_any.at[pl.ds(to, tile)], sems.at[used + 1]
+            )
+        )
+        used += 2
+    for i, ref in enumerate((grad_near, grad_far)):
+        for c in range(each):
+            for w in range(inner):
+                at = i * tile + (c * inner + w) * share
+                source = ref.at[step * each + c, index_ref[1] ^ (part * inner + w)]
+                g_in.append(pltpu.make_async_copy(source, g_tile.at[pl.ds(at, share)], sems.at[used]))
+                used += 1
+    copy_gu = pltpu.make_async_copy(gu_any.at[0], gu, sems.at[used])
+    copy_down = pltpu.make_async_copy(down_any.at[0], down, sems.at[used + 1])
+    for one in x_in + g_in:
+        one.start()
 
     @pl.when(step == 0)
     def _():
         copy_gu.start()
         copy_down.start()
 
-    def load(row_ref, grad_ref):
-        x_tile[...] = row_ref[...]
-        for c in range(chips):
-            for w in range(inner):
-                to = slice((c * inner + w) * share, (c * inner + w + 1) * share)
-                g_tile[to] = grad_ref[c, index_ref[1] ^ (first + w)][:, : g_tile.shape[1]]
-
-    @pl.when(step < tiles // 2)
-    def _():
-        load(row_near, grad_near)
-
-    @pl.when(step >= tiles // 2)
-    def _():
-        load(row_far, grad_far)
-
-    x = x_tile[:, :width]
+    earlier = lax.broadcasted_iota(jnp.int32, (rows, rows), 0) < lax.broadcasted_iota(jnp.int32, (rows, rows), 1)
+    for one in x_in:
+        one.wait()
+    for one in x_out:
+        one.start()
+    mask = x_tile[:, width:]
+    mine = lax.broadcasted_iota(jnp.int32, (8, mask.shape[1]), 1) == expert
+    routed = dot(jnp.where(mine, 1.0, 0.0).astype(low), mask, 1, 1)
+    place = dot(routed.astype(low), jnp.where(earlier, 1.0, 0.0).astype(low))
+    slot = lax.broadcasted_iota(jnp.int32, (slots, rows), 0).astype(full)
+    draw = jnp.where(jnp.where(routed[:1] > 0.5, place[:1], -1.0) == slot, 1.0, 0.0).astype(low)
+    drawn = dot(draw, x_tile[...]).astype(low)
+    x = drawn[:, :width]
     x_ref[...] = x
-    g = g_tile[...].astype(full)
-    chosen = x_tile[:, width:][:, :experts].astype(full) > 0.5
+    chosen = drawn[:, width:][:, :experts].astype(full) > 0.5
     logits = jnp.where(chosen, dot(x, router_ref[...], 1, 1), -1e30)
     shifted = jnp.exp(logits - jnp.max(logits, axis=-1, keepdims=True))
     shifted = jnp.where(chosen, shifted, 0.0)
-    mine = lax.broadcasted_iota(jnp.int32, shifted.shape, 1) == expert
-    own = jnp.sum(jnp.where(mine, shifted, 0.0), axis=-1, keepdims=True) / jnp.sum(
-        shifted, axis=-1, keepdims=True
-    )
+    own_lane = lax.broadcasted_iota(jnp.int32, shifted.shape, 1) == expert
+    total = jnp.sum(shifted, axis=-1, keepdims=True)
+    own = jnp.sum(jnp.where(own_lane, shifted, 0.0), axis=-1, keepdims=True) / jnp.where(total > 0.0, total, 1.0)
+    for one in g_in:
+        one.wait()
+    g = dot(draw, g_tile[...])
     deo = (g * own).astype(low)
     deo_ref[...] = deo
 
@@ -247,53 +268,38 @@
     high = dlw.astype(low)
     rest = (dlw - high.astype(full)).astype(low).astype(full)
     cols = near_ref.shape[1] - (2 if merged else 1) * width
-    lane = lax.broadcasted_iota(jnp.int32, (x.shape[0], cols), 1)
+    lane = lax.broadcasted_iota(jnp.int32, (slots, cols), 1)
     extra = jnp.where(lane == expert, high.astype(full), 0.0)
     extra = jnp.where(lane == experts + expert, rest, extra).astype(low)
-
-    def store(row_ref, moe_ref):
-        row_ref[:, :width] = back
-        row_ref[:, width : width + cols] = extra
-        moe_ref[:, moe_ref.shape[1] - width :] = moe
-
-    @pl.when(step < tiles // 2)
-    def _():
-        store(near_ref, moe_near_ref)
-
-    @pl.when(step >= tiles // 2)
-    def _():
-        store(far_ref, moe_far_ref)
-
-
-def run_expert(part, part_count, inner, merged, rows, grads, router, w_gate_up, w_down, index, into, cols):
+    for i, (ref, moe_ref) in enumerate(((near_ref, moe_near_ref), (far_ref, moe_far_ref))):
+        lay = draw[:, i * tile : (i + 1) * tile]
+        ref[:, :width] = dot(lay, back, 0, 0).astype(low)
+        ref[:, width : width + cols] = dot(lay, extra, 0, 0).astype(low)
+        moe_ref[:, moe_ref.shape[1] - width :] = dot(lay, moe, 0, 0).astype(low)
+    for one in x_out:
+        one.wait()
+
+
+def run_expert(part, part_count, inner, merged, rows, grads, router, w_gate_up, w_down, index, into, cols, most):
     chips, wt_count, share, width = grads[0].shape
     half_rows = chips * inner * share
     tile = min(256, half_rows)
-    near = half_rows // tile
-    tiles = 2 * near
-    each = chips // near
+    steps = half_rows // tile
+    slots = -(-2 * tile // share * most // 16) * 16
     ffw = w_down.shape[1]
     wide = rows[0].shape[-1]
-    everything = 2 * half_rows * part_count
-    offset = part * tiles
-    near_map = lambda i: (jnp.minimum(i, near - 1), 0)
-    far_map = lambda i: (jnp.maximum(i - near, 0), 0)
-    all_map = lambda i: (i + offset, 0)
     widths = [cols + width] if merged else [cols, width]
     outs, out_specs = [], []
     for one in widths:
         outs += [shape_of((half_rows, one), low)] * 2
-        out_specs += [pl.BlockSpec((tile, one), near_map), pl.BlockSpec((tile, one), far_map)]
+        out_specs += [pl.BlockSpec((tile, one), lambda i: (i, 0))] * 2
     lead_outs = len(outs)
+    outs.append(shape_of((2 * half_rows * part_count, width), low))
+    out_specs.append(in_any)
     for one in (width, ffw, 2 * ffw, width):
-        outs.append(shape_of((everything, one), low))
-        out_specs.append(pl.BlockSpec((tile, one), all_map))
-    ins = [in_smem]
-    for where in (near_map, far_map):
-        ins.append(pl.BlockSpec((tile, wide), where))
-    for where, grad in ((near_map, grads[0]), (far_map, grads[1])):
-        ins.append(pl.BlockSpec((each, *grad.shape[1:]), lambda i, where=where: (where(i)[0], 0, 0, 0)))
-    ins += [pl.BlockSpec(router.shape, lambda i: (0, 0)), in_any, in_any]
+        outs.append(shape_of((part_count * steps * slots, one), low))
+        out_specs.append(pl.BlockSpec((slots, one), lambda i: (i + part * steps, 0)))
+    ins = [in_smem] + [in_any] * 4 + [pl.BlockSpec(router.shape, lambda i: (0, 0)), in_any, in_any]
     args = [index, *rows, *grads, router, w_gate_up, w_down]
     lead = len(args)
     aliases = {}
@@ -304,21 +310,21 @@
             args.append(array)
 
     def body(*refs):
-        expert_kernel(tiles, part * inner, inner, merged, *refs[:lead], *refs[len(args) :])
+        expert_kernel(part, inner, merged, *refs[:lead], *refs[len(args) :])
 
     results = kernel_call(
         body,
         outs,
         ins,
         args,
-        grid=(tiles,),
+        grid=(steps,),
         out_specs=out_specs,
         scratch_shapes=[
-            pltpu.VMEM((tile, wide), low),
-            pltpu.VMEM((tile, width), low),
+            pltpu.VMEM((2 * tile, wide), low),
+            pltpu.VMEM((2 * tile, width), low),
             pltpu.VMEM(w_gate_up.shape[1:], low),
             pltpu.VMEM(w_down.shape[1:], low),
-            pltpu.SemaphoreType.DMA((2,)),
+            pltpu.SemaphoreType.DMA((6 + 2 * tile // share,)),
         ],
         input_output_aliases=aliases,
     )
@@ -808,8 +814,10 @@
     near_second = near_ctx(second)
     places = jnp.stack([my_expert, wt_index])
     sums_cols = width + extra_cols
+    most = max(2, share * top_count * 5 // (4 * experts) + 1)
     results, into = run_expert(
         0, parts, inner, True, rows_first, grads, router, w_gate_up, w_down, places, None, sums_cols,
+        most,
     )
     results, into, near_second = fence(results, into, near_second)
     rows_second, attn_near = kernel_call(
@@ -840,15 +848,16 @@
     back_received = [plane_swap(back_blocks[0])]
     results, into = run_expert(
         1, parts, inner, False, rows_second, grads, router, w_gate_up, w_down, places, into, sums_cols,
+        most,
     )
 
     results, into, back_received = fence(results, into, back_received)
     back_blocks.append(split_parts(results[0], swap(results[1], "ctx", 1)))
     back_blocks, moe_far, into = fence(back_blocks, results[3], into)
-    rows_all, hidden, gate_up_grad, expert_grad = into
+    rows_all, rows_drawn, hidden, gate_up_grad, expert_grad = into
     back_received.append(plane_swap(back_blocks[1]))
     moe_far = swap(moe_far, "ctx", 1)
-    w_gate_up_grad = dot(rows_all, gate_up_grad, 0, 0)
+    w_gate_up_grad = dot(rows_drawn, gate_up_grad, 0, 0)
     w_down_grad = dot(hidden, expert_grad, 0, 0)
     back_received, moe_far, w_gate_up_grad, w_down_grad, attn_rows = fence(
         back_received, moe_far, w_gate_up_grad, w_down_grad, attn_rows

time: 318 us -> 315 us (level)
  waiting for transfers between devices: 68.1 us -> 84.8 us
  Pallas kernels: 112 us -> 97.5 us
  matrix products: 22.9 us -> 16.9 us
    ppermute x62, waiting for transfers between devices: 68.1 us -> 84.8 us  [swap(): return lax.ppermute(array, axis, [(i, i ^ mask) for i in range(count)])]
    pallas_call x21, Pallas kernels: 112 us -> 97.5 us  [kernel_call(): pl.pallas_call(body, out_shape=outs + [shape_of(one.shape, one.dtype) for...]
    dot_general x5, matrix products: 22.9 us -> 16.9 us  [dot(): lax.dot_general(a, b, (((a_dim,), (b_dim,)), ((), ())), preferred_element...]
    unnamed x117 -> x135, local copies, waits for them, and re-layouts: 13 us -> 13.6 us
  transfers between devices with their start and end apart: 62 -> 62, of which waited for: 22 -> 24; matrix products, arithmetic and copies ran while one was open for 11% -> 8% of each run, Pallas kernels for 30% -> 25%
where the time goes in v1:
time: 315 us; the launch traced here: 312 us
  Pallas kernels  97.5 us (31%)
  waiting for transfers between devices  84.8 us (27%)
  starting transfers between devices  77 us (24%)
  local copies, waits for them, and re-layouts  18.8 us (6%)
  matrix products  16.9 us (5%)
  other arithmetic  15.1 us (5%)
    pallas_call x21, Pallas kernels, kernel_call(): pl.pallas_call(body, out_shape=outs + [shape_of(one.shape, one.dtype) for...  97.5 us
    ppermute x62, waiting for transfers between devices, swap(): return lax.ppermute(array, axis, [(i, i ^ mask) for i in range(count)])  84.8 us
    ppermute x62, starting transfers between devices, swap(): return lax.ppermute(array, axis, [(i, i ^ mask) for i in range(count)])  77 us
    dot_general x5, matrix products, dot(): lax.dot_general(a, b, (((a_dim,), (b_dim,)), ((), ())), preferred_element...  16.9 us
    unnamed x135, local copies, waits for them, and re-layouts  13.6 us
  transfers between devices with their start and end apart: 62, of which 24 were waited for; matrix products, arithmetic and copies ran while one was open for 8% of the time, Pallas kernels for 25%

profile of v1, /device:TPU:0, one launch (start us, length us, event | category | flops | bytes accessed | tf_op | source)
XLA Modules:
  0.0 311.5 jit_solution(4951546069531040379)
XLA Ops:
  3.0 3.0 shard_map.237
  6.0 3.0 collective-permute-start
  14.9 3.0 collective-permute-start.16
  17.9 3.2 %collective-permute-done.1.refs_3_ = bf16[128,768]{1,0:T(8,128)(2,1)S(1)} collective-permute-done((bf16[128,768]{1,0:T(8,128)(2,1)}, bf16[128,768]{1,0:T(8,128)(2,1)S(1)}, u32[]{:S(2)}, u32[]{:S(2)}) %collective-permute-start.1) | collective-permute-done | bytes 196640 | tf_op jit(solution)/shard_map/ppermute | solution.py:27
  25.0 4.9 %shard_map.238 = (f32[128,1024]{1,0:T(8,128)}, bf16[1024,128]{1,0:T(8,128)(2,1)}) custom-call(bf16[128,2048]{1,0:T(8,128)(2,1)} %get-tuple-element.207.refs_0_, bf16[2048,1024]{1,0:T(8,128)(2,1)} %refs_1_.2, f32[1,128]{1,0:T(1,128)} %bitcast.60, f32[128,128]{1,0:T(8,128)} %pad_maximum_fusion.refs_6_.refs_3_.refs_8_, ...), custom_call_target="tpu_custom_call" | custom-call | tf_op jit(solution)/shard_map/pallas_call | solution.py:52
  31.4 7.4 %shard_map.240 = (bf16[128,1024]{1,0:T(8,128)(2,1)}, bf16[1024,1024]{1,0:T(8,128)(2,1)}, bf16[1024,128]{1,0:T(8,128)(2,1)}, bf16[1024,128]{1,0:T(8,128)(2,1)}, f...) custom-call(s32[256,1]{1,0:T(8,128)} %copy.40.refs_0_, ...), custom_call_target="tpu_custom_call" | custom-call | tf_op jit(solution)/shard_map/pallas_call | solution.py:52
  43.0 4.6 %collective-permute-done.4.refs_4_ = bf16[32,2048]{1,0:T(8,128)(2,1)S(1)} collective-permute-done((bf16[32,2048]{1,0:T(8,128)(2,1)}, bf16[32,2048]{1,0:T(8,128)(2,1)S(1)}, u32[]{:S(2)}, u32[]{:S(2)}) %collective-permute-start.4) | collective-permute-done | bytes 131104 | tf_op jit(solution)/shard_map/ppermute | solution.py:27
  51.0 3.7 %collective-permute-done.6.refs_6_ = bf16[32,2048]{1,0:T(8,128)(2,1)S(1)} collective-permute-done((bf16[32,2048]{1,0:T(8,128)(2,1)}, bf16[32,2048]{1,0:T(8,128)(2,1)S(1)}, u32[]{:S(2)}, u32[]{:S(2)}) %collective-permute-start.6) | collective-permute-done | bytes 131104 | tf_op jit(solution)/shard_map/ppermute | solution.py:27
  58.6 3.0 shard_map.244
  64.8 5.7 %collective-permute-done.7.refs_1_ = bf16[32,2176]{1,0:T(8,128)(2,1)S(1)} collective-permute-done((bf16[32,2176]{1,0:T(8,128)(2,1)S(1)}, bf16[32,2176]{1,0:T(8,128)(2,1)S(1)}, u32[]{:S(2)}, u32[]{:S(2)}) %collective-permute-start.7) | collective-permute-done | bytes 139296 | tf_op jit(solution)/shard_map/ppermute | solution.py:27
  78.0 5.4 %collective-permute-done.12.refs_5_.refs_2_ = bf16[32,2176]{1,0:T(8,128)(2,1)S(1)} collective-permute-done((bf16[32,2176]{1,0:T(8,128)(2,1)S(1)}, bf16[32,2176]{1,0:T(8,128)(2,1)S(1)}, u32[]{:S(2)}, u32[]{:S(2)}) %collective-permute-start.12) | collective-permute-done | bytes 139296 | tf_op jit(solution)/shard_map/ppermute | solution.py:27
  83.4 3.0 collective-permute-done.9.refs_2_
  98.7 14.7 %shard_map.245 = (bf16[256,4224]{1,0:T(8,128)(2,1)}, bf16[256,4224]{1,0:T(8,128)(2,1)}, bf16[1024,2048]{1,0:T(8,128)(2,1)}, bf16[352,2048]{1,0:T(8,128)(2,1)}, b...) custom-call(s32[2]{0:T(128)} %pad_add_fusion.1.refs_0_, ...), custom_call_target="tpu_custom_call" | custom-call | tf_op jit(solution)/shard_map/pallas_call | solution.py:52
  113.4 7.2 %collective-permute-done.19.refs_2_ = bf16[64,4224]{1,0:T(8,128)(2,1)} collective-permute-done((bf16[64,4224]{1,0:T(8,128)(2,1)}, bf16[64,4224]{1,0:T(8,128)(2,1)}, u32[]{:S(2)}, u32[]{:S(2)}) %collective-permute-start.19) | collective-permute-done | bytes 540704 | tf_op jit(solution)/shard_map/ppermute | solution.py:27
  120.7 3.0 shard_map.247
  132.1 14.9 %shard_map.248 = (bf16[256,2176]{1,0:T(8,128)(2,1)}, bf16[256,2176]{1,0:T(8,128)(2,1)}, bf16[256,2048]{1,0:T(8,128)(2,1)}, bf16[256,2048]{1,0:T(8,128)(2,1)}, bf...) custom-call(s32[2]{0:T(128)} %pad_add_fusion.1.refs_0_, ...), custom_call_target="tpu_custom_call", output_to_operand_aliasing={{4}: (8, {}), {5}: (9, {}), {6}: (10, {}), {7}: (11, {}), {... | custom-call | tf_op jit(solution)/shard_map/pallas_call | solution.py:52
  147.0 7.1 %collective-permute-done.24 = bf16[64,4224]{1,0:T(8,128)(2,1)S(1)} collective-permute-done((bf16[64,4224]{1,0:T(8,128)(2,1)}, bf16[64,4224]{1,0:T(8,128)(2,1)S(1)}, u32[]{:S(2)}, u32[]{:S(2)}) %collective-permute-start.24) | collective-permute-done | bytes 540704 | tf_op jit(solution)/shard_map/ppermute | solution.py:27
  155.7 3.0 collective-permute-done.26
  165.5 6.6 %fusion.30 = f32[2048,1536]{1,0:T(8,128)} fusion(bf16[352,2048]{1,0:T(8,128)(2,1)S(1)} %copy-done.1, bf16[352,1536]{1,0:T(8,128)(2,1)S(1)} %copy-done.3), kind=kOutput, calls=%fused_computation.76 | convolution fusion | flops 2214592512 | bytes 15106048 | tf_op jit(solution)/shard_map/dot_general | solution.py:22
  172.1 4.5 %fusion.31 = f32[768,2048]{1,0:T(8,128)} fusion(bf16[352,768]{1,0:T(8,128)(2,1)S(1)} %copy-done.6, bf16[352,2048]{1,0:T(8,128)(2,1)S(1)} %copy-done.2), kind=kOutput, calls=%fused_computation.77 | convolution fusion | flops 1107296256 | bytes 8273920 | tf_op jit(solution)/shard_map/dot_general | solution.py:22
  187.6 6.4 %collective-permute-done.32 = bf16[32,2176]{1,0:T(8,128)(2,1)S(1)} collective-permute-done((bf16[32,2176]{1,0:T(8,128)(2,1)S(1)}, bf16[32,2176]{1,0:T(8,128)(2,1)S(1)}, u32[]{:S(2)}, u32[]{:S(2)}) %collective-permute-start.32) | collective-permute-done | bytes 139296 | tf_op jit(solution)/shard_map/ppermute | solution.py:27
  205.3 7.9 %collective-permute-done.35.refs_12_ = bf16[32,2176]{1,0:T(8,128)(2,1)S(1)} collective-permute-done((bf16[32,2176]{1,0:T(8,128)(2,1)S(1)}, bf16[32,2176]{1,0:T(8,128)(2,1)S(1)}, u32[]{:S(2)}, u32[]{:S(2)}) %collective-permute-start.35) | collective-permute-done | bytes 139296 | tf_op jit(solution)/shard_map/ppermute | solution.py:27
  214.3 3.2 %collective-permute-start.40 = (bf16[32,2048]{1,0:T(8,128)(2,1)S(1)}, bf16[32,2048]{1,0:T(8,128)(2,1)S(1)}, u32[]{:S(2)}, u32[]{:S(2)}) collective-permute-start(bf16[32,2048]{1,0:T(8,128)(2,1)S(1)} %slice.236), channel_id=1, source_target_pairs={{0,1},{1,0},{2,3},{3,2},{4,5},{5,4},{6,7},{7,6},{8,9},{9,8},{10,11... | collective-permute-start | bytes 393224 | tf_op jit(solution)/shard_map/ppermute | solution.py:27
  220.0 11.0 %shard_map.249 = (bf16[512,256]{1,0:T(8,128)(2,1)}, bf16[512,256]{1,0:T(8,128)(2,1)}, bf16[128,1024]{1,0:T(8,128)(2,1)}, f32[1,128]{1,0:T(1,128)}, bf16[128,640]...) custom-call(s32[1]{0:T(128)} %bitcast.1.refs_0_, ...), custom_call_target="tpu_custom_call" | custom-call | tf_op jit(solution)/shard_map/pallas_call | solution.py:52
  238.2 4.7 %fusion.32.refs_2_ = f32[128,2048]{1,0:T(8,128)} fusion(bf16[128,1024]{1,0:T(8,128)(2,1)S(1)} %copy-done.26, bf16[2048,1024]{1,0:T(8,128)(2,1)} %refs_1_.2), kind=kOutput, calls=%fused_computation.78 | convolution fusion | flops 536870912 | bytes 5505024 | tf_op jit(solution)/shard_map/dot_general | solution.py:22
  243.9 3.5 %shard_map.250 = (f32[32,2048]{1,0:T(8,128)}, bf16[32,2432]{1,0:T(8,128)(2,1)}, bf16[32,2432]{1,0:T(8,128)(2,1)}, bf16[32,2432]{1,0:T(8,128)(2,1)}, bf16[128,128...) custom-call(f32[1,2048]{1,0:T(1,128)} %bitcast.58, ...), custom_call_target="tpu_custom_call", output_to_operand_aliasing={{6}: (17, {}), {7}: (18, {}), {8}: (19, {}), {9}: (20, {})} | custom-call | tf_op jit(solution)/shard_map/pallas_call | solution.py:52
  261.0 4.5 %collective-permute-done.49.refs_10_ = bf16[32,2432]{1,0:T(8,128)(2,1)S(1)} collective-permute-done((bf16[32,2432]{1,0:T(8,128)(2,1)}, bf16[32,2432]{1,0:T(8,128)(2,1)S(1)}, u32[]{:S(2)}, u32[]{:S(2)}) %collective-permute-start.49) | collective-permute-done | bytes 155680 | tf_op jit(solution)/shard_map/ppermute | solution.py:27
  281.4 3.5 %shard_map.254.refs_7_.refs_6_ = f32[1024,256]{1,0:T(8,128)} custom-call(bf16[512,1024]{1,0:T(8,128)(2,1)} %get-tuple-element.364.refs_0_, bf16[512,1024]{1,0:T(8,128)(2,1)} %copy-done.4, bf16[512,256]{1,0:T(8,128)(2,1)} %get-tuple-element.383.refs_2_, bf16[512,384]{1,0:T(8,128)(2,1)} %copy-done.9, bf16[32,4096]{1,0:T(8,128)(2,1)} %get-tuple-element.379.refs_4_.refs_1_), custom_call_target="tpu_custom_call" | custom-call | tf_op jit(solution)/shard_map/pallas_call | solution.py:52
  284.8 5.0 %shard_map.253.refs_8_.refs_5_ = f32[32,2048]{1,0:T(8,128)} custom-call(s32[2]{0:T(128)} %pad_add_fusion.2.refs_0_, bf16[2,8,2,32,2048]{4,3,2,1,0:T(8,128)(2,1)} %bitcast.42, bf16[512,128]{1,0:T(8,128)(2,1)} %get-tuple-element.381.refs_2_, bf16[512,384]{1,0:T(8,128)(2,1)} %copy-done.9), custom_call_target="tpu_custom_call" | custom-call | tf_op jit(solution)/shard_map/pallas_call | solution.py:52
  289.9 6.5 %collective-permute-done.55.refs_5_.refs_3_ = bf16[32,4096]{1,0:T(8,128)(2,1)S(1)} collective-permute-done((bf16[32,4096]{1,0:T(8,128)(2,1)}, bf16[32,4096]{1,0:T(8,128)(2,1)S(1)}, u32[]{:S(2)}, u32[]{:S(2)}) %collective-permute-start.55) | collective-permute-done | bytes 262176 | tf_op jit(solution)/shard_map/ppermute | solution.py:27
  300.7 3.5 %collective-permute-done.61.refs_4_ = bf16[576,1280]{1,0:T(8,128)(2,1)S(1)} collective-permute-done((bf16[576,1280]{1,0:T(8,128)(2,1)}, bf16[576,1280]{1,0:T(8,128)(2,1)S(1)}, u32[]{:S(2)}, u32[]{:S(2)}) %collective-permute-start.61) | collective-permute-done | bytes 1474592 | tf_op jit(solution)/shard_map/ppermute | solution.py:27
  305.3 4.0 %shard_map.256 = (f32[256,1024]{1,0:T(8,128)}, f32[256,128]{1,0:T(8,128)}, f32[256,128]{1,0:T(8,128)}, f32[16,128]{1,0:T(8,128)}, f32[16,128]{1,0:T(8,128)}, /*index=5*/f32[1,128]{1,0:T(1,128)}, f32[1,128]{1,0:T(1,128)}) custom-call(s32[1]{0:T(128)} %bitcast.17.refs_0_, bf16[512,256]{1,0:T(8,128)(2,1)} %get-tuple-element.384.refs_1_, ...), custom_call_target="tpu_custom_call" | custom-call | tf_op jit(solution)/shard_map/pallas_call | solution.py:52
  (302 shorter events, 135.4 us)
Async XLA Ops:
  8.9 12.2 %collective-permute-start.1 = (bf16[128,768]{1,0:T(8,128)(2,1)}, bf16[128,768]{1,0:T(8,128)(2,1)S(1)}, u32[]{:S(2)}, u32[]{:S(2)}) collective-permute-start(bf16[128,768]{1,0:T(8,128)(2,1)} %get-tuple-element.211), channel_id=1, source_target_pairs={{0,16},{4,20},{8,24},{12,28},{16,0},{20,4},{24,8},{28,12},{1,17},{... | collective-permute-start | bytes 589832 | tf_op jit(solution)/shard_map/ppermute | solution.py:27
  10.5 46.9 %collective-permute-start.14 = (bf16[128,2048]{1,0:T(8,128)(2,1)S(1)}, bf16[128,2048]{1,0:T(8,128)(2,1)S(1)}, u32[]{:S(2)}, u32[]{:S(2)}) collective-permute-start(bf16[128,2048]{1,0:T(8,128)(2,1)S(1)} %bitcast.51), channel_id=1, source_target_pairs={{0,8},{4,12},{8,0},{12,4},{16,24},{20,28},{24,16},{28,20},{1,9},{5... | collective-permute-start | bytes 1572872 | tf_op jit(solution)/shard_map/ppermute | solution.py:27
  12.4 45.0 %collective-permute-start.15 = (bf16[128,2048]{1,0:T(8,128)(2,1)S(1)}, bf16[128,2048]{1,0:T(8,128)(2,1)S(1)}, u32[]{:S(2)}, u32[]{:S(2)}) collective-permute-start(bf16[128,2048]{1,0:T(8,128)(2,1)S(1)} %bitcast.52), channel_id=1, source_target_pairs={{0,16},{4,20},{8,24},{12,28},{16,0},{20,4},{24,8},{28,12},{1,17},{... | collective-permute-start | bytes 1572872 | tf_op jit(solution)/shard_map/ppermute | solution.py:27
  14.9 42.5 %collective-permute-start.16 = (bf16[128,2048]{1,0:T(8,128)(2,1)S(1)}, bf16[128,2048]{1,0:T(8,128)(2,1)S(1)}, u32[]{:S(2)}, u32[]{:S(2)}) collective-permute-start(bf16[128,2048]{1,0:T(8,128)(2,1)S(1)} %bitcast.53), channel_id=1, source_target_pairs={{0,24},{4,28},{8,16},{12,20},{16,8},{20,12},{24,0},{28,4},{1,25},{... | collective-permute-start | bytes 1572872 | tf_op jit(solution)/shard_map/ppermute | solution.py:27
  61.6 35.4 %collective-permute-start.17 = (bf16[512,2048]{1,0:T(8,128)(2,1)}, bf16[512,2048]{1,0:T(8,128)(2,1)S(1)}, u32[]{:S(2)}, u32[]{:S(2)}) collective-permute-start(bf16[512,2048]{1,0:T(8,128)(2,1)} %shard_map.244), channel_id=1, source_target_pairs={{0,4},{4,0},{8,12},{12,8},{16,20},{20,16},{24,28},{28,24},{1,5},{5... | collective-permute-start | bytes 6291464 | tf_op jit(solution)/shard_map/ppermute | solution.py:27
  63.1 13.2 %collective-permute-start.11 = (bf16[32,2176]{1,0:T(8,128)(2,1)S(1)}, bf16[32,2176]{1,0:T(8,128)(2,1)S(1)}, u32[]{:S(2)}, u32[]{:S(2)}) collective-permute-start(bf16[32,2176]{1,0:T(8,128)(2,1)S(1)} %copy-done.31), channel_id=1, source_target_pairs={{0,2},{1,3},{2,0},{3,1},{4,6},{5,7},{6,4},{7,5},{8,10},{9,11},{10,... | collective-permute-start | bytes 417800 | tf_op jit(solution)/shard_map/ppermute | solution.py:27
  73.8 12.6 %collective-permute-start.9 = (bf16[64,2176]{1,0:T(8,128)(2,1)}, bf16[64,2176]{1,0:T(8,128)(2,1)S(1)}, u32[]{:S(2)}, u32[]{:S(2)}) collective-permute-start(bf16[64,2176]{1,0:T(8,128)(2,1)} %shard_map.242.refs_0_), channel_id=1, source_target_pairs={{0,16},{4,20},{8,24},{12,28},{16,0},{20,4},{24,8},{28,12},{1,17},{... | collective-permute-start | bytes 835592 | tf_op jit(solution)/shard_map/ppermute | solution.py:27
  75.0 13.0 %collective-permute-start.10 = (bf16[64,2176]{1,0:T(8,128)(2,1)}, bf16[64,2176]{1,0:T(8,128)(2,1)S(1)}, u32[]{:S(2)}, u32[]{:S(2)}) collective-permute-start(bf16[64,2176]{1,0:T(8,128)(2,1)} %shard_map.242.refs_0_), channel_id=1, source_target_pairs={{0,24},{4,28},{8,16},{12,20},{16,8},{20,12},{24,0},{28,4},{1,25},{... | collective-permute-start | bytes 835592 | tf_op jit(solution)/shard_map/ppermute | solution.py:27
  92.9 20.5 %collective-permute-start.18 = (bf16[64,4224]{1,0:T(8,128)(2,1)}, bf16[64,4224]{1,0:T(8,128)(2,1)}, u32[]{:S(2)}, u32[]{:S(2)}) collective-permute-start(bf16[64,4224]{1,0:T(8,128)(2,1)} %shard_map.246.refs_0_), channel_id=1, source_target_pairs={{0,8},{4,12},{8,0},{12,4},{16,24},{20,28},{24,16},{28,20},{1,9},{5... | collective-permute-start | bytes 1622024 | tf_op jit(solution)/shard_map/ppermute | solution.py:27
  94.4 26.3 %collective-permute-start.19 = (bf16[64,4224]{1,0:T(8,128)(2,1)}, bf16[64,4224]{1,0:T(8,128)(2,1)}, u32[]{:S(2)}, u32[]{:S(2)}) collective-permute-start(bf16[64,4224]{1,0:T(8,128)(2,1)} %shard_map.246.refs_0_), channel_id=1, source_target_pairs={{0,16},{4,20},{8,24},{12,28},{16,0},{20,4},{24,8},{28,12},{1,17},{... | collective-permute-start | bytes 1622024 | tf_op jit(solution)/shard_map/ppermute | solution.py:27
  95.9 24.8 %collective-permute-start.20 = (bf16[64,4224]{1,0:T(8,128)(2,1)}, bf16[64,4224]{1,0:T(8,128)(2,1)}, u32[]{:S(2)}, u32[]{:S(2)}) collective-permute-start(bf16[64,4224]{1,0:T(8,128)(2,1)} %shard_map.246.refs_0_), channel_id=1, source_target_pairs={{0,24},{4,28},{8,16},{12,20},{16,8},{20,12},{24,0},{28,4},{1,25},{... | collective-permute-start | bytes 1622024 | tf_op jit(solution)/shard_map/ppermute | solution.py:27
  128.6 18.4 %collective-permute-start.23 = (bf16[64,4224]{1,0:T(8,128)(2,1)}, bf16[64,4224]{1,0:T(8,128)(2,1)S(1)}, u32[]{:S(2)}, u32[]{:S(2)}) collective-permute-start(bf16[64,4224]{1,0:T(8,128)(2,1)} %get-tuple-element.247), channel_id=1, source_target_pairs={{0,8},{4,12},{8,0},{12,4},{16,24},{20,28},{24,16},{28,20},{1,9},{5... | collective-permute-start | bytes 1622024 | tf_op jit(solution)/shard_map/ppermute | solution.py:27
  129.9 24.3 %collective-permute-start.24 = (bf16[64,4224]{1,0:T(8,128)(2,1)}, bf16[64,4224]{1,0:T(8,128)(2,1)S(1)}, u32[]{:S(2)}, u32[]{:S(2)}) collective-permute-start(bf16[64,4224]{1,0:T(8,128)(2,1)} %get-tuple-element.248), channel_id=1, source_target_pairs={{0,16},{4,20},{8,24},{12,28},{16,0},{20,4},{24,8},{28,12},{1,17},{... | collective-permute-start | bytes 1622024 | tf_op jit(solution)/shard_map/ppermute | solution.py:27
  130.7 25.0 %collective-permute-start.25 = (bf16[64,4224]{1,0:T(8,128)(2,1)}, bf16[64,4224]{1,0:T(8,128)(2,1)S(1)}, u32[]{:S(2)}, u32[]{:S(2)}) collective-permute-start(bf16[64,4224]{1,0:T(8,128)(2,1)} %get-tuple-element.249), channel_id=1, source_target_pairs={{0,24},{4,28},{8,16},{12,20},{16,8},{20,12},{24,0},{28,4},{1,25},{... | collective-permute-start | bytes 1622024 | tf_op jit(solution)/shard_map/ppermute | solution.py:27
  161.1 15.8 %collective-permute-start.30 = (bf16[256,2048]{1,0:T(8,128)(2,1)}, bf16[256,2048]{1,0:T(8,128)(2,1)}, u32[]{:S(2)}, u32[]{:S(2)}) collective-permute-start(bf16[256,2048]{1,0:T(8,128)(2,1)} %get-tuple-element.281), channel_id=1, source_target_pairs={{0,4},{4,0},{8,12},{12,8},{16,20},{20,16},{24,28},{28,24},{1,5},{5... | collective-permute-start | bytes 3145736 | tf_op jit(solution)/shard_map/ppermute | solution.py:27
  161.3 15.4 %collective-permute-start.27 = (bf16[64,2176]{1,0:T(8,128)(2,1)}, bf16[64,2176]{1,0:T(8,128)(2,1)S(1)}, u32[]{:S(2)}, u32[]{:S(2)}) collective-permute-start(bf16[64,2176]{1,0:T(8,128)(2,1)} %get-tuple-element.278), channel_id=1, source_target_pairs={{0,8},{4,12},{8,0},{12,4},{16,24},{20,28},{24,16},{28,20},{1,9},{5... | collective-permute-start | bytes 835592 | tf_op jit(solution)/shard_map/ppermute | solution.py:27
  162.1 14.8 %collective-permute-start.28 = (bf16[64,2176]{1,0:T(8,128)(2,1)}, bf16[64,2176]{1,0:T(8,128)(2,1)S(1)}, u32[]{:S(2)}, u32[]{:S(2)}) collective-permute-start(bf16[64,2176]{1,0:T(8,128)(2,1)} %get-tuple-element.279), channel_id=1, source_target_pairs={{0,16},{4,20},{8,24},{12,28},{16,0},{20,4},{24,8},{28,12},{1,17},{... | collective-permute-start | bytes 835592 | tf_op jit(solution)/shard_map/ppermute | solution.py:27
  163.6 13.3 %collective-permute-start.29 = (bf16[64,2176]{1,0:T(8,128)(2,1)}, bf16[64,2176]{1,0:T(8,128)(2,1)S(1)}, u32[]{:S(2)}, u32[]{:S(2)}) collective-permute-start(bf16[64,2176]{1,0:T(8,128)(2,1)} %get-tuple-element.280), channel_id=1, source_target_pairs={{0,24},{4,28},{8,16},{12,20},{16,8},{20,12},{24,0},{28,4},{1,25},{... | collective-permute-start | bytes 835592 | tf_op jit(solution)/shard_map/ppermute | solution.py:27
  180.8 13.2 %collective-permute-start.32 = (bf16[32,2176]{1,0:T(8,128)(2,1)S(1)}, bf16[32,2176]{1,0:T(8,128)(2,1)S(1)}, u32[]{:S(2)}, u32[]{:S(2)}) collective-permute-start(bf16[32,2176]{1,0:T(8,128)(2,1)S(1)} %get-tuple-element.296), channel_id=1, source_target_pairs={{0,2},{1,3},{2,0},{3,1},{4,6},{5,7},{6,4},{7,5},{8,10},{9,11},{10,... | collective-permute-start | bytes 417800 | tf_op jit(solution)/shard_map/ppermute | solution.py:27
  199.4 13.8 %collective-permute-start.37 = (bf16[64,2048]{1,0:T(8,128)(2,1)S(1)}, bf16[64,2048]{1,0:T(8,128)(2,1)S(1)}, u32[]{:S(2)}, u32[]{:S(2)}) collective-permute-start(bf16[64,2048]{1,0:T(8,128)(2,1)S(1)} %copy-done.46), channel_id=1, source_target_pairs={{0,8},{4,12},{8,0},{12,4},{16,24},{20,28},{24,16},{28,20},{1,9},{5... | collective-permute-start | bytes 786440 | tf_op jit(solution)/shard_map/ppermute | solution.py:27
  200.9 12.4 %collective-permute-start.38 = (bf16[64,2048]{1,0:T(8,128)(2,1)S(1)}, bf16[64,2048]{1,0:T(8,128)(2,1)S(1)}, u32[]{:S(2)}, u32[]{:S(2)}) collective-permute-start(bf16[64,2048]{1,0:T(8,128)(2,1)S(1)} %get-tuple-element.319), channel_id=1, source_target_pairs={{0,16},{4,20},{8,24},{12,28},{16,0},{20,4},{24,8},{28,12},{1,17},{... | collective-permute-start | bytes 786440 | tf_op jit(solution)/shard_map/ppermute | solution.py:27
  214.3 16.7 %collective-permute-start.40 = (bf16[32,2048]{1,0:T(8,128)(2,1)S(1)}, bf16[32,2048]{1,0:T(8,128)(2,1)S(1)}, u32[]{:S(2)}, u32[]{:S(2)}) collective-permute-start(bf16[32,2048]{1,0:T(8,128)(2,1)S(1)} %slice.236), channel_id=1, source_target_pairs={{0,1},{1,0},{2,3},{3,2},{4,5},{5,4},{6,7},{7,6},{8,9},{9,8},{10,11... | collective-permute-start | bytes 393224 | tf_op jit(solution)/shard_map/ppermute | solution.py:27
  217.5 13.5 %collective-permute-start.41 = (bf16[32,2048]{1,0:T(8,128)(2,1)S(1)}, bf16[32,2048]{1,0:T(8,128)(2,1)S(1)}, u32[]{:S(2)}, u32[]{:S(2)}) collective-permute-start(bf16[32,2048]{1,0:T(8,128)(2,1)S(1)} %get-tuple-element.340), channel_id=1, source_target_pairs={{0,2},{1,3},{2,0},{3,1},{4,6},{5,7},{6,4},{7,5},{8,10},{9,11},{10,... | collective-permute-start | bytes 393224 | tf_op jit(solution)/shard_map/ppermute | solution.py:27
  217.9 13.2 %collective-permute-start.42 = (bf16[32,2048]{1,0:T(8,128)(2,1)S(1)}, bf16[32,2048]{1,0:T(8,128)(2,1)S(1)}, u32[]{:S(2)}, u32[]{:S(2)}) collective-permute-start(bf16[32,2048]{1,0:T(8,128)(2,1)S(1)} %get-tuple-element.341), channel_id=1, source_target_pairs={{0,3},{1,2},{2,1},{3,0},{4,7},{5,6},{6,5},{7,4},{8,11},{9,10},{10,... | collective-permute-start | bytes 393224 | tf_op jit(solution)/shard_map/ppermute | solution.py:27
  220.0 22.9 %collective-permute-start.47 = (bf16[512,1024]{1,0:T(8,128)(2,1)S(1)}, bf16[512,1024]{1,0:T(8,128)(2,1)S(1)}, u32[]{:S(2)}, u32[]{:S(2)}) collective-permute-start(bf16[512,1024]{1,0:T(8,128)(2,1)S(1)} %copy-done.25), channel_id=1, source_target_pairs={{0,4},{4,0},{8,12},{12,8},{16,20},{20,16},{24,28},{28,24},{1,5},{5... | collective-permute-start | bytes 3145736 | tf_op jit(solution)/shard_map/ppermute | solution.py:27
  252.0 13.5 %collective-permute-start.49 = (bf16[32,2432]{1,0:T(8,128)(2,1)}, bf16[32,2432]{1,0:T(8,128)(2,1)S(1)}, u32[]{:S(2)}, u32[]{:S(2)}) collective-permute-start(bf16[32,2432]{1,0:T(8,128)(2,1)} %get-tuple-element.373), channel_id=1, source_target_pairs={{0,2},{1,3},{2,0},{3,1},{4,6},{5,7},{6,4},{7,5},{8,10},{9,11},{10,... | collective-permute-start | bytes 466952 | tf_op jit(solution)/shard_map/ppermute | solution.py:27
  260.9 17.6 %collective-permute-start.57 = (bf16[512,384]{1,0:T(8,128)(2,1)}, bf16[512,384]{1,0:T(8,128)(2,1)S(1)}, u32[]{:S(2)}, u32[]{:S(2)}) collective-permute-start(bf16[512,384]{1,0:T(8,128)(2,1)} %get-tuple-element.382), channel_id=1, source_target_pairs={{0,4},{4,0},{8,12},{12,8},{16,20},{20,16},{24,28},{28,24},{1,5},{5... | collective-permute-start | bytes 1179656 | tf_op jit(solution)/shard_map/ppermute | solution.py:27
  271.2 25.2 %collective-permute-start.58 = (bf16[144,1280]{1,0:T(8,128)(2,1)}, bf16[144,1280]{1,0:T(8,128)(2,1)S(1)}, u32[]{:S(2)}, u32[]{:S(2)}) collective-permute-start(bf16[144,1280]{1,0:T(8,128)(2,1)} %get-tuple-element.385.refs_0_), channel_id=1, source_target_pairs={{0,8},{4,12},{8,0},{12,4},{16,24},{20,28},{24,16},{28,20},{1,9},{5... | collective-permute-start | bytes 1105928 | tf_op jit(solution)/shard_map/ppermute | solution.py:27
  272.8 23.6 %collective-permute-start.59 = (bf16[144,1280]{1,0:T(8,128)(2,1)}, bf16[144,1280]{1,0:T(8,128)(2,1)S(1)}, u32[]{:S(2)}, u32[]{:S(2)}) collective-permute-start(bf16[144,1280]{1,0:T(8,128)(2,1)} %get-tuple-element.385.refs_0_), channel_id=1, source_target_pairs={{0,16},{4,20},{8,24},{12,28},{16,0},{20,4},{24,8},{28,12},{1,17},{... | collective-permute-start | bytes 1105928 | tf_op jit(solution)/shard_map/ppermute | solution.py:27
  273.7 22.7 %collective-permute-start.60 = (bf16[144,1280]{1,0:T(8,128)(2,1)}, bf16[144,1280]{1,0:T(8,128)(2,1)S(1)}, u32[]{:S(2)}, u32[]{:S(2)}) collective-permute-start(bf16[144,1280]{1,0:T(8,128)(2,1)} %get-tuple-element.385.refs_0_), channel_id=1, source_target_pairs={{0,24},{4,28},{8,16},{12,20},{16,8},{20,12},{24,0},{28,4},{1,25},{... | collective-permute-start | bytes 1105928 | tf_op jit(solution)/shard_map/ppermute | solution.py:27
  276.7 19.7 %collective-permute-start.55 = (bf16[32,4096]{1,0:T(8,128)(2,1)}, bf16[32,4096]{1,0:T(8,128)(2,1)S(1)}, u32[]{:S(2)}, u32[]{:S(2)}) collective-permute-start(bf16[32,4096]{1,0:T(8,128)(2,1)} %get-tuple-element.379.refs_4_.refs_1_), channel_id=1, source_target_pairs={{0,2},{1,3},{2,0},{3,1},{4,6},{5,7},{6,4},{7,5},{8,10},{9,11},{10,... | collective-permute-start | bytes 786440 | tf_op jit(solution)/shard_map/ppermute | solution.py:27
  278.5 17.9 %collective-permute-start.56 = (bf16[32,4096]{1,0:T(8,128)(2,1)}, bf16[32,4096]{1,0:T(8,128)(2,1)S(1)}, u32[]{:S(2)}, u32[]{:S(2)}) collective-permute-start(bf16[32,4096]{1,0:T(8,128)(2,1)} %get-tuple-element.379.refs_4_.refs_1_), channel_id=1, source_target_pairs={{0,3},{1,2},{2,1},{3,0},{4,7},{5,6},{6,5},{7,4},{8,11},{9,10},{10,... | collective-permute-start | bytes 786440 | tf_op jit(solution)/shard_map/ppermute | solution.py:27
  (100 other events, 614.7 us)

commit v2 on v1

--- a/solution.py
+++ b/solution.py
@@ -168,13 +168,9 @@
 
 
 def expert_kernel(
-    part, inner, merged, index_ref, row_near, row_far, grad_near, grad_far, router_ref, gu_any, down_any, *refs
+    part, inner, index_ref, row_near, row_far, grad_near, grad_far, router_ref, gu_any, down_any, *refs
 ):
-    if merged:
-        near_ref, far_ref, *refs = refs
-        moe_near_ref, moe_far_ref = near_ref, far_ref
-    else:
-        near_ref, far_ref, moe_near_ref, moe_far_ref, *refs = refs
+    near_ref, far_ref, moe_near_ref, moe_far_ref, *refs = refs
     all_any, x_ref, hidden_ref, dgu_ref, deo_ref, x_tile, g_tile, gu, down, sems = refs
     step = pl.program_id(0)
     rows, width = g_tile.shape
@@ -267,7 +263,7 @@
     back = (dot(dgate, gu[:, :ffw], 1, 1) + dot(dup, gu[:, ffw:], 1, 1)).astype(low)
     high = dlw.astype(low)
     rest = (dlw - high.astype(full)).astype(low).astype(full)
-    cols = near_ref.shape[1] - (2 if merged else 1) * width
+    cols = near_ref.shape[1] - width
     lane = lax.broadcasted_iota(jnp.int32, (slots, cols), 1)
     extra = jnp.where(lane == expert, high.astype(full), 0.0)
     extra = jnp.where(lane == experts + expert, rest, extra).astype(low)
@@ -275,12 +271,12 @@
         lay = draw[:, i * tile : (i + 1) * tile]
         ref[:, :width] = dot(lay, back, 0, 0).astype(low)
         ref[:, width : width + cols] = dot(lay, extra, 0, 0).astype(low)
-        moe_ref[:, moe_ref.shape[1] - width :] = dot(lay, moe, 0, 0).astype(low)
+        moe_ref[...] = dot(lay, moe, 0, 0).astype(low)
     for one in x_out:
         one.wait()
 
 
-def run_expert(part, part_count, inner, merged, rows, grads, router, w_gate_up, w_down, index, into, cols, most):
+def run_expert(part, part_count, inner, rows, grads, router, w_gate_up, w_down, index, into, cols, most):
     chips, wt_count, share, width = grads[0].shape
     half_rows = chips * inner * share
     tile = min(256, half_rows)
@@ -288,7 +284,7 @@
     slots = -(-2 * tile // share * most // 16) * 16
     ffw = w_down.shape[1]
     wide = rows[0].shape[-1]
-    widths = [cols + width] if merged else [cols, width]
+    widths = [cols, width]
     outs, out_specs = [], []
     for one in widths:
         outs += [shape_of((half_rows, one), low)] * 2
@@ -310,7 +306,7 @@
             args.append(array)
 
     def body(*refs):
-        expert_kernel(part, inner, merged, *refs[:lead], *refs[len(args) :])
+        expert_kernel(part, inner, *refs[:lead], *refs[len(args) :])
 
     results = kernel_call(
         body,
@@ -352,15 +348,14 @@
             at += rows
 
 
-def last_kernel(index_ref, x_ref, inv_ref, gain_ref, grad_ref, out_rows_ref, proj_ref, gains_ref, own_ref, *refs):
+def last_kernel(index_ref, x_ref, inv_ref, gain_ref, grad_ref, proj_ref, gains_ref, own_ref, *refs):
     *received, last_ref, message_ref, parts, stack = refs
     total = own_ref[...]
     share, width = total.shape
     for one in received:
         total = total + one[:, :width].astype(full)
-    last_ref[:, :width] = out_rows_ref[...]
     grad = grad_ref[...] + norm_back(total, x_ref[0].astype(full), inv_ref[:share], gain_ref[...])
-    last_ref[:, width:] = grad.astype(low)
+    last_ref[...] = grad.astype(low)
     parts[index_ref[0]] = gains_ref[...]
     for i, one in enumerate(received):
         for j in range(gains_ref.shape[0] // share):
@@ -431,6 +426,32 @@
         [core, *pieces],
         **more,
     )
+
+
+def mid_back_kernel(index_ref, sum_ref, rows_ref, mask_ref, router_ref, mid_ref, inv_ref, gain_ref, g_ref, *refs):
+    *received, grad_ref, part_ref, message_ref, cols = refs
+    total = sum_ref[...]
+    for one in received:
+        total = total + one[...].astype(full)
+    width = grad_ref.shape[1]
+    experts = router_ref.shape[0]
+    weight_grads = total[:, width : width + experts] + total[:, width + experts : width + 2 * experts]
+    chosen = mask_ref[:, :experts].astype(full) > 0.5
+    logits = jnp.where(chosen, dot(rows_ref[:, :width], router_ref[...], 1, 1), -1e30)
+    shifted = jnp.where(chosen, jnp.exp(logits - jnp.max(logits, axis=-1, keepdims=True)), 0.0)
+    routes = shifted / jnp.sum(shifted, axis=-1, keepdims=True)
+    logits_grad = routes * (weight_grads - jnp.sum(routes * weight_grads, axis=-1, keepdims=True))
+    high, rest = split_low(logits_grad)
+    cols[...] = jnp.zeros_like(cols)
+    cols[:, :experts] = high.astype(full)
+    cols[:, experts : 2 * experts] = rest.astype(full)
+    grad = total[:, :width] + dot(high, router_ref[...]) + dot(rest, router_ref[...])
+    mid, inverse = mid_ref[...], inv_ref[...]
+    part_ref[...] = jnp.sum(grad * mid * inverse, axis=0, keepdims=True)
+    grad = g_ref[index_ref[0]].astype(full) + norm_back(grad, mid, inverse, gain_ref[...])
+    grad_ref[...] = grad
+    message_ref[:, :width] = grad.astype(low)
+    message_ref[:, width:] = cols[...].astype(low)
 
 
 def attend_back_kernel(scale, pieces, index_ref, w_ref, probs_ref, keys_ref, values_ref, q_ref, raw_ref,
@@ -803,7 +824,6 @@
     first = join([message] + [swap(message, "wt", m) for m in range(1, inner)])
     others = [swap(message, "wt", m) for m in range(inner, wt_count)]
     grads = [one.reshape(half, wt_count, share, width) for one in both(grad_near, message)]
-    rows_first = both(near_ctx(first), others)
     chunks = pair_len // (inner * share)
     second = kernel_call(
         pack_kernel,
@@ -811,12 +831,13 @@
         [in_vmem] * (1 + inner),
         [attn_rows, *others],
     )
+    rows_first = both(near_ctx(first), second)
     near_second = near_ctx(second)
     places = jnp.stack([my_expert, wt_index])
     sums_cols = width + extra_cols
     most = max(2, share * top_count * 5 // (4 * experts) + 1)
     results, into = run_expert(
-        0, parts, inner, True, rows_first, grads, router, w_gate_up, w_down, places, None, sums_cols,
+        0, parts, inner, rows_first, grads, router, w_gate_up, w_down, places, None, sums_cols,
         most,
     )
     results, into, near_second = fence(results, into, near_second)
@@ -844,10 +865,11 @@
         return [one[w * share : (w + 1) * share] for one in sums for w in range(inner)]
 
     back_blocks = [split_parts(results[0], swap(results[1], "ctx", 1))]
+    moe_blocks = [split_parts(results[2], swap(results[3], "ctx", 1))]
     rows_second, back_blocks, into = fence(rows_second, back_blocks, into)
     back_received = [plane_swap(back_blocks[0])]
     results, into = run_expert(
-        1, parts, inner, False, rows_second, grads, router, w_gate_up, w_down, places, into, sums_cols,
+        1, parts, inner, rows_second, grads, router, w_gate_up, w_down, places, into, sums_cols,
         most,
     )
 
@@ -862,37 +884,27 @@
     back_received, moe_far, w_gate_up_grad, w_down_grad, attn_rows = fence(
         back_received, moe_far, w_gate_up_grad, w_down_grad, attn_rows
     )
-    moe_blocks = [[one[:, sums_cols:] for one in back_blocks[0]], split_parts(results[2], moe_far)]
-    moe_received = [[one[:, sums_cols:] for one in back_received[0]]]
-    back_blocks[0] = [one[:, :sums_cols] for one in back_blocks[0]]
-    back_received[0] = [one[:, :sums_cols] for one in back_received[0]]
+    moe_blocks.append(split_parts(results[2], moe_far))
+    moe_received = [plane_swap(moe_blocks[0])]
     sums = wt_parts([plane_sum(b, r) for b, r in zip(back_blocks, back_received)])
     sums_low = [one.astype(low) for one in sums[1:]]
-    sums_low, attn_rows, moe_blocks = fence(sums_low, attn_rows, moe_blocks)
     received = [swap(one, "wt", m + 1) for m, one in enumerate(sums_low)]
-    received, moe_blocks = fence(received, moe_blocks)
-    summed = plane_sum(sums, received)
-    rows_sum = summed[:, :width]
-    weight_grads = (
-        summed[:, width : width + experts] + summed[:, width + experts : width + 2 * experts]
-    )
-    chosen = own_mask[:, :experts] > 0.5
-    logits = jnp.where(chosen, dot(message[:, :width], router, 1, 1), -1e30)
-    shifted = jnp.where(chosen, jnp.exp(logits - jnp.max(logits, axis=-1, keepdims=True)), 0.0)
-    own_routes = shifted / jnp.sum(shifted, axis=-1, keepdims=True)
-    logits_grad = own_routes * (
-        weight_grads - jnp.sum(own_routes * weight_grads, axis=-1, keepdims=True)
-    )
-    logits_cols = jnp.concatenate(split_low(logits_grad), axis=1)
-    router_term = dot(logits_cols, jnp.concatenate([router, router], axis=0), 1, 0)
-    normed_two_grad = rows_sum + router_term
-    moe_gain_part = jnp.sum(normed_two_grad * mid_rows * inverse_two, axis=0)
-    grad_rows = lax.dynamic_slice_in_dim(cotangent[0], wt_index * share, share, 0).astype(full)
-    mid_grad = grad_rows + norm_back(normed_two_grad, mid_rows, inverse_two, moe_gain)
-    logits_cols = jnp.pad(logits_cols, ((0, 0), (0, extra_cols - 2 * experts)))
-    mid_message = jnp.concatenate([mid_grad.astype(low), logits_cols], axis=1)
-
-    mid_message, moe_blocks = fence(mid_message, moe_blocks)
+    mid_grad, moe_gain_part, mid_message = kernel_call(
+        mid_back_kernel,
+        [
+            shape_of((share, width), full),
+            shape_of((1, width), full),
+            shape_of((share, width + extra_cols), low),
+        ],
+        [in_smem] + [in_vmem] * (7 + wt_count),
+        [
+            index, sums[0], message, own_mask, router, mid_rows, inverse_two, moe_gain.reshape(1, -1),
+            cotangent.reshape(wt_count, share, width), *received,
+        ],
+        after=moe_received,
+        scratch_shapes=[pltpu.VMEM((share, extra_cols), full)],
+    )
+
     mid_pieces = gather_wt(mid_message)
     moe_received.append(plane_swap(moe_blocks[1]))
     mid_pieces, moe_received = fence(mid_pieces, moe_received)
@@ -948,6 +960,7 @@
     out_rows = (mid_rows + plane_sum(moe_sums, moe_received)).astype(low)
     kv_near, query_grad, out_rows = fence(kv_near, query_grad, out_rows)
     kv_received = plane_swap(kv_near)
+    out_pieces = gather_wt(out_rows)
     query_term = dot(query_grad, w_query, 1, 1)
     kv_received, query_term = fence(kv_received, query_term)
     gain_rows = 2 * width // 128 + 2 * head_dim // 128
@@ -966,7 +979,7 @@
             key_gain.reshape(1, -1), cosine, sine, key_weight, value_weight, token_rows, inverse_one,
             kv_near[0], *kv_received,
         ],
-        after=attn_got,
+        after=[attn_got, out_pieces],
         through=logits_messages,
         scratch_shapes=[pltpu.VMEM((gain_rows, 128), full)],
     )
@@ -979,10 +992,10 @@
     message_rows = pair_len + 16
     last_rows, projection = kernel_call(
         last_kernel,
-        [shape_of((share, 2 * width), low), shape_of((message_rows, query_cols + 2 * head_dim), low)],
-        [in_smem] + [in_vmem] * (7 + wt_count),
-        [
-            index, token_rows, inverse_one, attn_gain.reshape(1, -1), mid_grad, out_rows, projection_own,
+        [shape_of((share, width), low), shape_of((message_rows, query_cols + 2 * head_dim), low)],
+        [in_smem] + [in_vmem] * (6 + wt_count),
+        [
+            index, token_rows, inverse_one, attn_gain.reshape(1, -1), mid_grad, projection_own,
             gains, one_own, *received,
         ],
         after=logits_near,
@@ -1015,7 +1028,6 @@
         shape_of((query_cols, block_cols), full),
         [in_vmem] * 4,
         [attn_near, attn_got, mid_keep, logits_got],
-        after=last_rows,
     )
     w_query_grad, w_key_grad, w_value_grad, *gains = kernel_call(
         functools.partial(projection_kernel, half),
@@ -1033,8 +1045,9 @@
         ],
     )
     attn_gain_grad, moe_gain_grad, query_gain_grad, key_gain_grad = [one.reshape(-1) for one in gains]
-    block_out, tokens_grad = place_rows(
-        index, last_pieces, width, 2, after=[router_grad, w_output_grad, w_query_grad]
+    (block_out,) = place_rows(index, out_pieces, width, 1)
+    (tokens_grad,) = place_rows(
+        index, last_pieces, width, 1, after=[router_grad, w_output_grad, w_query_grad]
     )
     w_router_grad = router_grad.T
 

time: 315 us -> 309 us (0.981)
  waiting for transfers between devices: 84.8 us -> 76.8 us
  starting transfers between devices: 77 us -> 84.1 us
  other arithmetic: 15.1 us -> 10 us
  Pallas kernels: 97.5 us -> 102 us
    ppermute x62 -> x69, waiting for transfers between devices: 84.8 us -> 76.8 us  [swap(): return lax.ppermute(array, axis, [(i, i ^ mask) for i in range(count)])]
    ppermute x62 -> x69, starting transfers between devices: 77 us -> 84.1 us  [swap(): return lax.ppermute(array, axis, [(i, i ^ mask) for i in range(count)])]
    pallas_call x21 -> x23, Pallas kernels: 97.5 us -> 102 us  [kernel_call(): pl.pallas_call(body, out_shape=outs + [shape_of(one.shape, one.dtype) for...]
    add x3 -> x4, other arithmetic: 5.23 us -> 1.29 us  [split_parts(): total = (near + far_sent).reshape(half, inner * share, cols)]
    dot_general x5 -> x3, matrix products: 16.9 us -> 15.8 us  [dot(): lax.dot_general(a, b, (((a_dim,), (b_dim,)), ((), ())), preferred_element...]
    unnamed x135 -> x141, local copies, waits for them, and re-layouts: 13.6 us -> 13.3 us
  transfers between devices with their start and end apart: 62 -> 69, of which waited for: 24 -> 24; matrix products, arithmetic and copies ran while one was open for 8% -> 8% of each run, Pallas kernels for 25% -> 27%
where the time goes in v2:
time: 309 us; the launch traced here: 308 us
  Pallas kernels  102 us (33%)
  starting transfers between devices  84.1 us (27%)
  waiting for transfers between devices  76.8 us (25%)
  local copies, waits for them, and re-layouts  18.1 us (6%)
  matrix products  15.8 us (5%)
  other arithmetic  10 us (3%)
    pallas_call x23, Pallas kernels, kernel_call(): pl.pallas_call(body, out_shape=outs + [shape_of(one.shape, one.dtype) for...  102 us
    ppermute x69, starting transfers between devices, swap(): return lax.ppermute(array, axis, [(i, i ^ mask) for i in range(count)])  84.1 us
    ppermute x69, waiting for transfers between devices, swap(): return lax.ppermute(array, axis, [(i, i ^ mask) for i in range(count)])  76.8 us
    dot_general x3, matrix products, dot(): lax.dot_general(a, b, (((a_dim,), (b_dim,)), ((), ())), preferred_element...  15.8 us
    unnamed x141, local copies, waits for them, and re-layouts  13.3 us
  transfers between devices with their start and end apart: 69, of which 24 were waited for; matrix products, arithmetic and copies ran while one was open for 8% of the time, Pallas kernels for 27%

profile of v2, /device:TPU:0, one launch (start us, length us, event | category | flops | bytes accessed | tf_op | source)
XLA Modules:
  0.0 308.5 jit_solution(16270414837805454334)
XLA Ops:
  3.0 3.0 shard_map.237
  6.0 3.0 collective-permute-start
  14.9 3.0 collective-permute-start.16
  17.9 3.3 %collective-permute-done.1.refs_3_ = bf16[128,768]{1,0:T(8,128)(2,1)S(1)} collective-permute-done((bf16[128,768]{1,0:T(8,128)(2,1)}, bf16[128,768]{1,0:T(8,128)(2,1)S(1)}, u32[]{:S(2)}, u32[]{:S(2)}) %collective-permute-start.1) | collective-permute-done | bytes 196640 | tf_op jit(solution)/shard_map/ppermute | solution.py:27
  25.0 4.9 %shard_map.238 = (f32[128,1024]{1,0:T(8,128)}, bf16[1024,128]{1,0:T(8,128)(2,1)}) custom-call(bf16[128,2048]{1,0:T(8,128)(2,1)} %get-tuple-element.188.refs_0_, bf16[2048,1024]{1,0:T(8,128)(2,1)} %refs_1_.2, f32[1,128]{1,0:T(1,128)} %bitcast.57, f32[128,128]{1,0:T(8,128)} %pad_maximum_fusion.refs_6_.refs_3_.refs_8_, ...), custom_call_target="tpu_custom_call" | custom-call | tf_op jit(solution)/shard_map/pallas_call | solution.py:52
  31.4 7.4 %shard_map.240 = (bf16[128,1024]{1,0:T(8,128)(2,1)}, bf16[1024,1024]{1,0:T(8,128)(2,1)}, bf16[1024,128]{1,0:T(8,128)(2,1)}, bf16[1024,128]{1,0:T(8,128)(2,1)}, f...) custom-call(s32[256,1]{1,0:T(8,128)} %copy.39.refs_0_, ...), custom_call_target="tpu_custom_call" | custom-call | tf_op jit(solution)/shard_map/pallas_call | solution.py:52
  43.0 4.6 %collective-permute-done.4.refs_4_ = bf16[32,2048]{1,0:T(8,128)(2,1)S(1)} collective-permute-done((bf16[32,2048]{1,0:T(8,128)(2,1)}, bf16[32,2048]{1,0:T(8,128)(2,1)S(1)}, u32[]{:S(2)}, u32[]{:S(2)}) %collective-permute-start.4) | collective-permute-done | bytes 131104 | tf_op jit(solution)/shard_map/ppermute | solution.py:27
  51.0 3.7 %collective-permute-done.6.refs_6_ = bf16[32,2048]{1,0:T(8,128)(2,1)S(1)} collective-permute-done((bf16[32,2048]{1,0:T(8,128)(2,1)}, bf16[32,2048]{1,0:T(8,128)(2,1)S(1)}, u32[]{:S(2)}, u32[]{:S(2)}) %collective-permute-start.6) | collective-permute-done | bytes 131104 | tf_op jit(solution)/shard_map/ppermute | solution.py:27
  58.6 3.0 shard_map.245
  64.8 5.7 %collective-permute-done.7.refs_1_ = bf16[32,2176]{1,0:T(8,128)(2,1)S(1)} collective-permute-done((bf16[32,2176]{1,0:T(8,128)(2,1)S(1)}, bf16[32,2176]{1,0:T(8,128)(2,1)S(1)}, u32[]{:S(2)}, u32[]{:S(2)}) %collective-permute-start.7) | collective-permute-done | bytes 139296 | tf_op jit(solution)/shard_map/ppermute | solution.py:27
  78.0 5.4 %collective-permute-done.12.refs_2_ = bf16[32,2176]{1,0:T(8,128)(2,1)S(1)} collective-permute-done((bf16[32,2176]{1,0:T(8,128)(2,1)S(1)}, bf16[32,2176]{1,0:T(8,128)(2,1)S(1)}, u32[]{:S(2)}, u32[]{:S(2)}) %collective-permute-start.12) | collective-permute-done | bytes 139296 | tf_op jit(solution)/shard_map/ppermute | solution.py:27
  96.5 14.7 %shard_map.246 = (bf16[256,2176]{1,0:T(8,128)(2,1)}, bf16[256,2176]{1,0:T(8,128)(2,1)}, bf16[256,2048]{1,0:T(8,128)(2,1)}, bf16[256,2048]{1,0:T(8,128)(2,1)}, bf...) custom-call(s32[2]{0:T(128)} %pad_add_fusion.1.refs_0_, ...), custom_call_target="tpu_custom_call" | custom-call | tf_op jit(solution)/shard_map/pallas_call | solution.py:52
  111.2 7.4 %collective-permute-done.19.refs_2_ = bf16[64,4224]{1,0:T(8,128)(2,1)} collective-permute-done((bf16[64,4224]{1,0:T(8,128)(2,1)S(1)}, bf16[64,4224]{1,0:T(8,128)(2,1)}, u32[]{:S(2)}, u32[]{:S(2)}) %collective-permute-start.19) | collective-permute-done | bytes 540704 | tf_op jit(solution)/shard_map/ppermute | solution.py:27
  118.6 3.1 %shard_map.247 = (bf16[256,2176]{1,0:T(8,128)(2,1)}, bf16[512,1024]{1,0:T(8,128)(2,1)}) custom-call(bf16[64,4224]{1,0:T(8,128)(2,1)} %shard_map.243.refs_4_.refs_0_, bf16[64,4224]{1,0:T(8,128)(2,1)} %copy-done.28, bf16[64,4224]{1,0:T(8,128)(2,1)} %collective-permute-done.19.refs_2_, bf16[64,4224]{1,0:T(8,128)(2,1)} %collective-permute-done.20.refs_3_), custom_call_target="tpu_custom_call" | custom-call | tf_op jit(solution)/shard_map/pallas_call | solution.py:52
  128.3 14.9 %shard_map.248 = (bf16[256,2176]{1,0:T(8,128)(2,1)}, bf16[256,2176]{1,0:T(8,128)(2,1)}, bf16[256,2048]{1,0:T(8,128)(2,1)}, bf16[256,2048]{1,0:T(8,128)(2,1)}, bf...) custom-call(s32[2]{0:T(128)} %pad_add_fusion.1.refs_0_, ...), custom_call_target="tpu_custom_call", output_to_operand_aliasing={{4}: (8, {}), {5}: (9, {}), {6}: (10, {}), {7}: (11, {}), {... | custom-call | tf_op jit(solution)/shard_map/pallas_call | solution.py:52
  144.0 3.8 %collective-permute-done.21 = bf16[256,2048]{1,0:T(8,128)(2,1)S(1)} collective-permute-done((bf16[256,2048]{1,0:T(8,128)(2,1)}, bf16[256,2048]{1,0:T(8,128)(2,1)S(1)}, u32[]{:S(2)}, u32[]{:S(2)}) %collective-permute-start.21) | collective-permute-done | bytes 1048608 | tf_op jit(solution)/shard_map/ppermute | solution.py:27
  154.5 6.6 %fusion.18 = f32[2048,1536]{1,0:T(8,128)} fusion(bf16[352,2048]{1,0:T(8,128)(2,1)S(1)} %copy-done.1, bf16[352,1536]{1,0:T(8,128)(2,1)S(1)} %copy-done.4), kind=kOutput, calls=%fused_computation.49 | convolution fusion | flops 2214592512 | bytes 15106048 | tf_op jit(solution)/shard_map/dot_general | solution.py:22
  161.1 4.5 %fusion.19 = f32[768,2048]{1,0:T(8,128)} fusion(bf16[352,768]{1,0:T(8,128)(2,1)S(1)} %copy-done.6, bf16[352,2048]{1,0:T(8,128)(2,1)S(1)} %copy-done.2), kind=kOutput, calls=%fused_computation.50 | convolution fusion | flops 1107296256 | bytes 8273920 | tf_op jit(solution)/shard_map/dot_general | solution.py:22
  167.9 4.1 %collective-permute-done.30 = bf16[64,2176]{1,0:T(8,128)(2,1)S(1)} collective-permute-done((bf16[64,2176]{1,0:T(8,128)(2,1)S(1)}, bf16[64,2176]{1,0:T(8,128)(2,1)S(1)}, u32[]{:S(2)}, u32[]{:S(2)}) %collective-permute-start.30) | collective-permute-done | bytes 278560 | tf_op jit(solution)/shard_map/ppermute | solution.py:27
  176.6 5.9 %collective-permute-done.36.refs_13_ = bf16[64,2048]{1,0:T(8,128)(2,1)S(1)} collective-permute-done((bf16[64,2048]{1,0:T(8,128)(2,1)S(1)}, bf16[64,2048]{1,0:T(8,128)(2,1)S(1)}, u32[]{:S(2)}, u32[]{:S(2)}) %collective-permute-start.36) | collective-permute-done | bytes 262176 | tf_op jit(solution)/shard_map/ppermute | solution.py:27
  187.0 3.0 collective-permute-done.34.refs_11_
  190.0 3.1 shard_map.249
  200.6 5.7 %collective-permute-done.39.refs_12_ = bf16[32,2176]{1,0:T(8,128)(2,1)S(1)} collective-permute-done((bf16[32,2176]{1,0:T(8,128)(2,1)}, bf16[32,2176]{1,0:T(8,128)(2,1)S(1)}, u32[]{:S(2)}, u32[]{:S(2)}) %collective-permute-start.39) | collective-permute-done | bytes 139296 | tf_op jit(solution)/shard_map/ppermute | solution.py:27
  214.5 11.1 %shard_map.250 = (bf16[512,256]{1,0:T(8,128)(2,1)}, bf16[512,256]{1,0:T(8,128)(2,1)}, bf16[128,1024]{1,0:T(8,128)(2,1)}, f32[1,128]{1,0:T(1,128)}, bf16[128,640]...) custom-call(s32[1]{0:T(128)} %bitcast.1.refs_0_, ...), custom_call_target="tpu_custom_call" | custom-call | tf_op jit(solution)/shard_map/pallas_call | solution.py:52
  237.1 4.7 %fusion.20.refs_2_ = f32[128,2048]{1,0:T(8,128)} fusion(bf16[128,1024]{1,0:T(8,128)(2,1)S(1)} %copy-done.24, bf16[2048,1024]{1,0:T(8,128)(2,1)} %refs_1_.2), kind=kOutput, calls=%fused_computation.51 | convolution fusion | flops 536870912 | bytes 5505024 | tf_op jit(solution)/shard_map/dot_general | solution.py:22
  245.0 3.5 %shard_map.252 = (f32[32,2048]{1,0:T(8,128)}, bf16[32,2432]{1,0:T(8,128)(2,1)}, bf16[32,2432]{1,0:T(8,128)(2,1)}, bf16[32,2432]{1,0:T(8,128)(2,1)}, bf16[128,128...) custom-call(f32[1,2048]{1,0:T(1,128)} %get-tuple-element.320.refs_0_, ...), custom_call_target="tpu_custom_call", output_to_operand_aliasing={{6}: (21, {}), {7}: (22, {}), {8}: (23, {}), {9}: (24, {})} | custom-call | tf_op jit(solution)/shard_map/pallas_call | solution.py:52
  260.1 7.1 %collective-permute-done.56.refs_9_ = bf16[32,2432]{1,0:T(8,128)(2,1)S(1)} collective-permute-done((bf16[32,2432]{1,0:T(8,128)(2,1)}, bf16[32,2432]{1,0:T(8,128)(2,1)S(1)}, u32[]{:S(2)}, u32[]{:S(2)}) %collective-permute-start.56) | collective-permute-done | bytes 155680 | tf_op jit(solution)/shard_map/ppermute | solution.py:27
  276.4 3.5 %collective-permute-done.61.refs_4_.refs_2_ = bf16[32,2048]{1,0:T(8,128)(2,1)S(1)} collective-permute-done((bf16[32,2048]{1,0:T(8,128)(2,1)}, bf16[32,2048]{1,0:T(8,128)(2,1)S(1)}, u32[]{:S(2)}, u32[]{:S(2)}) %collective-permute-start.61) | collective-permute-done | bytes 131104 | tf_op jit(solution)/shard_map/ppermute | solution.py:27
  281.7 2.9 collective-permute-start.63
  285.3 3.5 %shard_map.256.refs_7_.refs_6_ = f32[1024,256]{1,0:T(8,128)} custom-call(bf16[512,1024]{1,0:T(8,128)(2,1)} %get-tuple-element.332.refs_0_, bf16[512,1024]{1,0:T(8,128)(2,1)} %copy-done.5, bf16[512,256]{1,0:T(8,128)(2,1)} %get-tuple-element.351.refs_2_, bf16[512,384]{1,0:T(8,128)(2,1)} %copy-done.9), custom_call_target="tpu_custom_call" | custom-call | tf_op jit(solution)/shard_map/pallas_call | solution.py:52
  288.7 5.0 %shard_map.255.refs_8_.refs_5_ = f32[32,2048]{1,0:T(8,128)} custom-call(s32[2]{0:T(128)} %pad_add_fusion.2.refs_0_, bf16[2,8,2,32,2048]{4,3,2,1,0:T(8,128)(2,1)} %bitcast.36, bf16[512,128]{1,0:T(8,128)(2,1)} %get-tuple-element.349.refs_2_, bf16[512,384]{1,0:T(8,128)(2,1)} %copy-done.9), custom_call_target="tpu_custom_call" | custom-call | tf_op jit(solution)/shard_map/pallas_call | solution.py:52
  302.6 4.0 %shard_map.258 = (f32[256,1024]{1,0:T(8,128)}, f32[256,128]{1,0:T(8,128)}, f32[256,128]{1,0:T(8,128)}, f32[16,128]{1,0:T(8,128)}, f32[16,128]{1,0:T(8,128)}, /*index=5*/f32[1,128]{1,0:T(1,128)}, f32[1,128]{1,0:T(1,128)}) custom-call(s32[1]{0:T(128)} %bitcast.17.refs_0_, bf16[512,256]{1,0:T(8,128)(2,1)} %get-tuple-element.352.refs_1_, ...), custom_call_target="tpu_custom_call" | custom-call | tf_op jit(solution)/shard_map/pallas_call | solution.py:52
  (309 shorter events, 138.2 us)
Async XLA Ops:
  10.5 47.0 %collective-permute-start.14 = (bf16[128,2048]{1,0:T(8,128)(2,1)S(1)}, bf16[128,2048]{1,0:T(8,128)(2,1)S(1)}, u32[]{:S(2)}, u32[]{:S(2)}) collective-permute-start(bf16[128,2048]{1,0:T(8,128)(2,1)S(1)} %bitcast.43), channel_id=1, source_target_pairs={{0,8},{4,12},{8,0},{12,4},{16,24},{20,28},{24,16},{28,20},{1,9},{5... | collective-permute-start | bytes 1572872 | tf_op jit(solution)/shard_map/ppermute | solution.py:27
  12.4 45.0 %collective-permute-start.15 = (bf16[128,2048]{1,0:T(8,128)(2,1)S(1)}, bf16[128,2048]{1,0:T(8,128)(2,1)S(1)}, u32[]{:S(2)}, u32[]{:S(2)}) collective-permute-start(bf16[128,2048]{1,0:T(8,128)(2,1)S(1)} %bitcast.44), channel_id=1, source_target_pairs={{0,16},{4,20},{8,24},{12,28},{16,0},{20,4},{24,8},{28,12},{1,17},{... | collective-permute-start | bytes 1572872 | tf_op jit(solution)/shard_map/ppermute | solution.py:27
  14.9 42.6 %collective-permute-start.16 = (bf16[128,2048]{1,0:T(8,128)(2,1)S(1)}, bf16[128,2048]{1,0:T(8,128)(2,1)S(1)}, u32[]{:S(2)}, u32[]{:S(2)}) collective-permute-start(bf16[128,2048]{1,0:T(8,128)(2,1)S(1)} %bitcast.45), channel_id=1, source_target_pairs={{0,24},{4,28},{8,16},{12,20},{16,8},{20,12},{24,0},{28,4},{1,25},{... | collective-permute-start | bytes 1572872 | tf_op jit(solution)/shard_map/ppermute | solution.py:27
  61.6 33.5 %collective-permute-start.17 = (bf16[512,2048]{1,0:T(8,128)(2,1)}, bf16[512,2048]{1,0:T(8,128)(2,1)S(1)}, u32[]{:S(2)}, u32[]{:S(2)}) collective-permute-start(bf16[512,2048]{1,0:T(8,128)(2,1)} %shard_map.245), channel_id=1, source_target_pairs={{0,4},{4,0},{8,12},{12,8},{16,20},{20,16},{24,28},{28,24},{1,5},{5... | collective-permute-start | bytes 6291464 | tf_op jit(solution)/shard_map/ppermute | solution.py:27
  63.2 13.2 %collective-permute-start.11 = (bf16[32,2176]{1,0:T(8,128)(2,1)S(1)}, bf16[32,2176]{1,0:T(8,128)(2,1)S(1)}, u32[]{:S(2)}, u32[]{:S(2)}) collective-permute-start(bf16[32,2176]{1,0:T(8,128)(2,1)S(1)} %copy-done.11), channel_id=1, source_target_pairs={{0,2},{1,3},{2,0},{3,1},{4,6},{5,7},{6,4},{7,5},{8,10},{9,11},{10,... | collective-permute-start | bytes 417800 | tf_op jit(solution)/shard_map/ppermute | solution.py:27
  72.9 13.1 %collective-permute-start.8 = (bf16[64,2176]{1,0:T(8,128)(2,1)}, bf16[64,2176]{1,0:T(8,128)(2,1)S(1)}, u32[]{:S(2)}, u32[]{:S(2)}) collective-permute-start(bf16[64,2176]{1,0:T(8,128)(2,1)} %shard_map.242.refs_0_), channel_id=1, source_target_pairs={{0,8},{4,12},{8,0},{12,4},{16,24},{20,28},{24,16},{28,20},{1,9},{5... | collective-permute-start | bytes 835592 | tf_op jit(solution)/shard_map/ppermute | solution.py:27
  75.0 13.0 %collective-permute-start.10 = (bf16[64,2176]{1,0:T(8,128)(2,1)}, bf16[64,2176]{1,0:T(8,128)(2,1)S(1)}, u32[]{:S(2)}, u32[]{:S(2)}) collective-permute-start(bf16[64,2176]{1,0:T(8,128)(2,1)} %shard_map.242.refs_0_), channel_id=1, source_target_pairs={{0,24},{4,28},{8,16},{12,20},{16,8},{20,12},{24,0},{28,4},{1,25},{... | collective-permute-start | bytes 835592 | tf_op jit(solution)/shard_map/ppermute | solution.py:27
  91.1 20.1 %collective-permute-start.18 = (bf16[64,4224]{1,0:T(8,128)(2,1)S(1)}, bf16[64,4224]{1,0:T(8,128)(2,1)S(1)}, u32[]{:S(2)}, u32[]{:S(2)}) collective-permute-start(bf16[64,4224]{1,0:T(8,128)(2,1)S(1)} %copy-done.3), channel_id=1, source_target_pairs={{0,8},{4,12},{8,0},{12,4},{16,24},{20,28},{24,16},{28,20},{1,9},{5... | collective-permute-start | bytes 1622024 | tf_op jit(solution)/shard_map/ppermute | solution.py:27
  92.5 26.1 %collective-permute-start.19 = (bf16[64,4224]{1,0:T(8,128)(2,1)S(1)}, bf16[64,4224]{1,0:T(8,128)(2,1)}, u32[]{:S(2)}, u32[]{:S(2)}) collective-permute-start(bf16[64,4224]{1,0:T(8,128)(2,1)S(1)} %copy-done.3), channel_id=1, source_target_pairs={{0,16},{4,20},{8,24},{12,28},{16,0},{20,4},{24,8},{28,12},{1,17},{... | collective-permute-start | bytes 1622024 | tf_op jit(solution)/shard_map/ppermute | solution.py:27
  94.1 24.5 %collective-permute-start.20 = (bf16[64,4224]{1,0:T(8,128)(2,1)S(1)}, bf16[64,4224]{1,0:T(8,128)(2,1)}, u32[]{:S(2)}, u32[]{:S(2)}) collective-permute-start(bf16[64,4224]{1,0:T(8,128)(2,1)S(1)} %copy-done.3), channel_id=1, source_target_pairs={{0,24},{4,28},{8,16},{12,20},{16,8},{20,12},{24,0},{28,4},{1,25},{... | collective-permute-start | bytes 1622024 | tf_op jit(solution)/shard_map/ppermute | solution.py:27
  124.8 18.4 %collective-permute-start.24 = (bf16[64,2176]{1,0:T(8,128)(2,1)}, bf16[64,2176]{1,0:T(8,128)(2,1)S(1)}, u32[]{:S(2)}, u32[]{:S(2)}) collective-permute-start(bf16[64,2176]{1,0:T(8,128)(2,1)} %get-tuple-element.236), channel_id=1, source_target_pairs={{0,8},{4,12},{8,0},{12,4},{16,24},{20,28},{24,16},{28,20},{1,9},{5... | collective-permute-start | bytes 835592 | tf_op jit(solution)/shard_map/ppermute | solution.py:27
  126.1 17.1 %collective-permute-start.25 = (bf16[64,2176]{1,0:T(8,128)(2,1)S(1)}, bf16[64,2176]{1,0:T(8,128)(2,1)S(1)}, u32[]{:S(2)}, u32[]{:S(2)}) collective-permute-start(bf16[64,2176]{1,0:T(8,128)(2,1)S(1)} %get-tuple-element.237), channel_id=1, source_target_pairs={{0,16},{4,20},{8,24},{12,28},{16,0},{20,4},{24,8},{28,12},{1,17},{... | collective-permute-start | bytes 835592 | tf_op jit(solution)/shard_map/ppermute | solution.py:27
  126.9 16.3 %collective-permute-start.26 = (bf16[64,2176]{1,0:T(8,128)(2,1)S(1)}, bf16[64,2176]{1,0:T(8,128)(2,1)S(1)}, u32[]{:S(2)}, u32[]{:S(2)}) collective-permute-start(bf16[64,2176]{1,0:T(8,128)(2,1)S(1)} %get-tuple-element.238), channel_id=1, source_target_pairs={{0,24},{4,28},{8,16},{12,20},{16,8},{20,12},{24,0},{28,4},{1,25},{... | collective-permute-start | bytes 835592 | tf_op jit(solution)/shard_map/ppermute | solution.py:27
  149.4 22.5 %collective-permute-start.31 = (bf16[256,2048]{1,0:T(8,128)(2,1)S(1)}, bf16[256,2048]{1,0:T(8,128)(2,1)S(1)}, u32[]{:S(2)}, u32[]{:S(2)}) collective-permute-start(bf16[256,2048]{1,0:T(8,128)(2,1)S(1)} %copy-done.69), channel_id=1, source_target_pairs={{0,4},{4,0},{8,12},{12,8},{16,20},{20,16},{24,28},{28,24},{1,5},{5... | collective-permute-start | bytes 3145736 | tf_op jit(solution)/shard_map/ppermute | solution.py:27
  149.7 24.6 %collective-permute-start.35 = (bf16[64,2048]{1,0:T(8,128)(2,1)S(1)}, bf16[64,2048]{1,0:T(8,128)(2,1)S(1)}, u32[]{:S(2)}, u32[]{:S(2)}) collective-permute-start(bf16[64,2048]{1,0:T(8,128)(2,1)S(1)} %get-tuple-element.380), channel_id=1, source_target_pairs={{0,8},{4,12},{8,0},{12,4},{16,24},{20,28},{24,16},{28,20},{1,9},{5... | collective-permute-start | bytes 786440 | tf_op jit(solution)/shard_map/ppermute | solution.py:27
  151.0 14.7 %collective-permute-start.28 = (bf16[64,2176]{1,0:T(8,128)(2,1)S(1)}, bf16[64,2176]{1,0:T(8,128)(2,1)S(1)}, u32[]{:S(2)}, u32[]{:S(2)}) collective-permute-start(bf16[64,2176]{1,0:T(8,128)(2,1)S(1)} %get-tuple-element.267), channel_id=1, source_target_pairs={{0,8},{4,12},{8,0},{12,4},{16,24},{20,28},{24,16},{28,20},{1,9},{5... | collective-permute-start | bytes 835592 | tf_op jit(solution)/shard_map/ppermute | solution.py:27
  151.8 14.8 %collective-permute-start.29 = (bf16[64,2176]{1,0:T(8,128)(2,1)S(1)}, bf16[64,2176]{1,0:T(8,128)(2,1)S(1)}, u32[]{:S(2)}, u32[]{:S(2)}) collective-permute-start(bf16[64,2176]{1,0:T(8,128)(2,1)S(1)} %get-tuple-element.268), channel_id=1, source_target_pairs={{0,16},{4,20},{8,24},{12,28},{16,0},{20,4},{24,8},{28,12},{1,17},{... | collective-permute-start | bytes 835592 | tf_op jit(solution)/shard_map/ppermute | solution.py:27
  153.3 18.6 %collective-permute-start.30 = (bf16[64,2176]{1,0:T(8,128)(2,1)S(1)}, bf16[64,2176]{1,0:T(8,128)(2,1)S(1)}, u32[]{:S(2)}, u32[]{:S(2)}) collective-permute-start(bf16[64,2176]{1,0:T(8,128)(2,1)S(1)} %get-tuple-element.269), channel_id=1, source_target_pairs={{0,24},{4,28},{8,16},{12,20},{16,8},{20,12},{24,0},{28,4},{1,25},{... | collective-permute-start | bytes 835592 | tf_op jit(solution)/shard_map/ppermute | solution.py:27
  165.7 16.8 %collective-permute-start.36 = (bf16[64,2048]{1,0:T(8,128)(2,1)S(1)}, bf16[64,2048]{1,0:T(8,128)(2,1)S(1)}, u32[]{:S(2)}, u32[]{:S(2)}) collective-permute-start(bf16[64,2048]{1,0:T(8,128)(2,1)S(1)} %get-tuple-element.379), channel_id=1, source_target_pairs={{0,16},{4,20},{8,24},{12,28},{16,0},{20,4},{24,8},{28,12},{1,17},{... | collective-permute-start | bytes 786440 | tf_op jit(solution)/shard_map/ppermute | solution.py:27
  166.5 17.6 %collective-permute-start.37 = (bf16[64,2048]{1,0:T(8,128)(2,1)S(1)}, bf16[64,2048]{1,0:T(8,128)(2,1)S(1)}, u32[]{:S(2)}, u32[]{:S(2)}) collective-permute-start(bf16[64,2048]{1,0:T(8,128)(2,1)S(1)} %get-tuple-element.378), channel_id=1, source_target_pairs={{0,24},{4,28},{8,16},{12,20},{16,8},{20,12},{24,0},{28,4},{1,25},{... | collective-permute-start | bytes 786440 | tf_op jit(solution)/shard_map/ppermute | solution.py:27
  173.5 21.9 %collective-permute-start.41 = (bf16[64,2048]{1,0:T(8,128)(2,1)}, bf16[64,2048]{1,0:T(8,128)(2,1)S(1)}, u32[]{:S(2)}, u32[]{:S(2)}) collective-permute-start(bf16[64,2048]{1,0:T(8,128)(2,1)} %get-tuple-element.377), channel_id=1, source_target_pairs={{0,8},{4,12},{8,0},{12,4},{16,24},{20,28},{24,16},{28,20},{1,9},{5... | collective-permute-start | bytes 786440 | tf_op jit(solution)/shard_map/ppermute | solution.py:27
  184.2 13.8 %collective-permute-start.42 = (bf16[64,2048]{1,0:T(8,128)(2,1)}, bf16[64,2048]{1,0:T(8,128)(2,1)S(1)}, u32[]{:S(2)}, u32[]{:S(2)}) collective-permute-start(bf16[64,2048]{1,0:T(8,128)(2,1)} %get-tuple-element.376), channel_id=1, source_target_pairs={{0,16},{4,20},{8,24},{12,28},{16,0},{20,4},{24,8},{28,12},{1,17},{... | collective-permute-start | bytes 786440 | tf_op jit(solution)/shard_map/ppermute | solution.py:27
  184.8 13.1 %collective-permute-start.43 = (bf16[64,2048]{1,0:T(8,128)(2,1)}, bf16[64,2048]{1,0:T(8,128)(2,1)S(1)}, u32[]{:S(2)}, u32[]{:S(2)}) collective-permute-start(bf16[64,2048]{1,0:T(8,128)(2,1)} %get-tuple-element.375), channel_id=1, source_target_pairs={{0,24},{4,28},{8,16},{12,20},{16,8},{20,12},{24,0},{28,4},{1,25},{... | collective-permute-start | bytes 786440 | tf_op jit(solution)/shard_map/ppermute | solution.py:27
  193.1 13.2 %collective-permute-start.39 = (bf16[32,2176]{1,0:T(8,128)(2,1)}, bf16[32,2176]{1,0:T(8,128)(2,1)S(1)}, u32[]{:S(2)}, u32[]{:S(2)}) collective-permute-start(bf16[32,2176]{1,0:T(8,128)(2,1)} %get-tuple-element.297.refs_10_), channel_id=1, source_target_pairs={{0,2},{1,3},{2,0},{3,1},{4,6},{5,7},{6,4},{7,5},{8,10},{9,11},{10,... | collective-permute-start | bytes 417800 | tf_op jit(solution)/shard_map/ppermute | solution.py:27
  210.1 15.5 %collective-permute-start.44 = (bf16[32,2048]{1,0:T(8,128)(2,1)}, bf16[32,2048]{1,0:T(8,128)(2,1)S(1)}, u32[]{:S(2)}, u32[]{:S(2)}) collective-permute-start(bf16[32,2048]{1,0:T(8,128)(2,1)} %slice.180), channel_id=1, source_target_pairs={{0,1},{1,0},{2,3},{3,2},{4,5},{5,4},{6,7},{7,6},{8,9},{9,8},{10,11... | collective-permute-start | bytes 393224 | tf_op jit(solution)/shard_map/ppermute | solution.py:27
  211.8 13.8 %collective-permute-start.45 = (bf16[32,2048]{1,0:T(8,128)(2,1)S(1)}, bf16[32,2048]{1,0:T(8,128)(2,1)S(1)}, u32[]{:S(2)}, u32[]{:S(2)}) collective-permute-start(bf16[32,2048]{1,0:T(8,128)(2,1)S(1)} %get-tuple-element.305), channel_id=1, source_target_pairs={{0,2},{1,3},{2,0},{3,1},{4,6},{5,7},{6,4},{7,5},{8,10},{9,11},{10,... | collective-permute-start | bytes 393224 | tf_op jit(solution)/shard_map/ppermute | solution.py:27
  214.5 27.3 %collective-permute-start.54 = (bf16[512,1024]{1,0:T(8,128)(2,1)S(1)}, bf16[512,1024]{1,0:T(8,128)(2,1)S(1)}, u32[]{:S(2)}, u32[]{:S(2)}) collective-permute-start(bf16[512,1024]{1,0:T(8,128)(2,1)S(1)} %copy-done.19), channel_id=1, source_target_pairs={{0,4},{4,0},{8,12},{12,8},{16,20},{20,16},{24,28},{28,24},{1,5},{5... | collective-permute-start | bytes 3145736 | tf_op jit(solution)/shard_map/ppermute | solution.py:27
  260.1 21.7 %collective-permute-start.64 = (bf16[512,384]{1,0:T(8,128)(2,1)}, bf16[512,384]{1,0:T(8,128)(2,1)S(1)}, u32[]{:S(2)}, u32[]{:S(2)}) collective-permute-start(bf16[512,384]{1,0:T(8,128)(2,1)} %get-tuple-element.350), channel_id=1, source_target_pairs={{0,4},{4,0},{8,12},{12,8},{16,20},{20,16},{24,28},{28,24},{1,5},{5... | collective-permute-start | bytes 1179656 | tf_op jit(solution)/shard_map/ppermute | solution.py:27
  270.3 23.5 %collective-permute-start.65 = (bf16[144,1280]{1,0:T(8,128)(2,1)}, bf16[144,1280]{1,0:T(8,128)(2,1)S(1)}, u32[]{:S(2)}, u32[]{:S(2)}) collective-permute-start(bf16[144,1280]{1,0:T(8,128)(2,1)} %get-tuple-element.353.refs_0_), channel_id=1, source_target_pairs={{0,8},{4,12},{8,0},{12,4},{16,24},{20,28},{24,16},{28,20},{1,9},{5... | collective-permute-start | bytes 1105928 | tf_op jit(solution)/shard_map/ppermute | solution.py:27
  271.2 22.6 %collective-permute-start.66 = (bf16[144,1280]{1,0:T(8,128)(2,1)}, bf16[144,1280]{1,0:T(8,128)(2,1)S(1)}, u32[]{:S(2)}, u32[]{:S(2)}) collective-permute-start(bf16[144,1280]{1,0:T(8,128)(2,1)} %get-tuple-element.353.refs_0_), channel_id=1, source_target_pairs={{0,16},{4,20},{8,24},{12,28},{16,0},{20,4},{24,8},{28,12},{1,17},{... | collective-permute-start | bytes 1105928 | tf_op jit(solution)/shard_map/ppermute | solution.py:27
  272.7 21.2 %collective-permute-start.67 = (bf16[144,1280]{1,0:T(8,128)(2,1)}, bf16[144,1280]{1,0:T(8,128)(2,1)S(1)}, u32[]{:S(2)}, u32[]{:S(2)}) collective-permute-start(bf16[144,1280]{1,0:T(8,128)(2,1)} %get-tuple-element.353.refs_0_), channel_id=1, source_target_pairs={{0,24},{4,28},{8,16},{12,20},{16,8},{20,12},{24,0},{28,4},{1,25},{... | collective-permute-start | bytes 1105928 | tf_op jit(solution)/shard_map/ppermute | solution.py:27
  279.9 13.9 %collective-permute-start.62 = (bf16[32,2048]{1,0:T(8,128)(2,1)}, bf16[32,2048]{1,0:T(8,128)(2,1)S(1)}, u32[]{:S(2)}, u32[]{:S(2)}) collective-permute-start(bf16[32,2048]{1,0:T(8,128)(2,1)} %get-tuple-element.347.refs_1_), channel_id=1, source_target_pairs={{0,2},{1,3},{2,0},{3,1},{4,6},{5,7},{6,4},{7,5},{8,10},{9,11},{10,... | collective-permute-start | bytes 393224 | tf_op jit(solution)/shard_map/ppermute | solution.py:27
  (107 other events, 670.7 us)

commit v3 on v2

--- a/solution.py
+++ b/solution.py
@@ -823,7 +823,7 @@
 
     first = join([message] + [swap(message, "wt", m) for m in range(1, inner)])
     others = [swap(message, "wt", m) for m in range(inner, wt_count)]
-    grads = [one.reshape(half, wt_count, share, width) for one in both(grad_near, message)]
+    grads = [one.reshape(half, wt_count, share, width) for one in both(grad_near, first)]
     chunks = pair_len // (inner * share)
     second = kernel_call(
         pack_kernel,
@@ -901,7 +901,6 @@
             index, sums[0], message, own_mask, router, mid_rows, inverse_two, moe_gain.reshape(1, -1),
             cotangent.reshape(wt_count, share, width), *received,
         ],
-        after=moe_received,
         scratch_shapes=[pltpu.VMEM((share, extra_cols), full)],
     )
 

time: 309 us -> 302 us (0.977)
  waiting for transfers between devices: 76.8 us -> 70.1 us
    ppermute x69, waiting for transfers between devices: 76.8 us -> 70.1 us  [swap(): return lax.ppermute(array, axis, [(i, i ^ mask) for i in range(count)])]
  transfers between devices with their start and end apart: 69 -> 69, of which waited for: 24 -> 22; matrix products, arithmetic and copies ran while one was open for 8% -> 9% of each run, Pallas kernels for 27% -> 28%
where the time goes in v3:
time: 302 us
  Pallas kernels  102 us (34%)
  starting transfers between devices  84.2 us (28%)
  waiting for transfers between devices  70.1 us (23%)
  local copies, waits for them, and re-layouts  18.8 us (6%)
  matrix products  15.8 us (5%)
  other arithmetic  8.93 us (3%)
    pallas_call x23, Pallas kernels, kernel_call(): pl.pallas_call(body, out_shape=outs + [shape_of(one.shape, one.dtype) for...  102 us
    ppermute x69, starting transfers between devices, swap(): return lax.ppermute(array, axis, [(i, i ^ mask) for i in range(count)])  84.2 us
    ppermute x69, waiting for transfers between devices, swap(): return lax.ppermute(array, axis, [(i, i ^ mask) for i in range(count)])  70.1 us
    dot_general x3, matrix products, dot(): lax.dot_general(a, b, (((a_dim,), (b_dim,)), ((), ())), preferred_element...  15.8 us
    unnamed x141, local copies, waits for them, and re-layouts  14 us
  transfers between devices with their start and end apart: 69, of which 22 were waited for; matrix products, arithmetic and copies ran while one was open for 9% of the time, Pallas kernels for 28%

profile of v3, /device:TPU:0, one launch (start us, length us, event | category | flops | bytes accessed | tf_op | source)
XLA Modules:
  0.0 301.6 jit_solution(14338348199962560195)
XLA Ops:
  3.0 3.0 shard_map.237
  6.0 3.0 collective-permute-start
  14.7 4.9 %shard_map.238 = (f32[128,1024]{1,0:T(8,128)}, bf16[1024,128]{1,0:T(8,128)(2,1)}) custom-call(bf16[128,2048]{1,0:T(8,128)(2,1)} %get-tuple-element.188.refs_0_, bf16[2048,1024]{1,0:T(8,128)(2,1)} %refs_1_.2, f32[1,128]{1,0:T(1,128)} %bitcast.57, f32[128,128]{1,0:T(8,128)} %pad_maximum_fusion.refs_6_.refs_3_.refs_8_, ...), custom_call_target="tpu_custom_call" | custom-call | tf_op jit(solution)/shard_map/pallas_call | solution.py:52
  27.0 7.4 %shard_map.240 = (bf16[128,1024]{1,0:T(8,128)(2,1)}, bf16[1024,1024]{1,0:T(8,128)(2,1)}, bf16[1024,128]{1,0:T(8,128)(2,1)}, bf16[1024,128]{1,0:T(8,128)(2,1)}, f...) custom-call(s32[256,1]{1,0:T(8,128)} %copy.39.refs_0_, ...), custom_call_target="tpu_custom_call" | custom-call | tf_op jit(solution)/shard_map/pallas_call | solution.py:52
  38.6 3.9 %collective-permute-done.4.refs_4_ = bf16[32,2048]{1,0:T(8,128)(2,1)S(1)} collective-permute-done((bf16[32,2048]{1,0:T(8,128)(2,1)}, bf16[32,2048]{1,0:T(8,128)(2,1)S(1)}, u32[]{:S(2)}, u32[]{:S(2)}) %collective-permute-start.4) | collective-permute-done | bytes 131104 | tf_op jit(solution)/shard_map/ppermute | solution.py:27
  42.5 2.9 collective-permute-start.6
  46.2 3.4 %collective-permute-done.6.refs_6_ = bf16[32,2048]{1,0:T(8,128)(2,1)S(1)} collective-permute-done((bf16[32,2048]{1,0:T(8,128)(2,1)}, bf16[32,2048]{1,0:T(8,128)(2,1)S(1)}, u32[]{:S(2)}, u32[]{:S(2)}) %collective-permute-start.6) | collective-permute-done | bytes 131104 | tf_op jit(solution)/shard_map/ppermute | solution.py:27
  54.3 3.9 %collective-permute-done.7.refs_1_ = bf16[32,2176]{1,0:T(8,128)(2,1)S(1)} collective-permute-done((bf16[32,2176]{1,0:T(8,128)(2,1)}, bf16[32,2176]{1,0:T(8,128)(2,1)S(1)}, u32[]{:S(2)}, u32[]{:S(2)}) %collective-permute-start.7) | collective-permute-done | bytes 139296 | tf_op jit(solution)/shard_map/ppermute | solution.py:27
  62.3 3.0 shard_map.245
  71.1 4.1 %collective-permute-done.11.refs_1_ = bf16[32,2176]{1,0:T(8,128)(2,1)S(1)} collective-permute-done((bf16[32,2176]{1,0:T(8,128)(2,1)S(1)}, bf16[32,2176]{1,0:T(8,128)(2,1)S(1)}, u32[]{:S(2)}, u32[]{:S(2)}) %collective-permute-start.11) | collective-permute-done | bytes 139296 | tf_op jit(solution)/shard_map/ppermute | solution.py:27
  77.5 4.8 %collective-permute-done.12.refs_2_ = bf16[32,2176]{1,0:T(8,128)(2,1)S(1)} collective-permute-done((bf16[32,2176]{1,0:T(8,128)(2,1)S(1)}, bf16[32,2176]{1,0:T(8,128)(2,1)S(1)}, u32[]{:S(2)}, u32[]{:S(2)}) %collective-permute-start.12) | collective-permute-done | bytes 139296 | tf_op jit(solution)/shard_map/ppermute | solution.py:27
  93.4 14.7 %shard_map.246 = (bf16[256,2176]{1,0:T(8,128)(2,1)}, bf16[256,2176]{1,0:T(8,128)(2,1)}, bf16[256,2048]{1,0:T(8,128)(2,1)}, bf16[256,2048]{1,0:T(8,128)(2,1)}, bf...) custom-call(s32[2]{0:T(128)} %pad_add_fusion.1.refs_0_, ...), custom_call_target="tpu_custom_call" | custom-call | tf_op jit(solution)/shard_map/pallas_call | solution.py:52
  108.2 5.5 %collective-permute-done.19.refs_2_ = bf16[64,4224]{1,0:T(8,128)(2,1)} collective-permute-done((bf16[64,4224]{1,0:T(8,128)(2,1)S(1)}, bf16[64,4224]{1,0:T(8,128)(2,1)}, u32[]{:S(2)}, u32[]{:S(2)}) %collective-permute-start.19) | collective-permute-done | bytes 540704 | tf_op jit(solution)/shard_map/ppermute | solution.py:27
  115.3 3.1 %shard_map.247 = (bf16[256,2176]{1,0:T(8,128)(2,1)}, bf16[512,1024]{1,0:T(8,128)(2,1)}) custom-call(bf16[64,4224]{1,0:T(8,128)(2,1)} %shard_map.243.refs_4_.refs_0_, bf16[64,4224]{1,0:T(8,128)(2,1)} %copy-done.25, bf16[64,4224]{1,0:T(8,128)(2,1)} %collective-permute-done.19.refs_2_, bf16[64,4224]{1,0:T(8,128)(2,1)} %collective-permute-done.20.refs_3_), custom_call_target="tpu_custom_call" | custom-call | tf_op jit(solution)/shard_map/pallas_call | solution.py:52
  125.0 14.9 %shard_map.248 = (bf16[256,2176]{1,0:T(8,128)(2,1)}, bf16[256,2176]{1,0:T(8,128)(2,1)}, bf16[256,2048]{1,0:T(8,128)(2,1)}, bf16[256,2048]{1,0:T(8,128)(2,1)}, bf...) custom-call(s32[2]{0:T(128)} %pad_add_fusion.1.refs_0_, ...), custom_call_target="tpu_custom_call", output_to_operand_aliasing={{4}: (8, {}), {5}: (9, {}), {6}: (10, {}), {7}: (11, {}), {... | custom-call | tf_op jit(solution)/shard_map/pallas_call | solution.py:52
  140.6 3.8 %collective-permute-done.21 = bf16[256,2048]{1,0:T(8,128)(2,1)S(1)} collective-permute-done((bf16[256,2048]{1,0:T(8,128)(2,1)}, bf16[256,2048]{1,0:T(8,128)(2,1)S(1)}, u32[]{:S(2)}, u32[]{:S(2)}) %collective-permute-start.21) | collective-permute-done | bytes 1048608 | tf_op jit(solution)/shard_map/ppermute | solution.py:27
  151.5 6.6 %fusion.18 = f32[2048,1536]{1,0:T(8,128)} fusion(bf16[352,2048]{1,0:T(8,128)(2,1)S(1)} %copy-done.1, bf16[352,1536]{1,0:T(8,128)(2,1)S(1)} %copy-done.4), kind=kOutput, calls=%fused_computation.49 | convolution fusion | flops 2214592512 | bytes 15106048 | tf_op jit(solution)/shard_map/dot_general | solution.py:22
  158.1 4.5 %fusion.19 = f32[768,2048]{1,0:T(8,128)} fusion(bf16[352,768]{1,0:T(8,128)(2,1)S(1)} %copy-done.7, bf16[352,2048]{1,0:T(8,128)(2,1)S(1)} %copy-done.2), kind=kOutput, calls=%fused_computation.50 | convolution fusion | flops 1107296256 | bytes 8273920 | tf_op jit(solution)/shard_map/dot_general | solution.py:22
  164.1 4.0 %collective-permute-done.30 = bf16[64,2176]{1,0:T(8,128)(2,1)S(1)} collective-permute-done((bf16[64,2176]{1,0:T(8,128)(2,1)S(1)}, bf16[64,2176]{1,0:T(8,128)(2,1)S(1)}, u32[]{:S(2)}, u32[]{:S(2)}) %collective-permute-start.30) | collective-permute-done | bytes 278560 | tf_op jit(solution)/shard_map/ppermute | solution.py:27
  176.8 5.1 %collective-permute-done.33.refs_10_ = bf16[32,2176]{1,0:T(8,128)(2,1)S(1)} collective-permute-done((bf16[32,2176]{1,0:T(8,128)(2,1)S(1)}, bf16[32,2176]{1,0:T(8,128)(2,1)S(1)}, u32[]{:S(2)}, u32[]{:S(2)}) %collective-permute-start.33) | collective-permute-done | bytes 139296 | tf_op jit(solution)/shard_map/ppermute | solution.py:27
  185.5 3.1 %shard_map.249 = (f32[32,2048]{1,0:T(8,128)}, f32[1,2048]{1,0:T(1,128)}, bf16[32,2176]{1,0:T(8,128)(2,1)}) custom-call(s32[1]{0:T(128)} %bitcast.refs_0_, f32[32,2176]{1,0:T(8,128)} %slice.147.refs_1_, bf16[32,2176]{1,0:T(8,128)(2,1)} %get-tuple-element.210.refs_0_.refs_2_, bf16[32,128]{1,0:T(8,128)(2,1)} %convert_element_type.77.refs_2_.refs_3_, ...), custom_call_target="tpu_custom_call" | custom-call | tf_op jit(solution)/shard_map/pallas_call | solution.py:52
  194.5 7.3 %collective-permute-done.36.refs_12_ = bf16[32,2176]{1,0:T(8,128)(2,1)S(1)} collective-permute-done((bf16[32,2176]{1,0:T(8,128)(2,1)}, bf16[32,2176]{1,0:T(8,128)(2,1)S(1)}, u32[]{:S(2)}, u32[]{:S(2)}) %collective-permute-start.36) | collective-permute-done | bytes 139296 | tf_op jit(solution)/shard_map/ppermute | solution.py:27
  208.2 11.1 %shard_map.250 = (bf16[512,256]{1,0:T(8,128)(2,1)}, bf16[512,256]{1,0:T(8,128)(2,1)}, bf16[128,1024]{1,0:T(8,128)(2,1)}, f32[1,128]{1,0:T(1,128)}, bf16[128,640]...) custom-call(s32[1]{0:T(128)} %bitcast.1.refs_0_, ...), custom_call_target="tpu_custom_call" | custom-call | tf_op jit(solution)/shard_map/pallas_call | solution.py:52
  230.8 4.7 %fusion.20.refs_2_ = f32[128,2048]{1,0:T(8,128)} fusion(bf16[128,1024]{1,0:T(8,128)(2,1)S(1)} %copy-done.20, bf16[2048,1024]{1,0:T(8,128)(2,1)} %refs_1_.2), kind=kOutput, calls=%fused_computation.51 | convolution fusion | flops 536870912 | bytes 5505024 | tf_op jit(solution)/shard_map/dot_general | solution.py:22
  235.6 2.9 collective-permute-done.49.refs_3_.refs_19_
  239.2 3.5 %shard_map.252 = (f32[32,2048]{1,0:T(8,128)}, bf16[32,2432]{1,0:T(8,128)(2,1)}, bf16[32,2432]{1,0:T(8,128)(2,1)}, bf16[32,2432]{1,0:T(8,128)(2,1)}, bf16[128,128...) custom-call(f32[1,2048]{1,0:T(1,128)} %get-tuple-element.320.refs_0_, ...), custom_call_target="tpu_custom_call", output_to_operand_aliasing={{6}: (21, {}), {7}: (22, {}), {8}: (23, {}), {9}: (24, {})} | custom-call | tf_op jit(solution)/shard_map/pallas_call | solution.py:52
  254.3 7.1 %collective-permute-done.56.refs_9_ = bf16[32,2432]{1,0:T(8,128)(2,1)S(1)} collective-permute-done((bf16[32,2432]{1,0:T(8,128)(2,1)}, bf16[32,2432]{1,0:T(8,128)(2,1)S(1)}, u32[]{:S(2)}, u32[]{:S(2)}) %collective-permute-start.56) | collective-permute-done | bytes 155680 | tf_op jit(solution)/shard_map/ppermute | solution.py:27
  270.2 3.2 %collective-permute-done.61.refs_4_.refs_2_ = bf16[32,2048]{1,0:T(8,128)(2,1)S(1)} collective-permute-done((bf16[32,2048]{1,0:T(8,128)(2,1)}, bf16[32,2048]{1,0:T(8,128)(2,1)S(1)}, u32[]{:S(2)}, u32[]{:S(2)}) %collective-permute-start.61) | collective-permute-done | bytes 131104 | tf_op jit(solution)/shard_map/ppermute | solution.py:27
  273.4 3.8 %collective-permute-start.62 = (bf16[32,2048]{1,0:T(8,128)(2,1)}, bf16[32,2048]{1,0:T(8,128)(2,1)S(1)}, u32[]{:S(2)}, u32[]{:S(2)}) collective-permute-start(bf16[32,2048]{1,0:T(8,128)(2,1)} %get-tuple-element.347.refs_1_), channel_id=1, source_target_pairs={{0,2},{1,3},{2,0},{3,1},{4,6},{5,7},{6,4},{7,5},{8,10},{9,11},{10,... | collective-permute-start | bytes 393224 | tf_op jit(solution)/shard_map/ppermute | solution.py:27
  278.4 3.5 %shard_map.256.refs_7_.refs_6_ = f32[1024,256]{1,0:T(8,128)} custom-call(bf16[512,1024]{1,0:T(8,128)(2,1)} %get-tuple-element.332.refs_0_, bf16[512,1024]{1,0:T(8,128)(2,1)} %copy-done.5, bf16[512,256]{1,0:T(8,128)(2,1)} %get-tuple-element.351.refs_2_, bf16[512,384]{1,0:T(8,128)(2,1)} %copy-done.10), custom_call_target="tpu_custom_call" | custom-call | tf_op jit(solution)/shard_map/pallas_call | solution.py:52
  281.8 5.0 %shard_map.255.refs_8_.refs_5_ = f32[32,2048]{1,0:T(8,128)} custom-call(s32[2]{0:T(128)} %pad_add_fusion.2.refs_0_, bf16[2,8,2,32,2048]{4,3,2,1,0:T(8,128)(2,1)} %bitcast.36, bf16[512,128]{1,0:T(8,128)(2,1)} %get-tuple-element.349.refs_2_, bf16[512,384]{1,0:T(8,128)(2,1)} %copy-done.10), custom_call_target="tpu_custom_call" | custom-call | tf_op jit(solution)/shard_map/pallas_call | solution.py:52
  295.7 4.0 %shard_map.258 = (f32[256,1024]{1,0:T(8,128)}, f32[256,128]{1,0:T(8,128)}, f32[256,128]{1,0:T(8,128)}, f32[16,128]{1,0:T(8,128)}, f32[16,128]{1,0:T(8,128)}, /*index=5*/f32[1,128]{1,0:T(1,128)}, f32[1,128]{1,0:T(1,128)}) custom-call(s32[1]{0:T(128)} %bitcast.17.refs_0_, bf16[512,256]{1,0:T(8,128)(2,1)} %get-tuple-element.352.refs_1_, ...), custom_call_target="tpu_custom_call" | custom-call | tf_op jit(solution)/shard_map/pallas_call | solution.py:52
  (309 shorter events, 134.5 us)
Async XLA Ops:
  6.0 13.7 %collective-permute-start = (bf16[128,768]{1,0:T(8,128)(2,1)}, bf16[128,768]{1,0:T(8,128)(2,1)S(1)}, u32[]{:S(2)}, u32[]{:S(2)}) collective-permute-start(bf16[128,768]{1,0:T(8,128)(2,1)} %get-tuple-element.191), channel_id=1, source_target_pairs={{0,8},{4,12},{8,0},{12,4},{16,24},{20,28},{24,16},{28,20},{1,9},{5... | collective-permute-start | bytes 589832 | tf_op jit(solution)/shard_map/ppermute | solution.py:27
  10.5 50.1 %collective-permute-start.14 = (bf16[128,2048]{1,0:T(8,128)(2,1)S(1)}, bf16[128,2048]{1,0:T(8,128)(2,1)S(1)}, u32[]{:S(2)}, u32[]{:S(2)}) collective-permute-start(bf16[128,2048]{1,0:T(8,128)(2,1)S(1)} %bitcast.43), channel_id=1, source_target_pairs={{0,8},{4,12},{8,0},{12,4},{16,24},{20,28},{24,16},{28,20},{1,9},{5... | collective-permute-start | bytes 1572872 | tf_op jit(solution)/shard_map/ppermute | solution.py:27
  12.4 48.1 %collective-permute-start.15 = (bf16[128,2048]{1,0:T(8,128)(2,1)S(1)}, bf16[128,2048]{1,0:T(8,128)(2,1)S(1)}, u32[]{:S(2)}, u32[]{:S(2)}) collective-permute-start(bf16[128,2048]{1,0:T(8,128)(2,1)S(1)} %bitcast.44), channel_id=1, source_target_pairs={{0,16},{4,20},{8,24},{12,28},{16,0},{20,4},{24,8},{28,12},{1,17},{... | collective-permute-start | bytes 1572872 | tf_op jit(solution)/shard_map/ppermute | solution.py:27
  19.7 40.9 %collective-permute-start.16 = (bf16[128,2048]{1,0:T(8,128)(2,1)S(1)}, bf16[128,2048]{1,0:T(8,128)(2,1)S(1)}, u32[]{:S(2)}, u32[]{:S(2)}) collective-permute-start(bf16[128,2048]{1,0:T(8,128)(2,1)S(1)} %bitcast.45), channel_id=1, source_target_pairs={{0,24},{4,28},{8,16},{12,20},{16,8},{20,12},{24,0},{28,4},{1,25},{... | collective-permute-start | bytes 1572872 | tf_op jit(solution)/shard_map/ppermute | solution.py:27
  65.3 26.8 %collective-permute-start.17 = (bf16[512,2048]{1,0:T(8,128)(2,1)}, bf16[512,2048]{1,0:T(8,128)(2,1)S(1)}, u32[]{:S(2)}, u32[]{:S(2)}) collective-permute-start(bf16[512,2048]{1,0:T(8,128)(2,1)} %shard_map.245), channel_id=1, source_target_pairs={{0,4},{4,0},{8,12},{12,8},{16,20},{20,16},{24,28},{28,24},{1,5},{5... | collective-permute-start | bytes 6291464 | tf_op jit(solution)/shard_map/ppermute | solution.py:27
  67.6 17.3 %collective-permute-start.8 = (bf16[64,2176]{1,0:T(8,128)(2,1)S(1)}, bf16[64,2176]{1,0:T(8,128)(2,1)S(1)}, u32[]{:S(2)}, u32[]{:S(2)}) collective-permute-start(bf16[64,2176]{1,0:T(8,128)(2,1)S(1)} %copy-done.6), channel_id=1, source_target_pairs={{0,8},{4,12},{8,0},{12,4},{16,24},{20,28},{24,16},{28,20},{1,9},{5... | collective-permute-start | bytes 835592 | tf_op jit(solution)/shard_map/ppermute | solution.py:27
  68.6 16.3 %collective-permute-start.9 = (bf16[64,2176]{1,0:T(8,128)(2,1)S(1)}, bf16[64,2176]{1,0:T(8,128)(2,1)S(1)}, u32[]{:S(2)}, u32[]{:S(2)}) collective-permute-start(bf16[64,2176]{1,0:T(8,128)(2,1)S(1)} %copy-done.6), channel_id=1, source_target_pairs={{0,16},{4,20},{8,24},{12,28},{16,0},{20,4},{24,8},{28,12},{1,17},{... | collective-permute-start | bytes 835592 | tf_op jit(solution)/shard_map/ppermute | solution.py:27
  69.8 15.2 %collective-permute-start.10 = (bf16[64,2176]{1,0:T(8,128)(2,1)S(1)}, bf16[64,2176]{1,0:T(8,128)(2,1)}, u32[]{:S(2)}, u32[]{:S(2)}) collective-permute-start(bf16[64,2176]{1,0:T(8,128)(2,1)S(1)} %copy-done.6), channel_id=1, source_target_pairs={{0,24},{4,28},{8,16},{12,20},{16,8},{20,12},{24,0},{28,4},{1,25},{... | collective-permute-start | bytes 835592 | tf_op jit(solution)/shard_map/ppermute | solution.py:27
  88.0 20.2 %collective-permute-start.18 = (bf16[64,4224]{1,0:T(8,128)(2,1)S(1)}, bf16[64,4224]{1,0:T(8,128)(2,1)S(1)}, u32[]{:S(2)}, u32[]{:S(2)}) collective-permute-start(bf16[64,4224]{1,0:T(8,128)(2,1)S(1)} %copy-done.3), channel_id=1, source_target_pairs={{0,8},{4,12},{8,0},{12,4},{16,24},{20,28},{24,16},{28,20},{1,9},{5... | collective-permute-start | bytes 1622024 | tf_op jit(solution)/shard_map/ppermute | solution.py:27
  88.9 24.8 %collective-permute-start.19 = (bf16[64,4224]{1,0:T(8,128)(2,1)S(1)}, bf16[64,4224]{1,0:T(8,128)(2,1)}, u32[]{:S(2)}, u32[]{:S(2)}) collective-permute-start(bf16[64,4224]{1,0:T(8,128)(2,1)S(1)} %copy-done.3), channel_id=1, source_target_pairs={{0,16},{4,20},{8,24},{12,28},{16,0},{20,4},{24,8},{28,12},{1,17},{... | collective-permute-start | bytes 1622024 | tf_op jit(solution)/shard_map/ppermute | solution.py:27
  90.1 25.1 %collective-permute-start.20 = (bf16[64,4224]{1,0:T(8,128)(2,1)S(1)}, bf16[64,4224]{1,0:T(8,128)(2,1)}, u32[]{:S(2)}, u32[]{:S(2)}) collective-permute-start(bf16[64,4224]{1,0:T(8,128)(2,1)S(1)} %copy-done.3), channel_id=1, source_target_pairs={{0,24},{4,28},{8,16},{12,20},{16,8},{20,12},{24,0},{28,4},{1,25},{... | collective-permute-start | bytes 1622024 | tf_op jit(solution)/shard_map/ppermute | solution.py:27
  121.5 18.4 %collective-permute-start.24 = (bf16[64,2176]{1,0:T(8,128)(2,1)}, bf16[64,2176]{1,0:T(8,128)(2,1)S(1)}, u32[]{:S(2)}, u32[]{:S(2)}) collective-permute-start(bf16[64,2176]{1,0:T(8,128)(2,1)} %get-tuple-element.236), channel_id=1, source_target_pairs={{0,8},{4,12},{8,0},{12,4},{16,24},{20,28},{24,16},{28,20},{1,9},{5... | collective-permute-start | bytes 835592 | tf_op jit(solution)/shard_map/ppermute | solution.py:27
  122.3 17.5 %collective-permute-start.25 = (bf16[64,2176]{1,0:T(8,128)(2,1)S(1)}, bf16[64,2176]{1,0:T(8,128)(2,1)S(1)}, u32[]{:S(2)}, u32[]{:S(2)}) collective-permute-start(bf16[64,2176]{1,0:T(8,128)(2,1)S(1)} %get-tuple-element.237), channel_id=1, source_target_pairs={{0,16},{4,20},{8,24},{12,28},{16,0},{20,4},{24,8},{28,12},{1,17},{... | collective-permute-start | bytes 835592 | tf_op jit(solution)/shard_map/ppermute | solution.py:27
  123.8 16.1 %collective-permute-start.26 = (bf16[64,2176]{1,0:T(8,128)(2,1)S(1)}, bf16[64,2176]{1,0:T(8,128)(2,1)S(1)}, u32[]{:S(2)}, u32[]{:S(2)}) collective-permute-start(bf16[64,2176]{1,0:T(8,128)(2,1)S(1)} %get-tuple-element.238), channel_id=1, source_target_pairs={{0,24},{4,28},{8,16},{12,20},{16,8},{20,12},{24,0},{28,4},{1,25},{... | collective-permute-start | bytes 835592 | tf_op jit(solution)/shard_map/ppermute | solution.py:27
  146.1 22.0 %collective-permute-start.31 = (bf16[256,2048]{1,0:T(8,128)(2,1)S(1)}, bf16[256,2048]{1,0:T(8,128)(2,1)S(1)}, u32[]{:S(2)}, u32[]{:S(2)}) collective-permute-start(bf16[256,2048]{1,0:T(8,128)(2,1)S(1)} %copy-done.69), channel_id=1, source_target_pairs={{0,4},{4,0},{8,12},{12,8},{16,20},{20,16},{24,28},{28,24},{1,5},{5... | collective-permute-start | bytes 3145736 | tf_op jit(solution)/shard_map/ppermute | solution.py:27
  147.1 27.1 %collective-permute-start.38 = (bf16[64,2048]{1,0:T(8,128)(2,1)S(1)}, bf16[64,2048]{1,0:T(8,128)(2,1)S(1)}, u32[]{:S(2)}, u32[]{:S(2)}) collective-permute-start(bf16[64,2048]{1,0:T(8,128)(2,1)S(1)} %get-tuple-element.380), channel_id=1, source_target_pairs={{0,8},{4,12},{8,0},{12,4},{16,24},{20,28},{24,16},{28,20},{1,9},{5... | collective-permute-start | bytes 786440 | tf_op jit(solution)/shard_map/ppermute | solution.py:27
  148.0 14.7 %collective-permute-start.28 = (bf16[64,2176]{1,0:T(8,128)(2,1)S(1)}, bf16[64,2176]{1,0:T(8,128)(2,1)S(1)}, u32[]{:S(2)}, u32[]{:S(2)}) collective-permute-start(bf16[64,2176]{1,0:T(8,128)(2,1)S(1)} %get-tuple-element.267), channel_id=1, source_target_pairs={{0,8},{4,12},{8,0},{12,4},{16,24},{20,28},{24,16},{28,20},{1,9},{5... | collective-permute-start | bytes 835592 | tf_op jit(solution)/shard_map/ppermute | solution.py:27
  149.1 15.0 %collective-permute-start.29 = (bf16[64,2176]{1,0:T(8,128)(2,1)S(1)}, bf16[64,2176]{1,0:T(8,128)(2,1)S(1)}, u32[]{:S(2)}, u32[]{:S(2)}) collective-permute-start(bf16[64,2176]{1,0:T(8,128)(2,1)S(1)} %get-tuple-element.268), channel_id=1, source_target_pairs={{0,16},{4,20},{8,24},{12,28},{16,0},{20,4},{24,8},{28,12},{1,17},{... | collective-permute-start | bytes 835592 | tf_op jit(solution)/shard_map/ppermute | solution.py:27
  150.1 18.0 %collective-permute-start.30 = (bf16[64,2176]{1,0:T(8,128)(2,1)S(1)}, bf16[64,2176]{1,0:T(8,128)(2,1)S(1)}, u32[]{:S(2)}, u32[]{:S(2)}) collective-permute-start(bf16[64,2176]{1,0:T(8,128)(2,1)S(1)} %get-tuple-element.269), channel_id=1, source_target_pairs={{0,24},{4,28},{8,16},{12,20},{16,8},{20,12},{24,0},{28,4},{1,25},{... | collective-permute-start | bytes 835592 | tf_op jit(solution)/shard_map/ppermute | solution.py:27
  162.7 25.9 %collective-permute-start.39 = (bf16[64,2048]{1,0:T(8,128)(2,1)}, bf16[64,2048]{1,0:T(8,128)(2,1)}, u32[]{:S(2)}, u32[]{:S(2)}) collective-permute-start(bf16[64,2048]{1,0:T(8,128)(2,1)} %get-tuple-element.379), channel_id=1, source_target_pairs={{0,16},{4,20},{8,24},{12,28},{16,0},{20,4},{24,8},{28,12},{1,17},{... | collective-permute-start | bytes 786440 | tf_op jit(solution)/shard_map/ppermute | solution.py:27
  168.6 13.3 %collective-permute-start.33 = (bf16[32,2176]{1,0:T(8,128)(2,1)S(1)}, bf16[32,2176]{1,0:T(8,128)(2,1)S(1)}, u32[]{:S(2)}, u32[]{:S(2)}) collective-permute-start(bf16[32,2176]{1,0:T(8,128)(2,1)S(1)} %get-tuple-element.382), channel_id=1, source_target_pairs={{0,2},{1,3},{2,0},{3,1},{4,6},{5,7},{6,4},{7,5},{8,10},{9,11},{10,... | collective-permute-start | bytes 417800 | tf_op jit(solution)/shard_map/ppermute | solution.py:27
  174.2 15.2 %collective-permute-start.40 = (bf16[64,2048]{1,0:T(8,128)(2,1)}, bf16[64,2048]{1,0:T(8,128)(2,1)S(1)}, u32[]{:S(2)}, u32[]{:S(2)}) collective-permute-start(bf16[64,2048]{1,0:T(8,128)(2,1)} %get-tuple-element.378), channel_id=1, source_target_pairs={{0,24},{4,28},{8,16},{12,20},{16,8},{20,12},{24,0},{28,4},{1,25},{... | collective-permute-start | bytes 786440 | tf_op jit(solution)/shard_map/ppermute | solution.py:27
  175.6 15.7 %collective-permute-start.41 = (bf16[64,2048]{1,0:T(8,128)(2,1)}, bf16[64,2048]{1,0:T(8,128)(2,1)S(1)}, u32[]{:S(2)}, u32[]{:S(2)}) collective-permute-start(bf16[64,2048]{1,0:T(8,128)(2,1)} %get-tuple-element.377), channel_id=1, source_target_pairs={{0,8},{4,12},{8,0},{12,4},{16,24},{20,28},{24,16},{28,20},{1,9},{5... | collective-permute-start | bytes 786440 | tf_op jit(solution)/shard_map/ppermute | solution.py:27
  203.8 15.5 %collective-permute-start.44 = (bf16[32,2048]{1,0:T(8,128)(2,1)S(1)}, bf16[32,2048]{1,0:T(8,128)(2,1)S(1)}, u32[]{:S(2)}, u32[]{:S(2)}) collective-permute-start(bf16[32,2048]{1,0:T(8,128)(2,1)S(1)} %slice.180), channel_id=1, source_target_pairs={{0,1},{1,0},{2,3},{3,2},{4,5},{5,4},{6,7},{7,6},{8,9},{9,8},{10,11... | collective-permute-start | bytes 393224 | tf_op jit(solution)/shard_map/ppermute | solution.py:27
  205.4 13.9 %collective-permute-start.45 = (bf16[32,2048]{1,0:T(8,128)(2,1)S(1)}, bf16[32,2048]{1,0:T(8,128)(2,1)S(1)}, u32[]{:S(2)}, u32[]{:S(2)}) collective-permute-start(bf16[32,2048]{1,0:T(8,128)(2,1)S(1)} %get-tuple-element.305), channel_id=1, source_target_pairs={{0,2},{1,3},{2,0},{3,1},{4,6},{5,7},{6,4},{7,5},{8,10},{9,11},{10,... | collective-permute-start | bytes 393224 | tf_op jit(solution)/shard_map/ppermute | solution.py:27
  208.2 27.3 %collective-permute-start.54 = (bf16[512,1024]{1,0:T(8,128)(2,1)S(1)}, bf16[512,1024]{1,0:T(8,128)(2,1)S(1)}, u32[]{:S(2)}, u32[]{:S(2)}) collective-permute-start(bf16[512,1024]{1,0:T(8,128)(2,1)S(1)} %copy-done.18), channel_id=1, source_target_pairs={{0,4},{4,0},{8,12},{12,8},{16,20},{20,16},{24,28},{28,24},{1,5},{5... | collective-permute-start | bytes 3145736 | tf_op jit(solution)/shard_map/ppermute | solution.py:27
  248.3 13.1 %collective-permute-start.56 = (bf16[32,2432]{1,0:T(8,128)(2,1)}, bf16[32,2432]{1,0:T(8,128)(2,1)S(1)}, u32[]{:S(2)}, u32[]{:S(2)}) collective-permute-start(bf16[32,2432]{1,0:T(8,128)(2,1)} %get-tuple-element.341), channel_id=1, source_target_pairs={{0,2},{1,3},{2,0},{3,1},{4,6},{5,7},{6,4},{7,5},{8,10},{9,11},{10,... | collective-permute-start | bytes 466952 | tf_op jit(solution)/shard_map/ppermute | solution.py:27
  254.2 22.9 %collective-permute-start.64 = (bf16[512,384]{1,0:T(8,128)(2,1)}, bf16[512,384]{1,0:T(8,128)(2,1)S(1)}, u32[]{:S(2)}, u32[]{:S(2)}) collective-permute-start(bf16[512,384]{1,0:T(8,128)(2,1)} %get-tuple-element.350), channel_id=1, source_target_pairs={{0,4},{4,0},{8,12},{12,8},{16,20},{20,16},{24,28},{28,24},{1,5},{5... | collective-permute-start | bytes 1179656 | tf_op jit(solution)/shard_map/ppermute | solution.py:27
  264.6 22.3 %collective-permute-start.65 = (bf16[144,1280]{1,0:T(8,128)(2,1)}, bf16[144,1280]{1,0:T(8,128)(2,1)S(1)}, u32[]{:S(2)}, u32[]{:S(2)}) collective-permute-start(bf16[144,1280]{1,0:T(8,128)(2,1)} %get-tuple-element.353.refs_0_), channel_id=1, source_target_pairs={{0,8},{4,12},{8,0},{12,4},{16,24},{20,28},{24,16},{28,20},{1,9},{5... | collective-permute-start | bytes 1105928 | tf_op jit(solution)/shard_map/ppermute | solution.py:27
  266.0 21.0 %collective-permute-start.66 = (bf16[144,1280]{1,0:T(8,128)(2,1)}, bf16[144,1280]{1,0:T(8,128)(2,1)S(1)}, u32[]{:S(2)}, u32[]{:S(2)}) collective-permute-start(bf16[144,1280]{1,0:T(8,128)(2,1)} %get-tuple-element.353.refs_0_), channel_id=1, source_target_pairs={{0,16},{4,20},{8,24},{12,28},{16,0},{20,4},{24,8},{28,12},{1,17},{... | collective-permute-start | bytes 1105928 | tf_op jit(solution)/shard_map/ppermute | solution.py:27
  266.5 20.5 %collective-permute-start.67 = (bf16[144,1280]{1,0:T(8,128)(2,1)}, bf16[144,1280]{1,0:T(8,128)(2,1)S(1)}, u32[]{:S(2)}, u32[]{:S(2)}) collective-permute-start(bf16[144,1280]{1,0:T(8,128)(2,1)} %get-tuple-element.353.refs_0_), channel_id=1, source_target_pairs={{0,24},{4,28},{8,16},{12,20},{16,8},{20,12},{24,0},{28,4},{1,25},{... | collective-permute-start | bytes 1105928 | tf_op jit(solution)/shard_map/ppermute | solution.py:27
  273.4 13.5 %collective-permute-start.62 = (bf16[32,2048]{1,0:T(8,128)(2,1)}, bf16[32,2048]{1,0:T(8,128)(2,1)S(1)}, u32[]{:S(2)}, u32[]{:S(2)}) collective-permute-start(bf16[32,2048]{1,0:T(8,128)(2,1)} %get-tuple-element.347.refs_1_), channel_id=1, source_target_pairs={{0,2},{1,3},{2,0},{3,1},{4,6},{5,7},{6,4},{7,5},{8,10},{9,11},{10,... | collective-permute-start | bytes 393224 | tf_op jit(solution)/shard_map/ppermute | solution.py:27
  (107 other events, 631.0 us)
